TPU v7x, 32 devices: a whole 2x2x4 slice. The times are simulated.
32 devices in a mesh: dp: 8 (over z, x), tensor: 4 (over y, core).
Axes of the slice: x: 2, y: 2, z: 4, core: 2. Of those that a mesh axis runs over, the one named last changes fastest.
Arguments:
- tokens: bfloat16 [8192, 2048], P('dp'), may hold values from -6 to 6
- lengths: int32 [8], P('dp'), may hold values from 1 to 1024, 4915 in all
- norm_attn: float32 [2048], P('dp'), may hold values from 0.5 to 1.5
- query_proj: float32 [2048, 1024], P('dp', 'tensor'), may hold values from -0.125 to 0.125
- key_proj: float32 [2048, 1024], P('dp', 'tensor'), may hold values from -0.125 to 0.125
- value_proj: float32 [2048, 2048], P('dp', 'tensor'), may hold values from -0.125 to 0.125
- outgate_proj: float32 [2048, 2048], P('dp', 'tensor'), may hold values from -0.125 to 0.125
- rank_proj: float32 [2048, 16], P('dp'), may hold values from -0.125 to 0.125
- decay_proj: float32 [16, 4, 256], P(None, 'tensor', 'dp'), may hold values from -1.5 to 1.5
- decay_bias: float32 [4, 256], P('tensor', 'dp'), may hold values from -4 to 5
- head_gain: float32 [512], P('dp'), may hold values from 0.5 to 1.5
- out_proj: float32 [2048, 2048], P('tensor', 'dp'), may hold values from -0.25 to 0.25
- norm_ffn: float32 [2048], P('dp'), may hold values from 0.5 to 1.5
- gate_proj: float32 [2048, 5632], P('dp', 'tensor'), may hold values from -0.125 to 0.125
- up_proj: float32 [2048, 5632], P('dp', 'tensor'), may hold values from -0.125 to 0.125
- down_proj: float32 [5632, 2048], P('tensor', 'dp'), may hold values from -0.15625 to 0.15625
- cotangent: bfloat16 [8192, 2048], P('dp'), may hold values from -6 to 6
Outputs:
- output: bfloat16 [8192, 2048], P('dp')
- grad_tokens: bfloat16 [8192, 2048], P('dp')
- grad_norm_attn: float32 [2048], P('dp')
- grad_query_proj: float32 [2048, 1024], P('dp', 'tensor')
- grad_key_proj: float32 [2048, 1024], P('dp', 'tensor')
- grad_value_proj: float32 [2048, 2048], P('dp', 'tensor')
- grad_outgate_proj: float32 [2048, 2048], P('dp', 'tensor')
- grad_rank_proj: float32 [2048, 16], P('dp')
- grad_decay_proj: float32 [16, 4, 256], P(None, 'tensor', 'dp')
- grad_decay_bias: float32 [4, 256], P('tensor', 'dp')
- grad_head_gain: float32 [512], P('dp')
- grad_out_proj: float32 [2048, 2048], P('tensor', 'dp')
- grad_norm_ffn: float32 [2048], P('dp')
- grad_gate_proj: float32 [2048, 5632], P('dp', 'tensor')
- grad_up_proj: float32 [2048, 5632], P('dp', 'tensor')
- grad_down_proj: float32 [5632, 2048], P('tensor', 'dp')
Inputs may be any that keep to these rules, and one draw needn't show every extreme that they name: `lengths`: each slot's live positions come first; some slot is full.
All inputs are finite; a program needn't handle non-finite values. No bound on the sum of `lengths` on one device may be relied on, other than what follows from the above.
Results may differ from a plain program's by a relative error of at most 0.04.
Values may be sent and summed in bfloat16 or wider, within the bound.
A program may use at most 256 MiB of HBM per device.

v0:
```python
import jax
import jax.numpy as jnp
from jax import lax
from jax.sharding import PartitionSpec as P

DK = 256
DV = 512
GROUP = 64
SEQ_LEN = 1024


norm_eps = 1e-06
head_eps = 1.0
highest_precision = lax.Precision.HIGHEST


def rms_scale(values, gain):
    return values * lax.rsqrt(jnp.mean(values * values, axis=-1, keepdims=True) + norm_eps) * gain


def project(left, right):
    return jnp.dot(left, right, preferred_element_type=jnp.float32)


def collect(left, right):
    return lax.dot_general(
        left, right, (((0,), (0,)), ((), ())), preferred_element_type=jnp.float32
    )


def against(left, right):
    return lax.dot_general(
        left, right, (((1,), (1,)), ((), ())), preferred_element_type=jnp.float32
    )


def group_step(running_state, block):
    query_matrix, key_matrix, value_matrix, decay = block
    cumulative_decay = jnp.cumsum(decay, axis=1)
    steps = decay.shape[1]
    lower = (jnp.arange(steps)[:, None] >= jnp.arange(steps)[None, :]).astype(jnp.float32)
    spread = (
        jnp.exp(jnp.minimum(cumulative_decay[:, :, None, :] - cumulative_decay[:, None, :, :], 0.0))
        * lower[None, :, :, None]
    )
    weighted = query_matrix[:, :, None, :] * spread
    scores = jnp.einsum("hijk,hjk->hij", weighted, key_matrix, precision=highest_precision)
    inner = jnp.einsum("hij,hjv->hiv", scores, value_matrix, precision=highest_precision)
    outer_product = jnp.einsum(
        "muq,mqj->muj",
        query_matrix * jnp.exp(cumulative_decay),
        running_state,
        precision=highest_precision,
    )
    final_decay_row = cumulative_decay[:, -1:, :]
    carried_state = jnp.exp(final_decay_row[:, 0, :])[:, :, None] * running_state
    carried_state = carried_state + jnp.einsum(
        "zbm,zbi->zmi",
        key_matrix * jnp.exp(final_decay_row - cumulative_decay),
        value_matrix,
        precision=highest_precision,
    )
    return (carried_state, inner + outer_product)


def recurrence(query_matrix, key_matrix, value_matrix, decay):
    length = query_matrix.shape[0]
    heads = query_matrix.shape[1]
    count = length // GROUP

    def split(values):
        return jnp.transpose(values.reshape(count, GROUP, heads, values.shape[2]), (0, 2, 1, 3))

    start = jnp.zeros((heads, key_matrix.shape[2], value_matrix.shape[2]), jnp.float32)
    _, blocks = lax.scan(
        jax.checkpoint(group_step),
        start,
        (split(query_matrix), split(key_matrix), split(value_matrix), split(decay)),
    )
    return jnp.transpose(blocks, (0, 2, 1, 3)).reshape(length, heads, value_matrix.shape[2])


def mixer(
    query_matrix,
    key_matrix,
    value_matrix,
    outgate_rows,
    rank_rows,
    decay_weight,
    bias_weight,
    gain_weight,
):
    heads = bias_weight.shape[0]
    length = query_matrix.shape[0]
    seqs = length // SEQ_LEN
    before = jnp.dot(
        rank_rows,
        decay_weight.reshape(decay_weight.shape[0], -1),
        precision=highest_precision,
        preferred_element_type=jnp.float32,
    ) + bias_weight.reshape(-1)
    decay = jax.nn.log_sigmoid(before) / 16.0

    def arrange(values, width):
        return values.reshape(seqs, SEQ_LEN, heads, width)

    scale = DK ** (-0.5)
    mixed = jax.vmap(recurrence)(
        arrange(query_matrix * scale, DK),
        arrange(key_matrix, DK),
        arrange(value_matrix, DV),
        arrange(decay, DK),
    )
    mixed = mixed.reshape(length, heads, DV)
    normed = (
        mixed * lax.rsqrt(jnp.mean(mixed * mixed, axis=-1, keepdims=True) + head_eps) * gain_weight
    )
    return (normed * jax.nn.silu(outgate_rows.reshape(length, heads, DV))).reshape(
        length, heads * DV
    )


def swiglu(gate_rows, up_rows):
    return jax.nn.silu(gate_rows) * up_rows


def local(
    tokens,
    lengths,
    norm_attn,
    query_proj,
    key_proj,
    value_proj,
    outgate_proj,
    rank_proj,
    decay_proj,
    decay_bias,
    head_gain,
    out_proj,
    norm_ffn,
    gate_proj,
    up_proj,
    down_proj,
    cotangent,
):
    half = jnp.bfloat16
    (
        gain_attn,
        query_full,
        key_full,
        value_full,
        outgate_full,
        rank_full,
        decay_full,
        bias_full,
        head_full,
        out_full,
    ) = (
        lax.all_gather(norm_attn.astype(half), "dp", axis=0, tiled=True),
        lax.all_gather(query_proj.astype(half), "dp", axis=0, tiled=True),
        lax.all_gather(key_proj.astype(half), "dp", axis=0, tiled=True),
        lax.all_gather(value_proj.astype(half), "dp", axis=0, tiled=True),
        lax.all_gather(outgate_proj.astype(half), "dp", axis=0, tiled=True),
        lax.all_gather(rank_proj.astype(half), "dp", axis=0, tiled=True),
        lax.all_gather(decay_proj.astype(half), "dp", axis=2, tiled=True),
        lax.all_gather(decay_bias.astype(half), "dp", axis=1, tiled=True),
        lax.all_gather(head_gain.astype(half), "dp", axis=0, tiled=True),
        lax.all_gather(out_proj.astype(half), "dp", axis=1, tiled=True),
    )
    rows_total = tokens.shape[0]
    positions = jnp.arange(SEQ_LEN, dtype=jnp.int32)
    mask = (positions[None, :] < lengths[:, None]).astype(jnp.float32).reshape(rows_total, 1)
    tokens_full = tokens.astype(jnp.float32)
    normed, pull_first = jax.vjp(rms_scale, tokens_full, gain_attn.astype(jnp.float32))
    normed_half = normed.astype(half)
    query_matrix = project(normed_half, query_full)
    key_matrix = project(normed_half, key_full)
    value_matrix = project(normed_half, value_full)
    outgate_rows = project(normed_half, outgate_full)
    rank_rows = project(normed_half, rank_full)
    gated, pull_mix = jax.vjp(
        mixer,
        query_matrix,
        key_matrix,
        value_matrix,
        outgate_rows,
        rank_rows,
        decay_full.astype(jnp.float32),
        bias_full.astype(jnp.float32),
        head_full.astype(jnp.float32),
    )
    gated_half = gated.astype(half)
    attn = lax.psum(project(gated_half, out_full), "tensor")
    middle = tokens_full + attn
    gain_ffn, gate_full, up_full, down_full = (
        lax.all_gather(norm_ffn.astype(half), "dp", axis=0, tiled=True),
        lax.all_gather(gate_proj.astype(half), "dp", axis=0, tiled=True),
        lax.all_gather(up_proj.astype(half), "dp", axis=0, tiled=True),
        lax.all_gather(down_proj.astype(half), "dp", axis=1, tiled=True),
    )
    normed_ffn, pull_second = jax.vjp(rms_scale, middle, gain_ffn.astype(jnp.float32))
    normed_ffn_half = normed_ffn.astype(half)
    gate_rows = project(normed_ffn_half, gate_full)
    up_rows = project(normed_ffn_half, up_full)
    hidden, pull_glu = jax.vjp(swiglu, gate_rows, up_rows)
    hidden_half = hidden.astype(half)
    ffn = lax.psum(project(hidden_half, down_full).astype(jnp.bfloat16), "tensor").astype(
        jnp.float32
    )
    output = (mask * (middle + ffn)).astype(half)
    d_out = cotangent.astype(jnp.float32) * mask
    d_out_half = d_out.astype(half)
    gain_ffn, gate_full, up_full, down_full = (
        lax.all_gather(norm_ffn.astype(half), "dp", axis=0, tiled=True),
        lax.all_gather(gate_proj.astype(half), "dp", axis=0, tiled=True),
        lax.all_gather(up_proj.astype(half), "dp", axis=0, tiled=True),
        lax.all_gather(down_proj.astype(half), "dp", axis=1, tiled=True),
    )
    grad_down = collect(hidden_half, d_out_half)
    d_hidden = against(d_out_half, down_full)
    d_gate, d_up = pull_glu(d_hidden)
    d_gate_half = d_gate.astype(half)
    d_up_half = d_up.astype(half)
    grad_gate = collect(normed_ffn_half, d_gate_half)
    grad_up = collect(normed_ffn_half, d_up_half)
    d_normed_ffn = lax.psum(
        (against(d_gate_half, gate_full) + against(d_up_half, up_full)).astype(jnp.bfloat16),
        "tensor",
    ).astype(jnp.float32)
    d_middle_norm, grad_gain_ffn = pull_second(d_normed_ffn)
    grad_norm_ffn, grad_gate_proj, grad_up_proj, grad_down_proj = (
        lax.psum_scatter(
            grad_gain_ffn.astype(jnp.bfloat16), "dp", scatter_dimension=0, tiled=True
        ).astype(jnp.float32),
        lax.psum_scatter(
            grad_gate.astype(jnp.bfloat16), "dp", scatter_dimension=0, tiled=True
        ).astype(jnp.float32),
        lax.psum_scatter(
            grad_up.astype(jnp.bfloat16), "dp", scatter_dimension=0, tiled=True
        ).astype(jnp.float32),
        lax.psum_scatter(
            grad_down.astype(jnp.bfloat16), "dp", scatter_dimension=1, tiled=True
        ).astype(jnp.float32),
    )
    d_middle = d_out + d_middle_norm
    d_attn_half = d_middle.astype(half)
    (
        gain_attn,
        query_full,
        key_full,
        value_full,
        outgate_full,
        rank_full,
        decay_full,
        bias_full,
        head_full,
        out_full,
    ) = (
        lax.all_gather(norm_attn.astype(half), "dp", axis=0, tiled=True),
        lax.all_gather(query_proj.astype(half), "dp", axis=0, tiled=True),
        lax.all_gather(key_proj.astype(half), "dp", axis=0, tiled=True),
        lax.all_gather(value_proj.astype(half), "dp", axis=0, tiled=True),
        lax.all_gather(outgate_proj.astype(half), "dp", axis=0, tiled=True),
        lax.all_gather(rank_proj.astype(half), "dp", axis=0, tiled=True),
        lax.all_gather(decay_proj.astype(half), "dp", axis=2, tiled=True),
        lax.all_gather(decay_bias.astype(half), "dp", axis=1, tiled=True),
        lax.all_gather(head_gain.astype(half), "dp", axis=0, tiled=True),
        lax.all_gather(out_proj.astype(half), "dp", axis=1, tiled=True),
    )
    grad_out = collect(gated_half, d_attn_half)
    d_gated = against(d_attn_half, out_full)
    d_query, d_key, d_value, d_outgate, d_rank, grad_decay, grad_bias, grad_head = pull_mix(d_gated)
    d_query_half = d_query.astype(half)
    d_key_half = d_key.astype(half)
    d_value_half = d_value.astype(half)
    d_outgate_half = d_outgate.astype(half)
    grad_query = collect(normed_half, d_query_half)
    grad_key = collect(normed_half, d_key_half)
    grad_value = collect(normed_half, d_value_half)
    grad_outgate = collect(normed_half, d_outgate_half)
    d_normed_part = (
        against(d_query_half, query_full)
        + against(d_key_half, key_full)
        + against(d_value_half, value_full)
        + against(d_outgate_half, outgate_full)
    )
    d_normed, d_rank_total, grad_head_total = (
        lax.psum(d_normed_part.astype(jnp.bfloat16), "tensor").astype(jnp.float32),
        lax.psum(d_rank.astype(jnp.bfloat16), "tensor").astype(jnp.float32),
        lax.psum(grad_head.astype(jnp.bfloat16), "tensor").astype(jnp.float32),
    )
    d_rank_half = d_rank_total.astype(half)
    grad_rank = collect(normed_half, d_rank_half)
    d_normed = d_normed + against(d_rank_half, rank_full)
    d_tokens_norm, grad_gain_attn = pull_first(d_normed)
    grad_tokens = (d_middle + d_tokens_norm).astype(half)
    (
        grad_norm_attn,
        grad_query_proj,
        grad_key_proj,
        grad_value_proj,
        grad_outgate_proj,
        grad_rank_proj,
        grad_decay_proj,
        grad_decay_bias,
        grad_head_gain,
        grad_out_proj,
    ) = (
        lax.psum_scatter(
            grad_gain_attn.astype(jnp.bfloat16), "dp", scatter_dimension=0, tiled=True
        ).astype(jnp.float32),
        lax.psum_scatter(
            grad_query.astype(jnp.bfloat16), "dp", scatter_dimension=0, tiled=True
        ).astype(jnp.float32),
        lax.psum_scatter(
            grad_key.astype(jnp.bfloat16), "dp", scatter_dimension=0, tiled=True
        ).astype(jnp.float32),
        lax.psum_scatter(
            grad_value.astype(jnp.bfloat16), "dp", scatter_dimension=0, tiled=True
        ).astype(jnp.float32),
        lax.psum_scatter(
            grad_outgate.astype(jnp.bfloat16), "dp", scatter_dimension=0, tiled=True
        ).astype(jnp.float32),
        lax.psum_scatter(
            grad_rank.astype(jnp.bfloat16), "dp", scatter_dimension=0, tiled=True
        ).astype(jnp.float32),
        lax.psum_scatter(
            grad_decay.astype(jnp.bfloat16), "dp", scatter_dimension=2, tiled=True
        ).astype(jnp.float32),
        lax.psum_scatter(
            grad_bias.astype(jnp.bfloat16), "dp", scatter_dimension=1, tiled=True
        ).astype(jnp.float32),
        lax.psum_scatter(
            grad_head_total.astype(jnp.bfloat16), "dp", scatter_dimension=0, tiled=True
        ).astype(jnp.float32),
        lax.psum_scatter(
            grad_out.astype(jnp.bfloat16), "dp", scatter_dimension=1, tiled=True
        ).astype(jnp.float32),
    )
    return (
        output,
        grad_tokens,
        grad_norm_attn,
        grad_query_proj,
        grad_key_proj,
        grad_value_proj,
        grad_outgate_proj,
        grad_rank_proj,
        grad_decay_proj,
        grad_decay_bias,
        grad_head_gain,
        grad_out_proj,
        grad_norm_ffn,
        grad_gate_proj,
        grad_up_proj,
        grad_down_proj,
    )


def solution(mesh):
    return jax.shard_map(
        local,
        mesh=mesh,
        in_specs=(
            P("dp", None),
            P("dp"),
            P("dp"),
            P("dp", "tensor"),
            P("dp", "tensor"),
            P("dp", "tensor"),
            P("dp", "tensor"),
            P("dp", None),
            P(None, "tensor", "dp"),
            P("tensor", "dp"),
            P("dp"),
            P("tensor", "dp"),
            P("dp"),
            P("dp", "tensor"),
            P("dp", "tensor"),
            P("tensor", "dp"),
            P("dp", None),
        ),
        out_specs=(
            P("dp", None),
            P("dp", None),
            P("dp"),
            P("dp", "tensor"),
            P("dp", "tensor"),
            P("dp", "tensor"),
            P("dp", "tensor"),
            P("dp", None),
            P(None, "tensor", "dp"),
            P("tensor", "dp"),
            P("dp"),
            P("tensor", "dp"),
            P("dp"),
            P("dp", "tensor"),
            P("dp", "tensor"),
            P("tensor", "dp"),
        ),
        check_vma=False,
    )
```

profile of v0, /device:TPU:0, one launch (start us, length us, event | category | flops | bytes accessed | tf_op | source)
XLA Modules:
  0.0 2493.8 jit_solution(15633964255061561891)
XLA Ops:
  19.4 22.3 all-gather
  41.7 30.6 %all_gather.52 = bf16[2048,16]{0,1:T(8,128)(2,1)S(1)} all-gather(bf16[256,16]{0,1:T(8,128)(2,1)S(1)} %convert_element_type.283), channel_id=1, replica_groups=mesh['dp'=8,'tensor'=4] {'dp'}, dimensions={0}, use_global_device_ids=true | all-gather | bytes 73728 | tf_op jit(solution)/shard_map/all_gather | solution.py:164
  74.7 17.5 all-reduce.7
  92.4 30.9 %all_gather.53 = bf16[16,1,256]{0,1,2:T(2,128)(2,1)S(1)} all-gather(bf16[16,1,32]{0,1,2:T(2,128)(2,1)S(1)} %copy.93), channel_id=1, replica_groups=mesh['dp'=8,'tensor'=4] {'dp'}, dimensions={2}, use_global_device_ids=true | all-gather | bytes 9216 | tf_op jit(solution)/shard_map/all_gather | solution.py:165
  153.0 229.3 %while.40 = (s32[]{:T(128)}, f32[1,1,256,512]{3,2,1,0:T(8,128)S(1)}, f32[16,1,1,64,512]{4,3,2,1,0:T(8,128)S(1)}, f32[16,1,1,256,512]{4,3,2,1,0:T(8,128)}, f32[16...) while((s32[]{:T(128)}, ...), condition=%wide.region_3.4_spmd.clone.clone, body=%wide.region_1.3_spmd.clone.sunk.clone | while | flops 245047296 | bytes 12723313 | solution.py:75
  402.8 18.1 all-gather.1
  421.6 127.8 %all-reduce.13.cloned.1.call-done = f32[1024,2048]{1,0:T(8,128)} async-done(((f32[1024,2048]{1,0:T(8,128)}), f32[1024,2048]{1,0:T(8,128)}) %all-reduce.13.cloned.1.call-update) | async-done | bytes 8388624 | tf_op jit(solution)/shard_map/psum | solution.py:193
  561.1 82.9 %all-gather.21.cloned.1.call-done = bf16[2048,1408]{1,0:T(8,128)(2,1)} async-done(((bf16[256,1408]{1,0:T(8,128)(2,1)}), bf16[2048,1408]{1,0:T(8,128)(2,1)}) %all-gather.21.cloned.1.call-update) | async-done | bytes 5767184 | tf_op jit(solution)/shard_map/all_gather | solution.py:197
  656.2 80.5 %all-gather.23.cloned.1.call-done = bf16[2048,1408]{1,0:T(8,128)(2,1)} async-done(((bf16[256,1408]{1,0:T(8,128)(2,1)}), bf16[2048,1408]{1,0:T(8,128)(2,1)}) %all-gather.23.cloned.1.call-update) | async-done | bytes 5767184 | tf_op jit(solution)/shard_map/all_gather | solution.py:198
  748.4 81.7 %all-gather.25.cloned.1.call-done = bf16[1408,2048]{1,0:T(8,128)(2,1)} async-done(((bf16[1408,256]{1,0:T(8,128)(2,1)}), bf16[1408,2048]{1,0:T(8,128)(2,1)}) %all-gather.25.cloned.1.call-update) | async-done | bytes 5767184 | tf_op jit(solution)/shard_map/all_gather | solution.py:199
  867.1 81.9 %all-reduce.15.cloned.1.call-done = bf16[1024,2048]{1,0:T(8,128)(2,1)} async-done(((bf16[1024,2048]{1,0:T(8,128)(2,1)}), bf16[1024,2048]{1,0:T(8,128)(2,1)}) %all-reduce.15.cloned.1.call-update) | async-done | bytes 4194320 | tf_op jit(solution)/shard_map/psum | solution.py:226
  969.6 466.3 %while.41 = (s32[]{:T(128)}, f32[1,1,256,512]{2,3,1,0:T(8,128)S(1)}, f32[16,1,1,64,256]{4,3,2,1,0:T(8,128)S(1)}, bf16[16,1,1,64,256]{4,3,2,1,0:T(8,128)(2,1)}, b...) while((s32[]{:T(128)}, ...), condition=%wide.region_19.20_spmd.clone.clone, body=%wide.region_11.19_spmd.clone.sunk.clone | while | flops 502210560 | bytes 24297648 | solution.py:75
  1559.2 23.8 reduce-scatter.34.cloned.1.call-done
  1584.4 56.2 %reduce-scatter.24.cloned.1.call-done = bf16[256,16]{0,1:T(8,128)(2,1)} async-done(((bf16[2048,16]{0,1:T(8,128)(2,1)}), bf16[256,16]{0,1:T(8,128)(2,1)}) %reduce-scatter.24.cloned.1.call-update) | async-done | bytes 8208 | tf_op jit(solution)/shard_map/reduce_scatter | solution.py:324
  1641.8 65.8 %reduce-scatter.16.cloned.1.call-done = bf16[256,256]{1,0:T(8,128)(2,1)} async-done(((bf16[2048,256]{1,0:T(8,128)(2,1)}), bf16[256,256]{1,0:T(8,128)(2,1)}) %reduce-scatter.16.cloned.1.call-update) | async-done | bytes 131088 | tf_op jit(solution)/shard_map/reduce_scatter | solution.py:312
  1709.2 65.5 %reduce-scatter.18.cloned.1.call-done = bf16[256,256]{1,0:T(8,128)(2,1)} async-done(((bf16[2048,256]{1,0:T(8,128)(2,1)}), bf16[256,256]{1,0:T(8,128)(2,1)}) %reduce-scatter.18.cloned.1.call-update) | async-done | bytes 131088 | tf_op jit(solution)/shard_map/reduce_scatter | solution.py:315
  1776.3 152.7 %all-reduce.17.cloned.1.call-done = (bf16[1024,2048]{1,0:T(8,128)(2,1)}, bf16[1024,2048]{1,0:T(8,128)(2,1)}) async-done(((bf16[1024,2048]{1,0:T(8,128)(2,1)}, bf16[1024,2048]{1,0:T(8,128)(2,1)}), (bf16[1024,2048]{1,0:T(8,128)(2,1)}, bf16[1024,2048]{1,0:T(8,128)(2,1)})) %all-reduce.17.cloned.1.call-update) | async-done | bytes 8388624 | tf_op jit(solution)/shard_map/psum | solution.py:207
  1936.4 22.3 all-reduce.6
  1965.2 36.4 %reduce-scatter.26.cloned.1.call-done = bf16[512,256]{1,0:T(8,128)(2,1)} async-done(((bf16[512,2048]{1,0:T(8,128)(2,1)}), bf16[512,256]{1,0:T(8,128)(2,1)}) %reduce-scatter.26.cloned.1.call-update) | async-done | bytes 262160 | tf_op jit(solution)/shard_map/reduce_scatter | solution.py:336
  2003.4 69.1 %reduce-scatter.20.cloned.1.call-done = bf16[256,512]{1,0:T(8,128)(2,1)} async-done(((bf16[2048,512]{1,0:T(8,128)(2,1)}), bf16[256,512]{1,0:T(8,128)(2,1)}) %reduce-scatter.20.cloned.1.call-update) | async-done | bytes 262160 | tf_op jit(solution)/shard_map/reduce_scatter | solution.py:318
  2074.2 69.1 %reduce-scatter.22.cloned.1.call-done = bf16[256,512]{1,0:T(8,128)(2,1)} async-done(((bf16[2048,512]{1,0:T(8,128)(2,1)}), bf16[256,512]{1,0:T(8,128)(2,1)}) %reduce-scatter.22.cloned.1.call-update) | async-done | bytes 262160 | tf_op jit(solution)/shard_map/reduce_scatter | solution.py:321
  2161.6 94.9 %reduce-scatter.28.cloned.1.call-done = bf16[256,1408]{1,0:T(8,128)(2,1)} async-done(((bf16[2048,1408]{1,0:T(8,128)(2,1)}), bf16[256,1408]{1,0:T(8,128)(2,1)}) %reduce-scatter.28.cloned.1.call-update) | async-done | bytes 720912 | tf_op jit(solution)/shard_map/reduce_scatter | solution.py:235
  2258.8 111.3 %reduce-scatter.30.cloned.1.call-done = bf16[256,1408]{1,0:T(8,128)(2,1)} async-done(((bf16[2048,1408]{1,0:T(8,128)(2,1)}), bf16[256,1408]{1,0:T(8,128)(2,1)}) %reduce-scatter.30.cloned.1.call-update) | async-done | bytes 720912 | tf_op jit(solution)/shard_map/reduce_scatter | solution.py:238
  2372.5 111.8 %reduce-scatter.32.cloned.1.call-done = bf16[1408,256]{1,0:T(8,128)(2,1)} async-done(((bf16[1408,2048]{1,0:T(8,128)(2,1)}), bf16[1408,256]{1,0:T(8,128)(2,1)}) %reduce-scatter.32.cloned.1.call-update) | async-done | bytes 720912 | tf_op jit(solution)/shard_map/reduce_scatter | solution.py:241
  (926 shorter events, 1019.1 us)
Async XLA Ops:
  7.2 125.4 %all-gather.15.cloned.1.call-start = ((), (), s32[]{:S(2)}) async-start(), calls=%async_computation.13 | async-start | bytes 1179648 | tf_op jit(solution)/shard_map/all_gather | solution.py:160
  8.9 128.4 %all-gather.11.cloned.1.call-start = ((), (), s32[]{:S(2)}) async-start(), calls=%async_computation.11 | async-start | bytes 1179648 | tf_op jit(solution)/shard_map/all_gather | solution.py:161
  10.6 135.9 %all-gather.13.cloned.1.call-start = ((), (), s32[]{:S(2)}) async-start(), calls=%async_computation.12 | async-start | bytes 2359296 | tf_op jit(solution)/shard_map/all_gather | solution.py:162
  12.5 370.2 %all-gather.17.cloned.1.call-start = ((), (), s32[]{:S(2)}) async-start(), calls=%async_computation.14 | async-start | bytes 2359296 | tf_op jit(solution)/shard_map/all_gather | solution.py:163
  14.3 375.9 %all-gather.19.cloned.1.call-start = ((), (), s32[]{:S(2)}) async-start(), calls=%async_computation.15 | async-start | bytes 2359296 | tf_op jit(solution)/shard_map/all_gather | solution.py:168
  16.2 533.2 %all-reduce.13.cloned.1.call-start = ((), (), s32[]{:S(2)}) async-start(), calls=%async_computation.16 | async-start | bytes 16777216 | tf_op jit(solution)/shard_map/psum | solution.py:193
  397.8 246.2 %all-gather.21.cloned.1.call-start = ((), (), s32[]{:S(2)}) async-start(), calls=%async_computation.17 | async-start | bytes 6488064 | tf_op jit(solution)/shard_map/all_gather | solution.py:197
  400.1 336.6 %all-gather.23.cloned.1.call-start = ((), (), s32[]{:S(2)}) async-start(), calls=%async_computation.18 | async-start | bytes 6488064 | tf_op jit(solution)/shard_map/all_gather | solution.py:198
  401.2 428.9 %all-gather.25.cloned.1.call-start = ((), (), s32[]{:S(2)}) async-start(), calls=%async_computation.19 | async-start | bytes 6488064 | tf_op jit(solution)/shard_map/all_gather | solution.py:199
  402.7 546.3 %all-reduce.15.cloned.1.call-start = ((), (), s32[]{:S(2)}) async-start(), calls=%async_computation.20 | async-start | bytes 8388608 | tf_op jit(solution)/shard_map/psum | solution.py:226
  865.2 692.7 %reduce-scatter.36.cloned.1.call-start = ((), (), s32[]{:S(2)}) async-start(), calls=%async_computation.31 | async-start | bytes 73728
  1454.6 128.4 %reduce-scatter.34.cloned.1.call-start = ((), (), s32[]{:S(2)}) async-start(), calls=%async_computation.30 | async-start | bytes 73728
  1456.0 184.5 %reduce-scatter.24.cloned.1.call-start = ((), (), s32[]{:S(2)}) async-start(), calls=%async_computation.25 | async-start | bytes 73728 | tf_op jit(solution)/shard_map/reduce_scatter | solution.py:324
  1456.8 250.8 %reduce-scatter.16.cloned.1.call-start = ((), (), s32[]{:S(2)}) async-start(), calls=%async_computation.21 | async-start | bytes 1179648 | tf_op jit(solution)/shard_map/reduce_scatter | solution.py:312
  1461.3 313.4 %reduce-scatter.18.cloned.1.call-start = ((), (), s32[]{:S(2)}) async-start(), calls=%async_computation.22 | async-start | bytes 1179648 | tf_op jit(solution)/shard_map/reduce_scatter | solution.py:315
  1474.8 454.2 %all-reduce.17.cloned.1.call-start = ((), (), s32[]{:S(2)}) async-start(), calls=%async_computation.32 | async-start | bytes 16777216 | tf_op jit(solution)/shard_map/psum | solution.py:207
  1499.2 502.4 %reduce-scatter.26.cloned.1.call-start = ((), (), s32[]{:S(2)}) async-start(), calls=%async_computation.26 | async-start | bytes 2359296 | tf_op jit(solution)/shard_map/reduce_scatter | solution.py:336
  1507.5 564.9 %reduce-scatter.20.cloned.1.call-start = ((), (), s32[]{:S(2)}) async-start(), calls=%async_computation.23 | async-start | bytes 2359296 | tf_op jit(solution)/shard_map/reduce_scatter | solution.py:318
  1513.5 629.9 %reduce-scatter.22.cloned.1.call-start = ((), (), s32[]{:S(2)}) async-start(), calls=%async_computation.24 | async-start | bytes 2359296 | tf_op jit(solution)/shard_map/reduce_scatter | solution.py:321
  1519.7 736.8 %reduce-scatter.28.cloned.1.call-start = ((), (), s32[]{:S(2)}) async-start(), calls=%async_computation.27 | async-start | bytes 6488064 | tf_op jit(solution)/shard_map/reduce_scatter | solution.py:235
  1530.9 839.3 %reduce-scatter.30.cloned.1.call-start = ((), (), s32[]{:S(2)}) async-start(), calls=%async_computation.28 | async-start | bytes 6488064 | tf_op jit(solution)/shard_map/reduce_scatter | solution.py:238
  1543.6 940.7 %reduce-scatter.32.cloned.1.call-start = ((), (), s32[]{:S(2)}) async-start(), calls=%async_computation.29 | async-start | bytes 6488064 | tf_op jit(solution)/shard_map/reduce_scatter | solution.py:241
  1556.5 372.6 %copy-start.25 = (f32[8,1,256]{2,1,0:T(1,128)S(1)}, f32[8,1,256]{2,1,0:T(1,128)}, u32[]{:S(2)}) copy-start(f32[8,1,256]{2,1,0:T(1,128)} %copy-done.24) | copy-start | bytes 24580
  1556.5 372.6 %copy-start.29 = (f32[1024]{0:T(1024)S(1)}, f32[1024]{0:T(1024)}, u32[]{:S(2)}) copy-start(f32[1024]{0:T(1024)} %copy-done.28) | copy-start | bytes 12292
  (45 other events, 1430.8 us)
Sparse Core Ops, SparseCore 0:
  10.7 43.2 all-gather.14
  56.7 38.8 all-gather.10
  98.3 48.2 all-gather.12
  149.1 47.6 all-gather.16
  199.3 49.1 all-gather.18
  397.9 151.4 all-reduce.12
  551.5 92.4 all-gather.20
  646.2 90.4 all-gather.22
  738.7 91.3 all-gather.24
  865.3 83.6 all-reduce.14
  1454.7 62.8 reduce-scatter.35
  1521.5 61.4 reduce-scatter.33
  1586.7 53.8 reduce-scatter.23
  1644.4 63.1 reduce-scatter.15
  1711.4 63.2 reduce-scatter.17
  1777.2 151.8 all-reduce.16
  1932.4 69.1 reduce-scatter.25
  2005.0 67.3 reduce-scatter.19
  2076.0 67.3 reduce-scatter.21
  2146.9 109.6 reduce-scatter.27
  2260.2 109.9 reduce-scatter.29
  2373.8 110.3 reduce-scatter.31
where the time goes:
time: 2510 us; the launch traced here: 2490 us
  waiting for transfers between devices  1320 us (53%)
  matrix products  647 us (26%)
  other arithmetic  210 us (8%)
  blocking collectives  158 us (6%)
  local copies, waits for them, and re-layouts  139 us (6%)
    dot_general x48, matrix products, group_step(): jnp.einsum('hijk,hjk->hij', weighted, key_matrix, precision=highest_preci...  316 us
    psum x1, waiting for transfers between devices, local(): lax.psum(project(hidden_half, down_full).astype(jnp.bfloat16), 'tensor')  153 us
    psum x1, waiting for transfers between devices, local(): attn = lax.psum(project(gated_half, out_full), 'tensor')  128 us
    reduce_scatter x1, waiting for transfers between devices, local(): lax.psum_scatter(grad_down.astype(jnp.bfloat16), 'dp', scatter_dimension=...  112 us
    reduce_scatter x1, waiting for transfers between devices, local(): lax.psum_scatter(grad_up.astype(jnp.bfloat16), 'dp', scatter_dimension=0,...  111 us
    reduce_scatter x1, waiting for transfers between devices, local(): lax.psum_scatter(grad_gate.astype(jnp.bfloat16), 'dp', scatter_dimension=...  94.9 us
    all_gather x1, waiting for transfers between devices, local(): lax.all_gather(gate_proj.astype(half), 'dp', axis=0, tiled=True)  82.9 us
    psum x1, waiting for transfers between devices, local(): lax.psum((against(d_gate_half, gate_full) + against(d_up_half, up_full))....  81.9 us
  transfers between devices with their start and end apart: 22, of which 17 were waited for; matrix products, arithmetic and copies ran while one was open for 18% of the time, Pallas kernels for 0%

commit v1 on v0

v1 whole, which is shorter than its diff:
```python
import jax
import jax.numpy as jnp
from jax import lax
from jax.experimental import pallas as pl
from jax.experimental.pallas import tpu as pltpu
from jax.sharding import PartitionSpec as P

SEQ_LEN = 1024
LINE = 4

norm_eps = 1e-06
head_eps = 1.0
highest_precision = lax.Precision.HIGHEST
half = jnp.bfloat16
f32 = jnp.float32
CHUNK = 128


def level_count():
    return CHUNK.bit_length() - 1


def span_matrix():
    rows = lax.broadcasted_iota(jnp.int32, (CHUNK, CHUNK), 0)
    cols = lax.broadcasted_iota(jnp.int32, (CHUNK, CHUNK), 1)
    parts = []
    for level in range(level_count()):
        size = 1 << level
        middle = (rows // (2 * size)) * (2 * size) + size
        right = rows >= middle
        parts.append(
            jnp.where(right, (cols >= middle) & (cols <= rows), (cols > rows) & (cols < middle))
        )
    parts.append(cols <= rows)
    parts.append(cols > rows)
    stacked = jnp.concatenate(parts, axis=0).astype(half)
    return jnp.concatenate([stacked, stacked], axis=1)


def dot(left, right, dims):
    return lax.dot_general(left, right, (dims, ((), ())), preferred_element_type=f32)


NN = ((1,), (0,))
NT = ((1,), (1,))
TN = ((0,), (0,))


def log_decay(pre):
    return (jnp.minimum(pre, 0.0) - jnp.log1p(jnp.exp(-jnp.abs(pre)))) * (1.0 / 16.0)


def split_two(values):
    high = values.astype(half)
    low = (values - high.astype(f32)).astype(half)
    return jnp.concatenate([high, low], axis=0)


def level_parts(level):
    rows = lax.broadcasted_iota(jnp.int32, (CHUNK, CHUNK), 0)
    cols = lax.broadcasted_iota(jnp.int32, (CHUNK, CHUNK), 1)
    return rows, cols, (lax.shift_right_logical(rows ^ cols, level) == 1)


def forward_body(pre_ref, q_ref, k_ref, v_ref, span_ref, mixed_ref, score_ref, state_ref, state):
    @pl.when(pl.program_id(0) == 0)
    def _():
        state[...] = jnp.zeros_like(state)

    decay = log_decay(pre_ref[...])
    sums = dot(span_ref[...], split_two(decay), NN)
    q = q_ref[...]
    k = k_ref[...]
    v = v_ref[...]
    q32 = q.astype(f32)
    k32 = k.astype(f32)
    rows, cols, _ = level_parts(0)
    scores = jnp.where(rows == cols, dot(q, k, NT), 0.0)
    row_ids = lax.broadcasted_iota(jnp.int32, q.shape, 0)
    for level in range(level_count()):
        right = (lax.shift_right_logical(row_ids, level) & 1) == 1
        grow = jnp.exp(sums[level * CHUNK : (level + 1) * CHUNK])
        mixed_rows = (jnp.where(right, q32, k32) * grow).astype(half)
        pair = level_parts(level)[2] & (rows > cols)
        scores = jnp.where(pair, dot(mixed_rows, mixed_rows, NT), scores)
    levels = level_count()
    head_sum = sums[levels * CHUNK : (levels + 1) * CHUNK]
    tail_sum = sums[(levels + 1) * CHUNK :]
    q_in = (q32 * jnp.exp(head_sum)).astype(half)
    k_out = (k32 * jnp.exp(tail_sum)).astype(half)
    score_half = scores.astype(half)
    state_now = state[...]
    state_half = state_now.astype(half)
    mixed_ref[...] = (dot(score_half, v, NN) + dot(q_in, state_half, NN)).astype(mixed_ref.dtype)
    score_ref[...] = score_half
    state_ref[0] = state_half
    whole = jnp.exp(jnp.transpose(head_sum[CHUNK - 8 :, :]))[:, 7:8]
    state[...] = whole * state_now + dot(k_out, v, TN)


def backward_body(
    pre_ref, q_ref, k_ref, v_ref, d_ref, score_ref, state_ref, span_ref,
    dqkv_ref, dpre_ref, carry,
):
    @pl.when(pl.program_id(0) == 0)
    def _():
        carry[...] = jnp.zeros_like(carry)

    levels = level_count()
    pre = pre_ref[...]
    decay = log_decay(pre)
    sums = dot(span_ref[...], split_two(decay), NN)
    q = q_ref[...]
    k = k_ref[...]
    v = v_ref[...]
    d_mixed = d_ref[...]
    q32 = q.astype(f32)
    k32 = k.astype(f32)
    scores = score_ref[...]
    state_half = state_ref[0]
    carry_now = carry[...]
    carry_half = carry_now.astype(half)
    rows, cols, _ = level_parts(0)
    row_ids = lax.broadcasted_iota(jnp.int32, q.shape, 0)
    d_scores = dot(d_mixed, v, NT)
    diagonal = jnp.where(rows == cols, d_scores, 0.0)
    sym = jnp.where(rows > cols, d_scores, jnp.transpose(d_scores))
    diag_col = jnp.sum(diagonal, axis=1, keepdims=True)
    dq = diag_col * k32
    dk = diag_col * q32
    pieces = []
    for level in range(levels):
        right = (lax.shift_right_logical(row_ids, level) & 1) == 1
        grow = jnp.exp(sums[level * CHUNK : (level + 1) * CHUNK])
        scaled = jnp.where(right, q32, k32) * grow
        block = jnp.where(level_parts(level)[2], sym, 0.0).astype(half)
        back = dot(block, scaled.astype(half), NN)
        pieces.append((scaled * back).astype(half))
        grown = grow * back
        dq = dq + jnp.where(right, grown, 0.0)
        dk = dk + jnp.where(right, 0.0, grown)
    head_sum = sums[levels * CHUNK : (levels + 1) * CHUNK]
    tail_sum = sums[(levels + 1) * CHUNK :]
    head_grow = jnp.exp(head_sum)
    tail_grow = jnp.exp(tail_sum)
    q_in = q32 * head_grow
    k_out = k32 * tail_grow
    k_out_half = k_out.astype(half)
    back_q = dot(d_mixed, state_half, NT)
    back_k = dot(v, carry_half, NT)
    pieces.append((q_in * back_q).astype(half))
    pieces.append((k_out * back_k).astype(half))
    dq = dq + head_grow * back_q
    dk = dk + tail_grow * back_k
    wide = q.shape[1]
    dqkv_ref[:, :wide] = dq.astype(half)
    dqkv_ref[:, wide : 2 * wide] = dk.astype(half)
    dqkv_ref[:, 2 * wide :] = (
        dot(scores, d_mixed, TN) + dot(k_out_half, carry_half, NN)
    ).astype(half)
    whole = jnp.exp(jnp.transpose(head_sum[CHUNK - 8 :, :]))[:, 7:8]
    end_col = whole * jnp.sum(state_half.astype(f32) * carry_now, axis=1, keepdims=True)
    end_row = jnp.transpose(jnp.broadcast_to(end_col, (end_col.shape[0], 128)))[0:1, :]
    d_decay = dot(span_ref[:, :CHUNK], jnp.concatenate(pieces, axis=0), TN) + end_row
    dpre_ref[...] = d_decay * (jax.nn.sigmoid(-pre) * (1.0 / 16.0))
    carry[...] = whole * carry_now + dot(q_in.astype(half), d_mixed, TN)


def recur_forward(pre, qkv, span, dk, dv):
    length = qkv.shape[0]
    count = length // CHUNK

    def row(wide, place=0):
        return pl.BlockSpec((CHUNK, wide), lambda i: (i, place))

    return pl.pallas_call(
        forward_body,
        grid=(count,),
        in_specs=[
            row(dk), row(dk, 0), row(dk, 1), row(dv, 2 * dk // dv),
            pl.BlockSpec(span.shape, lambda i: (0, 0)),
        ],
        out_specs=[row(dv), row(CHUNK), pl.BlockSpec((1, dk, dv), lambda i: (i, 0, 0))],
        out_shape=[
            jax.ShapeDtypeStruct((length, dv), half),
            jax.ShapeDtypeStruct((length, CHUNK), half),
            jax.ShapeDtypeStruct((count, dk, dv), half),
        ],
        scratch_shapes=[pltpu.VMEM((dk, dv), f32)],
        compiler_params=pltpu.CompilerParams(dimension_semantics=("arbitrary",)),
        cost_estimate=pl.CostEstimate(
            flops=6 * 10**9, bytes_accessed=8 * 2**20, transcendentals=2 * 2**20
        ),
        name="recur_forward",
    )(pre, qkv, qkv, qkv, span)


def recur_backward(pre, qkv, d_mixed, scores, states, span, dk, dv):
    length = qkv.shape[0]
    count = length // CHUNK

    def row(wide, place=0):
        return pl.BlockSpec((CHUNK, wide), lambda i: (count - 1 - i, place))

    return pl.pallas_call(
        backward_body,
        grid=(count,),
        in_specs=[
            row(dk), row(dk, 0), row(dk, 1), row(dv, 2 * dk // dv), row(dv), row(CHUNK),
            pl.BlockSpec((1, dk, dv), lambda i: (count - 1 - i, 0, 0)),
            pl.BlockSpec(span.shape, lambda i: (0, 0)),
        ],
        out_specs=[row(2 * dk + dv), row(dk)],
        out_shape=[
            jax.ShapeDtypeStruct((length, 2 * dk + dv), half),
            jax.ShapeDtypeStruct((length, dk), f32),
        ],
        scratch_shapes=[pltpu.VMEM((dk, dv), f32)],
        compiler_params=pltpu.CompilerParams(dimension_semantics=("arbitrary",)),
        cost_estimate=pl.CostEstimate(
            flops=8 * 10**9, bytes_accessed=10 * 2**20, transcendentals=2 * 2**20
        ),
        name="recur_backward",
    )(pre, qkv, qkv, qkv, d_mixed, scores, states, span)

MESH = pl.DeviceIdType.MESH
BULK = 13
PIECES = 4


class Links:
    def __init__(self, send, recv, local):
        place = lax.axis_index("dp")
        self.z = place // 2
        self.x = place % 2
        self.t = lax.axis_index("tensor")
        self.core = self.t % 2
        self.send, self.recv, self.local = send, recv, local
        self.count = 0
        self.local_count = 0

    def take(self, number=1):
        first = self.count
        self.count += number
        return first

    def take_local(self, number=1):
        first = self.local_count
        self.local_count += number
        return first

    def beside(self):
        return {"dp": self.z * 2 + 1 - self.x}

    def up(self):
        return {"dp": self.z * 2 + 2 + self.x}

    def down(self):
        return {"dp": self.z * 2 - 2 + self.x}

    def partner(self):
        return {"tensor": self.t + 1 - 2 * self.core}

    def across(self):
        return {"tensor": (self.t + 2) % 4}

    def greet(self):
        barrier = pltpu.get_barrier_semaphore()
        around = [{"dp": ((self.z + step) % LINE) * 2 + self.x} for step in (1, 3)]
        for other in (*around, self.beside(), self.partner(), self.across()):
            pl.semaphore_signal(barrier, inc=1, device_id=other, device_id_type=MESH)
        pl.semaphore_wait(barrier, 5)

    def copy(self, index, src, dst, target):
        return pltpu.make_async_remote_copy(
            src_ref=src,
            dst_ref=dst,
            send_sem=self.send.at[index],
            recv_sem=self.recv.at[index],
            device_id=target,
            device_id_type=MESH,
        )

    def arrived(self, index, dst):
        self.copy(index, dst, dst, self.beside()).wait_recv()

    def sent(self, index, src):
        self.copy(index, src, src, self.beside()).wait_send()


class Gather:
    SEMS = 26

    def __init__(self, links, shard, full):
        self.links, self.shard, self.full = links, shard, full
        self.rows = shard.shape[0]
        self.bulk = self.rows * BULK // 16
        self.base = links.take(self.SEMS)
        self.own_sem = links.take_local()
        self.pending = []

    def at(self, z, x, rest):
        first = (z * 2 + x) * self.rows + (self.bulk if rest else 0)
        return self.full.at[pl.ds(first, self.rows - self.bulk if rest else self.bulk), :]

    def mine(self, rest):
        if rest:
            return self.shard.at[pl.ds(self.bulk, self.rows - self.bulk), :]
        return self.shard.at[pl.ds(0, self.bulk), :]

    def go(self, index, src, dst, target, when=None):
        links = self.links

        def start():
            links.copy(self.base + index, src, dst, target).start()

        if when is None:
            start()
        else:
            pl.when(when)(start)
        self.pending.append((index, src, when))

    def start(self):
        links = self.links
        z, x = links.z, links.x
        keep = self.full.at[pl.ds((z * 2 + x) * self.rows, self.rows), :]
        self.keep = pltpu.make_async_copy(self.shard, keep, links.local.at[self.own_sem])
        self.keep.start()
        self.go(0, self.mine(False), self.at(z, x, False), links.up(), z < 3)
        self.go(3, self.mine(False), self.at(z, x, False), links.down(), z > 0)
        self.go(13, self.mine(True), self.at(z, x, True), links.beside())
        self.go(6, self.mine(False), self.at(z, x, False), links.beside())

    def bulk_step(self, k):
        links = self.links
        z, x = links.z, links.x
        for side, base, cross, target, more in (
            (-k, 0, 7, links.up(), z < 3),
            (k, 3, 10, links.down(), z > 0),
        ):
            there = z + side
            valid = there >= 0 if side < 0 else there <= 3
            piece = self.at(there, x, False)

            @pl.when(valid)
            def _():
                links.arrived(self.base + base + k - 1, piece)

            if k < 3:
                self.go(base + k, piece, piece, target, valid & more)
            self.go(cross + k - 1, piece, piece, links.beside(), valid)

    def rest_start(self):
        links = self.links
        z, x = links.z, links.x
        other = self.at(z, 1 - x, True)
        links.arrived(self.base + 13, other)
        mine = self.mine(True)
        for index, src, dst in ((14, mine, self.at(z, x, True)), (15, other, other)):
            self.go(index, src, dst, links.up(), z < 3)
            self.go(index + 6, src, dst, links.down(), z > 0)

    def rest_step(self, k):
        links = self.links
        z, x = links.z, links.x
        for side, base, target, more in (
            (-k, 14, links.up(), z < 3),
            (k, 20, links.down(), z > 0),
        ):
            there = z + side
            valid = there >= 0 if side < 0 else there <= 3
            for which in range(2):
                piece = self.at(there, x if which == 0 else 1 - x, True)

                @pl.when(valid)
                def _():
                    links.arrived(self.base + base + 2 * (k - 1) + which, piece)

                if k < 3:
                    self.go(base + 2 * k + which, piece, piece, target, valid & more)

    def finish(self):
        links = self.links
        z, x = links.z, links.x
        links.arrived(self.base + 6, self.at(z, 1 - x, False))
        for k in (1, 2, 3):
            for side, cross in ((-k, 7), (k, 10)):
                there = z + side
                valid = there >= 0 if side < 0 else there <= 3

                @pl.when(valid)
                def _():
                    links.arrived(self.base + cross + k - 1, self.at(there, 1 - x, False))

        for index, src, when in self.pending:

            def done():
                links.sent(self.base + index, src)

            if when is None:
                done()
            else:
                pl.when(when)(done)
        self.keep.wait()


def add_rows(out, outs_at, terms, rows):
    def body(i, carry):
        tile = pl.ds(pl.multiple_of(i * 16, 16), 16)
        value = terms[0][tile, :].astype(f32)
        for term in terms[1:]:
            value = value + term[tile, :].astype(f32)
        out[pl.ds(pl.multiple_of(outs_at + i * 16, 16), 16), :] = value.astype(out.dtype)
        return carry

    lax.fori_loop(0, rows // 16, body, 0)


ORDER = ((3, 3, 0, 0), (2, 0, 3, 1), (1, 2, 1, 2), (0, 1, 2, 3))


class Scatter:
    SEMS = 15

    def __init__(self, links, total, own, buffers):
        self.links, self.total, self.own = links, total, own
        self.beside, self.kept, self.passed, self.kept2, self.passed2, self.last = buffers
        self.rows = total.shape[0] // (2 * LINE)
        self.bulk = self.rows * BULK // 16
        self.rest = self.rows - self.bulk
        self.base = links.take(self.SEMS)
        self.loads = links.take_local(12)
        low, high = links.z % 2, links.z // 2
        self.order = []
        for c in ORDER:
            self.order.append(
                c[0] + (c[1] - c[0]) * low + (c[2] - c[0]) * high
                + (c[3] - c[1] - c[2] + c[0]) * low * high
            )

    @staticmethod
    def scratch(rows, n):
        bulk = rows * BULK // 16
        rest = rows - bulk
        return [
            pltpu.VMEM((LINE, bulk, n), half),
            pltpu.VMEM((LINE, bulk, n), half),
            pltpu.VMEM((LINE + 1, bulk, n), half),
            pltpu.VMEM((LINE, 2 * rest, n), half),
            pltpu.VMEM((LINE + 1, 2 * rest, n), half),
            pltpu.VMEM((rest, n), half),
        ]

    def block(self, z, x, rest):
        first = (z * 2 + x) * self.rows + (self.bulk if rest else 0)
        return self.total.at[pl.ds(first, self.rest if rest else self.bulk), :]

    def load(self, k, part):
        links = self.links
        d = self.order[k]
        if part == 2:
            src, dst = self.block(d, links.x, False), self.kept.at[k]
        else:
            src = self.block(d, part, True)
            dst = self.kept2.at[k, pl.ds(part * self.rest, self.rest), :]
        return pltpu.make_async_copy(src, dst, links.local.at[self.loads + 3 * k + part])

    def start(self):
        links = self.links
        for k in range(LINE):
            for part in range(3):
                self.load(k, part).start()
        for k in range(LINE):
            src = self.block(self.order[k], 1 - links.x, False)
            links.copy(self.base + k, src, self.beside.at[k], links.beside()).start()

    def step(self, k, rest):
        links = self.links
        z = links.z
        d = self.order[k]
        if rest:
            kept, passed, rows, first = self.kept2.at[k], self.passed2, 2 * self.rest, self.base + 9
            self.load(k, 0).wait()
            self.load(k, 1).wait()
            terms = [kept]
        else:
            kept, passed, rows, first = self.kept.at[k], self.passed, self.bulk, self.base + 4
            self.load(k, 2).wait()
            links.arrived(self.base + k, self.beside.at[k])
            terms = [kept, self.beside.at[k]]
        upward = d > z
        carried = (upward & (z > 0)) | ((d < z) & (z < 3))

        @pl.when(carried)
        def _():
            links.arrived(first + d, passed.at[d])
            add_rows(kept, 0, terms + [passed.at[d]], rows)

        if not rest:

            @pl.when(jnp.logical_not(carried))
            def _():
                add_rows(kept, 0, terms, rows)

        @pl.when(upward)
        def _():
            links.copy(first + d, kept, passed.at[d], links.up()).start()

        @pl.when((d < z) & (d < z - 1))
        def _():
            links.copy(first + d, kept, passed.at[d], links.down()).start()

        @pl.when((d < z) & (d == z - 1))
        def _():
            links.copy(first + LINE, kept, passed.at[LINE], links.down()).start()

    def close(self, rest):
        links = self.links
        z, x = links.z, links.x
        k = LINE - 1
        if rest:
            kept, passed, rows, first = self.kept2.at[k], self.passed2, 2 * self.rest, self.base + 9
            self.load(k, 0).wait()
            self.load(k, 1).wait()
            terms, out = [kept], kept
        else:
            kept, passed, rows, first = self.kept.at[k], self.passed, self.bulk, self.base + 4
            self.load(k, 2).wait()
            links.arrived(self.base + k, self.beside.at[k])
            terms, out = [kept, self.beside.at[k]], self.own

        @pl.when(z > 0)
        def _():
            links.arrived(first + z, passed.at[z])

        @pl.when(z < 3)
        def _():
            links.arrived(first + LINE, passed.at[LINE])

        @pl.when(z == 0)
        def _():
            add_rows(out, 0, terms + [passed.at[LINE]], rows)

        @pl.when(z == 3)
        def _():
            add_rows(out, 0, terms + [passed.at[z]], rows)

        @pl.when((z > 0) & (z < 3))
        def _():
            add_rows(out, 0, terms + [passed.at[z], passed.at[LINE]], rows)

        if rest:
            away = kept.at[pl.ds((1 - x) * self.rest, self.rest), :]
            links.copy(self.base + 14, away, self.last, links.beside()).start()

    def finish(self):
        links = self.links
        z, x = links.z, links.x
        links.arrived(self.base + 14, self.last)
        mine = self.kept2.at[LINE - 1, pl.ds(x * self.rest, self.rest), :]
        add_rows(self.own, self.bulk, [mine, self.last], self.rest)
        links.sent(self.base + 14, self.last)
        for k in range(LINE):
            links.sent(self.base + k, self.beside.at[k])
        for k in range(LINE - 1):
            d = self.order[k]
            for kept, first in ((self.kept.at[k], self.base + 4), (self.kept2.at[k], self.base + 9)):

                @pl.when((d > z) | (d < z - 1))
                def _():
                    links.sent(first + d, kept)

                @pl.when(d == z - 1)
                def _():
                    links.sent(first + LINE, kept)


class Total:
    SEMS = 3 * PIECES

    def __init__(self, links, part, out, buffers):
        self.links, self.part, self.out = links, part, out
        self.mine, self.first, self.second = buffers
        self.rows = part.shape[0] // 2 // PIECES
        self.base = links.take(self.SEMS)
        self.loads = links.take_local(2 * PIECES)

    @staticmethod
    def scratch(rows, n):
        return [pltpu.VMEM((PIECES, rows // 2 // PIECES, n), half) for _ in range(3)]

    def at(self, ref, core, j):
        return ref.at[pl.ds((core * PIECES + j) * self.rows, self.rows), :]

    def load(self, j):
        src = self.at(self.part, self.links.core, j)
        return pltpu.make_async_copy(src, self.mine.at[j], self.links.local.at[self.loads + j])

    def store(self, j):
        dst = self.at(self.out, self.links.core, j)
        sem = self.links.local.at[self.loads + PIECES + j]
        return pltpu.make_async_copy(self.first.at[j], dst, sem)

    def start(self):
        links = self.links
        for j in range(PIECES):
            self.load(j).start()
            src = self.at(self.part, 1 - links.core, j)
            links.copy(self.base + j, src, self.first.at[j], links.partner()).start()

    def middle(self):
        links = self.links
        for j in range(PIECES):
            self.load(j).wait()
            links.arrived(self.base + j, self.first.at[j])
            add_rows(self.mine.at[j], 0, [self.mine.at[j], self.first.at[j]], self.rows)
            index = self.base + PIECES + j
            links.copy(index, self.mine.at[j], self.second.at[j], links.across()).start()

    def spread(self):
        links = self.links
        for j in range(PIECES):
            links.arrived(self.base + PIECES + j, self.second.at[j])
            add_rows(self.first.at[j], 0, [self.mine.at[j], self.second.at[j]], self.rows)
            index = self.base + 2 * PIECES + j
            dst = self.at(self.out, links.core, j)
            links.copy(index, self.first.at[j], dst, links.partner()).start()
            self.store(j).start()

    def finish(self):
        links = self.links
        for j in range(PIECES):
            links.arrived(self.base + 2 * PIECES + j, self.at(self.out, 1 - links.core, j))
            self.store(j).wait()
            for stage in range(3):
                links.sent(self.base + stage * PIECES + j, self.mine.at[j])


def exchange(number, shards=(), totals=(), parts=()):
    gathers, scatters, sums = len(shards), len(totals), len(parts)
    scratch = []
    for total in totals:
        scratch += Scatter.scratch(total.shape[0] // (2 * LINE), total.shape[1])
    for part in parts:
        scratch += Total.scratch(part.shape[0], part.shape[1])
    remote = Gather.SEMS * gathers + Scatter.SEMS * scatters + Total.SEMS * sums
    near = gathers + 12 * scatters + 2 * PIECES * sums
    scratch += [
        pltpu.SemaphoreType.DMA((remote,)),
        pltpu.SemaphoreType.DMA((remote,)),
        pltpu.SemaphoreType.DMA((near,)),
    ]

    def kernel(*refs):
        refs = list(refs)

        def pop(count):
            taken, refs[:count] = refs[:count], []
            return taken

        shard_refs, total_refs, part_refs = pop(gathers), pop(scatters), pop(sums)
        full_refs, own_refs, sum_refs = pop(gathers), pop(scatters), pop(sums)
        buffers = [pop(6) for _ in range(scatters)]
        sum_buffers = [pop(3) for _ in range(sums)]
        links = Links(*refs)
        gather = [Gather(links, s, f) for s, f in zip(shard_refs, full_refs)]
        scatter = [Scatter(links, *a) for a in zip(total_refs, own_refs, buffers)]
        total = [Total(links, *a) for a in zip(part_refs, sum_refs, sum_buffers)]
        links.greet()
        for item in gather + scatter + total:
            item.start()
        for item in total:
            item.middle()
        for k in range(LINE - 1):
            for item in scatter:
                item.step(k, True)
        for item in scatter:
            item.close(True)
        for item in gather:
            item.bulk_step(1)
        for item in gather:
            item.rest_start()
        for item in scatter:
            item.step(0, False)
        for item in gather:
            item.bulk_step(2)
        for item in gather:
            item.rest_step(1)
        for item in scatter:
            item.step(1, False)
        for item in gather:
            item.bulk_step(3)
        for item in scatter:
            item.step(2, False)
        for item in total:
            item.spread()
        for item in gather:
            item.rest_step(2)
        for item in scatter:
            item.close(False)
        for item in gather:
            item.rest_step(3)
        for item in gather + scatter + total:
            item.finish()

    whole = pl.BlockSpec(memory_space=pl.ANY)
    near_spec = pl.BlockSpec(memory_space=pltpu.VMEM)
    outs = pl.pallas_call(
        kernel,
        in_specs=[near_spec] * gathers + [whole] * (scatters + sums),
        out_specs=[whole] * gathers + [near_spec] * scatters + [whole] * sums,
        out_shape=[
            jax.ShapeDtypeStruct((s.shape[0] * 2 * LINE, s.shape[1]), half) for s in shards
        ]
        + [jax.ShapeDtypeStruct((t.shape[0] // (2 * LINE), t.shape[1]), f32) for t in totals]
        + [jax.ShapeDtypeStruct(p.shape, half) for p in parts],
        scratch_shapes=scratch,
        compiler_params=pltpu.CompilerParams(
            collective_id=number, has_side_effects=True, vmem_limit_bytes=60 * 2**20
        ),
        name=f"exchange_{number}",
    )(*shards, *totals, *parts)
    return outs[:gathers], outs[gathers : gathers + scatters], outs[gathers + scatters :]


class Ring:
    def __init__(self, size):
        self.size = size
        self.wide = size // LINE
        place = lax.axis_index("dp")
        self.z = place // self.wide
        self.x = place % self.wide

    def z_pairs(self, step):
        wide = self.wide
        return [
            (z * wide + x, ((z + step) % LINE) * wide + x) for z in range(LINE) for x in range(wide)
        ]

    def x_pairs(self, step):
        wide = self.wide
        return [(z * wide + x, z * wide + (x + step) % wide) for z in range(LINE) for x in range(wide)]


def gather(ring, shard):
    rows = shard.shape[0]
    pieces = [(ring.z, shard)]
    for step in (1, 3, 2):
        pieces.append(((ring.z - step) % LINE, lax.ppermute(shard, "dp", ring.z_pairs(step))))
    out = jnp.zeros((ring.size * rows, shard.shape[1]), shard.dtype)
    for z, piece in pieces:
        for step in range(ring.wide):
            moved = lax.ppermute(piece, "dp", ring.x_pairs(step)) if step else piece
            place = z * ring.wide + (ring.x - step) % ring.wide
            out = lax.dynamic_update_slice(out, moved, (place * rows, 0))
    return out


def scatter(ring, total):
    rows = total.shape[0] // ring.size

    def block(z, x):
        place = (z % LINE) * ring.wide + x % ring.wide
        return lax.dynamic_slice(total, (place * rows, 0), (rows, total.shape[1]))

    result = None
    for step in (2, 1, 3, 0):
        z = ring.z + step
        kept = block(z, ring.x).astype(f32)
        for side in range(1, ring.wide):
            away = lax.ppermute(block(z, ring.x + side), "dp", ring.x_pairs(side))
            kept = kept + away.astype(f32)
        if step:
            kept = lax.ppermute(kept.astype(half), "dp", ring.z_pairs(step)).astype(f32)
        result = kept if result is None else result + kept
    return result


CORE = [(i, i ^ 1) for i in range(4)]
ACROSS = [(i, i ^ 2) for i in range(4)]


def tensor_sum(part):
    rows = part.shape[0] // 2
    second = (lax.axis_index("tensor") & 1) == 1
    upper, lower = part[:rows], part[rows:]
    mine = jnp.where(second, lower, upper)
    away = jnp.where(second, upper, lower)
    mine = (mine.astype(f32) + lax.ppermute(away, "tensor", CORE).astype(f32)).astype(half)
    mine = (mine.astype(f32) + lax.ppermute(mine, "tensor", ACROSS).astype(f32)).astype(half)
    theirs = lax.ppermute(mine, "tensor", CORE)
    return jnp.concatenate(
        [jnp.where(second, theirs, mine), jnp.where(second, mine, theirs)], axis=0
    )


def rms_parts(values):
    scale = lax.rsqrt(jnp.mean(values * values, axis=-1, keepdims=True) + norm_eps)
    return values * scale, scale


def rms_back(unit, scale, gain, cot):
    weighted = cot * gain
    inner = jnp.mean(weighted * unit, axis=-1, keepdims=True)
    return scale * (weighted - unit * inner), jnp.sum(cot * unit, axis=0)


def gated_rows(mixed, outgate, gain):
    scale = lax.rsqrt(jnp.mean(mixed * mixed, axis=-1, keepdims=True) + head_eps)
    return mixed * scale * gain * jax.nn.silu(outgate)


def local(
    tokens, lengths, norm_attn, query_proj, key_proj, value_proj, outgate_proj, rank_proj,
    decay_proj, decay_bias, head_gain, out_proj, norm_ffn, gate_proj, up_proj, down_proj, cotangent,
    *, size,
):
    ring = Ring(size)
    rows_total = tokens.shape[0]
    width = norm_attn.shape[0]
    rank = rank_proj.shape[1]
    dk = query_proj.shape[1]
    dv = value_proj.shape[1]
    ff = gate_proj.shape[1]
    bits = decay_proj.shape[2]
    gains = head_gain.shape[0]

    def as_column(values):
        flat = values.reshape(-1, 1)
        return jnp.pad(flat, ((0, width - flat.shape[0]), (0, 0)))

    decay_cols = rank * bits // width
    small = jnp.concatenate(
        [
            rank_proj,
            norm_attn[:, None],
            norm_ffn[:, None],
            as_column(head_gain),
            as_column(decay_bias),
            decay_proj.reshape(decay_cols, width).T,
        ],
        axis=1,
    )
    small = jnp.pad(small, ((0, 0), (0, 128 - small.shape[1]))).astype(half)
    qkv = jnp.concatenate([query_proj * 0.0625, key_proj, value_proj], axis=1).astype(half)
    first = (qkv, small, outgate_proj.astype(half), out_proj.T.astype(half))
    second = (gate_proj.astype(half), up_proj.astype(half), down_proj.T.astype(half))
    fast = size == 2 * LINE

    def collect(number, shards, parts):
        if fast:
            fulls, _, sums = exchange(number, shards, (), parts)
            return fulls, sums
        return [gather(ring, s) for s in shards], [tensor_sum(p) for p in parts]

    def deliver(number, totals, parts):
        if fast:
            _, owns, sums = exchange(number, (), totals, parts)
            return owns, sums
        return [scatter(ring, t) for t in totals], [tensor_sum(p) for p in parts]

    (qkv_full, small_full, outgate_full, out_full), _ = collect(0, first, ())
    rank_full = small_full[:, :rank]
    small32 = small_full.astype(f32)
    gain_attn = small32[:, rank]
    gain_ffn = small32[:, rank + 1]
    by_place = small32.reshape(size, width, 128)
    gain_head = by_place[:, :gains, rank + 2].reshape(-1)
    bias = by_place[:, :bits, rank + 3].reshape(-1)
    decay_weight = jnp.transpose(
        jnp.transpose(by_place[:, :, rank + 4 : rank + 4 + decay_cols], (0, 2, 1)).reshape(
            size, rank, bits
        ),
        (1, 0, 2),
    ).reshape(rank, -1)

    positions = jnp.arange(SEQ_LEN, dtype=jnp.int32)
    mask = (positions[None, :] < lengths[:, None]).astype(f32).reshape(rows_total, 1)
    tokens32 = tokens.astype(f32)
    unit, scale = rms_parts(tokens32)
    normed = (unit * gain_attn).astype(half)
    qkv = dot(normed, qkv_full, NN).astype(half)
    rank_rows = dot(normed, rank_full, NN)
    pre = (
        jnp.dot(rank_rows, decay_weight, precision=highest_precision, preferred_element_type=f32)
        + bias
    )
    span = span_matrix()
    mixed, scores, states = recur_forward(pre, qkv, span, dk, dv)
    outgate = dot(normed, outgate_full, NN).astype(half)
    gated, pull_gated = jax.vjp(gated_rows, mixed.astype(f32), outgate.astype(f32), gain_head)
    gated = gated.astype(half)
    (gate_full, up_full, down_full), (attn,) = collect(
        1, second, (dot(gated, out_full, NT).astype(half),)
    )
    middle = tokens32 + attn.astype(f32)
    unit_ffn, scale_ffn = rms_parts(middle)
    normed_ffn = (unit_ffn * gain_ffn).astype(half)
    gate_rows = dot(normed_ffn, gate_full, NN)
    up_rows = dot(normed_ffn, up_full, NN)
    hidden, pull_glu = jax.vjp(lambda g, u: jax.nn.silu(g) * u, gate_rows, up_rows)
    hidden = hidden.astype(half)
    d_out = cotangent.astype(f32) * mask
    d_out_half = d_out.astype(half)
    grad_down = dot(d_out_half, hidden, TN).astype(half)
    d_gate, d_up = pull_glu(dot(d_out_half, down_full, NN))
    d_gate = d_gate.astype(half)
    d_up = d_up.astype(half)
    d_normed_ffn = (dot(d_gate, gate_full, NT) + dot(d_up, up_full, NT)).astype(half)
    grad_gate = dot(normed_ffn, d_gate, TN).astype(half)
    grad_up = dot(normed_ffn, d_up, TN).astype(half)
    ffn = dot(hidden, down_full, NT).astype(half)
    (down_own, gate_own, up_own), (d_normed_ffn, ffn) = deliver(
        2, (grad_down, grad_gate, grad_up), (d_normed_ffn, ffn)
    )
    output = (mask * (middle + ffn.astype(f32))).astype(half)
    d_back, grad_gain_ffn = rms_back(unit_ffn, scale_ffn, gain_ffn, d_normed_ffn.astype(f32))
    d_middle = d_out + d_back
    d_attn = d_middle.astype(half)
    grad_out = dot(d_attn, gated, TN).astype(half)
    d_mixed, d_outgate, grad_head = pull_gated(dot(d_attn, out_full, NN))
    d_outgate = d_outgate.astype(half)
    grad_outgate = dot(normed, d_outgate, TN).astype(half)
    d_qkv, d_pre = recur_backward(pre, qkv, d_mixed.astype(half), scores, states, span, dk, dv)
    d_rank = dot(d_pre.astype(half), decay_weight.astype(half), NT).astype(half)
    d_normed = (
        dot(d_qkv, qkv_full, NT) + dot(d_outgate, outgate_full, NT) + dot(d_rank, rank_full, NT)
    )
    grad_gain_attn = jnp.sum(d_normed * unit, axis=0)
    d_normed = d_normed.astype(half)
    grad_qkv = dot(normed, d_qkv, TN).astype(half)
    grad_rank = dot(normed, d_rank, TN)
    grad_decay = jnp.transpose(
        dot(rank_rows.astype(half), d_pre.astype(half), TN).reshape(rank, size, bits), (1, 0, 2)
    ).reshape(size, decay_cols, width)

    def spread(values):
        blocks = values.reshape(size, -1, 1)
        return jnp.pad(blocks, ((0, 0), (0, width - blocks.shape[1]), (0, 0)))

    grad_small = jnp.concatenate(
        [
            grad_rank.reshape(size, width, rank),
            grad_gain_attn.reshape(size, width, 1),
            grad_gain_ffn.reshape(size, width, 1),
            spread(grad_head),
            spread(jnp.sum(d_pre, axis=0)),
            jnp.transpose(grad_decay, (0, 2, 1)),
        ],
        axis=2,
    )
    grad_small = jnp.pad(grad_small, ((0, 0), (0, 0), (0, 128 - grad_small.shape[2])))
    grad_small = grad_small.reshape(size * width, 128).astype(half)

    (out_own, outgate_own, qkv_own, small_own), (d_normed,) = deliver(
        3, (grad_out, grad_outgate, grad_qkv, grad_small), (d_normed,)
    )
    d_back, _ = rms_back(unit, scale, gain_attn, d_normed.astype(f32))
    grad_tokens = (d_middle + d_back).astype(half)
    heads_own = small_own.astype(half)
    heads_own = heads_own.astype(f32) + lax.ppermute(heads_own, "tensor", CORE).astype(f32)
    heads_own = heads_own.astype(half)
    heads_own = heads_own.astype(f32) + lax.ppermute(heads_own, "tensor", ACROSS).astype(f32)
    return (
        output,
        grad_tokens,
        heads_own[:, rank],
        qkv_own[:, :dk] * 0.0625,
        qkv_own[:, dk : 2 * dk],
        qkv_own[:, 2 * dk : 2 * dk + dv],
        outgate_own,
        heads_own[:, :rank],
        small_own[:, rank + 4 : rank + 4 + decay_cols].T.reshape(decay_proj.shape),
        small_own[:bits, rank + 3].reshape(decay_bias.shape),
        heads_own[:gains, rank + 2],
        out_own.T,
        heads_own[:, rank + 1] * 0.25,
        gate_own,
        up_own,
        down_own.T,
    )


def solution(mesh):
    size = mesh.shape["dp"]

    def run(*args):
        return local(*args, size=size)

    weight = P("dp", "tensor")
    cross = P("tensor", "dp")
    return jax.shard_map(
        run,
        mesh=mesh,
        in_specs=(
            P("dp", None), P("dp"), P("dp"), weight, weight, weight, weight, P("dp", None),
            P(None, "tensor", "dp"), cross, P("dp"), cross, P("dp"), weight, weight, cross,
            P("dp", None),
        ),
        out_specs=(
            P("dp", None), P("dp", None), P("dp"), weight, weight, weight, weight, P("dp", None),
            P(None, "tensor", "dp"), cross, P("dp"), cross, P("dp"), weight, weight, cross,
        ),
        check_vma=False,
    )
```

time: 2510 us -> 873 us (0.35)
  waiting for transfers between devices: 1320 us -> 2.4 us
  Pallas kernels: 0 us -> 608 us
  matrix products: 647 us -> 166 us
  blocking collectives: 158 us -> 0 us
  other arithmetic: 210 us -> 58 us
  local copies, waits for them, and re-layouts: 139 us -> 25.6 us
    reduce_scatter x9 -> x0, waiting for transfers between devices: 680 us -> none  [the longest x1 112 us: local(): lax.psum_scatter(grad_down.astype(jnp.bfloat16), 'dp', scatter_dimension=...]
    pallas_call x0 -> x6, Pallas kernels: none -> 608 us  [the longest x4 586 us: exchange(): pl.pallas_call(kernel, in_specs=[near_spec] * gathers + [whole] * (scatte...]
    dot_general x222 -> x24, matrix products: 647 us -> 166 us  [the longest x23 164 us: dot(): lax.dot_general(left, right, (dims, ((), ())), preferred_element_type=f32)]
    psum x3 -> x0, waiting for transfers between devices: 362 us -> none  [the longest x1 153 us: local(): lax.psum(project(hidden_half, down_full).astype(jnp.bfloat16), 'tensor')]
    all_gather x8 -> x0, waiting for transfers between devices: 249 us -> none  [the longest x1 82.9 us: local(): lax.all_gather(gate_proj.astype(half), 'dp', axis=0, tiled=True)]
    all_gather x4 -> x0, blocking collectives: 102 us -> none  [the longest x1 30.9 us: local(): lax.all_gather(decay_proj.astype(half), 'dp', axis=2, tiled=True)]
    squeeze x64 -> x0, local copies, waits for them, and re-layouts: 57.2 us -> none  [recurrence(): lax.scan(jax.checkpoint(group_step), start, (split(query_matrix), split(k...]
    mul x48 -> x1, other arithmetic: 54.6 us -> 0.81 us  [local(): heads_own[:, rank + 1] * 0.25]
  transfers between devices with their start and end apart: 22 -> 2, of which waited for: 17 -> 1; matrix products, arithmetic and copies ran while one was open for 18% -> 2% of each run, Pallas kernels for 0% -> 0%
where the time goes in v1:
time: 873 us; the launch traced here: 864 us
  Pallas kernels  608 us (70%)
  matrix products  166 us (19%)
  other arithmetic  58 us (7%)
  local copies, waits for them, and re-layouts  25.6 us (3%)
    pallas_call x4, Pallas kernels, exchange(): pl.pallas_call(kernel, in_specs=[near_spec] * gathers + [whole] * (scatte...  586 us
    dot_general x23, matrix products, dot(): lax.dot_general(left, right, (dims, ((), ())), preferred_element_type=f32)  164 us
  transfers between devices with their start and end apart: 2, of which 1 were waited for; matrix products, arithmetic and copies ran while one was open for 2% of the time, Pallas kernels for 0%

profile of v1, /device:TPU:0, one launch (start us, length us, event | category | flops | bytes accessed | tf_op | source)
XLA Modules:
  0.0 863.7 jit_solution(6655295318558201603)
XLA Ops:
  13.4 93.4 %exchange_0.1 = (bf16[2048,1024]{1,0:T(8,128)(2,1)}, bf16[2048,128]{1,0:T(8,128)(2,1)}, bf16[2048,512]{1,0:T(8,128)(2,1)}, bf16[2048,512]{1,0:T(8,128)(2,1)}) custom-call(bf16[256,1024]{1,0:T(8,128)(2,1)} %pad_maximum_fusion.refs_0_, bf16[256,128]{1,0:T(8,128)(2,1)} %pad.32.refs_1_, bf16[256,512]{1,0:T(8,128)(2,1)} %convert_element_type.192.refs_2_, ...), custom_call_target="tpu_custom_call" | custom-call | tf_op jit(solution)/shard_map/exchange_0/pallas_call | solution.py:708
  133.8 9.7 %recur_forward.1 = (bf16[1024,512]{1,0:T(8,128)(2,1)}, bf16[1024,128]{1,0:T(8,128)(2,1)}, bf16[8,256,512]{2,1,0:T(8,128)(2,1)}) custom-call(f32[1024,256]{1,0:T(8,128)} %convolution_add_fusion.pre_ref, bf16[1024,1024]{1,0:T(8,128)(2,1)} %convolution_convert_fusion.9.q_ref.k_ref.v_ref, bf16[1024,1024]{1,0:T(8,128)(2,1)} %convolution_convert_fusion.9.q_ref.k_ref.v_ref, ...), custom_call_target="tpu_custom_call" | custom-call | flops 6000000000 | bytes 8388608 | tf_op jit(solution)/shard_map/recur_forward/pallas_call | solution.py:176
  145.1 6.7 convolution_convert_fusion.4.refs_3_
  151.8 170.2 %exchange_1.1 = (bf16[2048,1408]{1,0:T(8,128)(2,1)}, bf16[2048,1408]{1,0:T(8,128)(2,1)}, bf16[2048,1408]{1,0:T(8,128)(2,1)}, bf16[1024,2048]{1,0:T(8,128)(2,1)}) custom-call(bf16[256,1408]{1,0:T(8,128)(2,1)} %convert_element_type.188.refs_0_, bf16[256,1408]{1,0:T(8,128)(2,1)} %convert_element_type.189.refs_1_, bf16[256,1408]{1,0:T(8,128)(2,1)} %bitcast.68, ...), custom_call_target="tpu_custom_call" | custom-call | tf_op jit(solution)/shard_map/exchange_1/pallas_call | solution.py:708
  330.6 8.5 fusion.106
  339.1 8.9 %fusion.105 = f32[1024,1408]{1,0:T(8,128)} fusion(bf16[1024,2048]{1,0:T(8,128)(2,1)S(1)} %multiply_convert_fusion.1, bf16[2048,1408]{1,0:T(8,128)(2,1)S(1)} %bitcast.88), kind=kOutput, calls=%fused_computation.220 | convolution fusion | flops 5905580032 | bytes 15728640 | tf_op jit(solution)/shard_map/dot_general | solution.py:41
  348.0 14.9 %multiply_convert_fusion.2 = (bf16[1024,1408]{1,0:T(8,128)(2,1)}, bf16[1024,1408]{1,0:T(8,128)(2,1)S(1)}, bf16[1024,1408]{1,0:T(8,128)(2,1)}) fusion(f32[1024,1408]{1,0:T(8,128)} %fusion.105, f32[1024,1408]{1,0:T(8,128)} %fusion.106, bf16[2048,1408]{1,0:T(8,128)(2,1)} %get-tuple-element.47, bf16[1024,2048]{1,0:T(8,128)(2,1)S(1)} %copy-done.16, ...), kind=kOutput, calls=%fused_computation.39 | convolution fusion | flops 5934940160 | bytes 30150656 | tf_op jit(solution)/shard_map/dot_general | solution.py:41
  362.9 10.7 %fusion.107 = f32[1024,2048]{1,0:T(8,128)} fusion(bf16[1024,1408]{1,0:T(8,128)(2,1)S(1)} %get-tuple-element.119, bf16[2048,1408]{1,0:T(8,128)(2,1)} %get-tuple-element.45), kind=kOutput, calls=%fused_computation.222 | convolution fusion | flops 5905580032 | bytes 17039360 | tf_op jit(solution)/shard_map/dot_general | solution.py:41
  373.6 8.6 convolution_convert_fusion.1.refs_1_
  382.2 11.0 %convolution_convert_fusion.3.refs_4_ = bf16[1024,2048]{1,0:T(8,128)(2,1)} fusion(bf16[1024,1408]{1,0:T(8,128)(2,1)S(1)} %copy-done.39, bf16[2048,1408]{1,0:T(8,128)(2,1)} %get-tuple-element.47), kind=kOutput, calls=%fused_computation.43 | convolution fusion | flops 5907677184 | bytes 12845056 | tf_op jit(solution)/shard_map/dot_general | solution.py:41
  393.2 9.0 %convolution_convert_fusion.2.refs_0_ = bf16[2048,1408]{1,0:T(8,128)(2,1)} fusion(bf16[1024,1408]{1,0:T(8,128)(2,1)S(1)} %copy-done.39, bf16[1024,2048]{1,0:T(8,128)(2,1)S(1)} %copy-done.16, f32[1024]{0:T(1024)S(1)} %fusion.89), kind=kOutput, calls=%fused_computation.34 | convolution fusion | flops 5914755072 | bytes 12849152 | tf_op jit(solution)/shard_map/dot_general | solution.py:41
  402.2 8.7 %convolution_convert_fusion.refs_2_ = bf16[2048,1408]{1,0:T(8,128)(2,1)} fusion(bf16[1024,2048]{1,0:T(8,128)(2,1)S(1)} %multiply_convert_fusion.1, bf16[1024,1408]{1,0:T(8,128)(2,1)S(1)} %copy-done.40), kind=kOutput, calls=%fused_computation.32 | convolution fusion | flops 5908463616 | bytes 12845056 | tf_op jit(solution)/shard_map/dot_general | solution.py:41
  410.9 10.4 %add_convert_fusion.refs_3_ = bf16[1024,2048]{1,0:T(8,128)(2,1)} fusion(f32[1024,2048]{1,0:T(8,128)} %fusion.107, bf16[1024,1408]{1,0:T(8,128)(2,1)S(1)} %copy-done.40, bf16[2048,1408]{1,0:T(8,128)(2,1)S(1)} %bitcast.86), kind=kOutput, calls=%fused_computation.27 | convolution fusion | flops 5909774336 | bytes 21233664 | tf_op jit(solution)/shard_map/dot_general | solution.py:41
  421.3 205.7 %exchange_2.1 = (f32[256,1408]{1,0:T(8,128)}, f32[256,1408]{1,0:T(8,128)}, f32[256,1408]{1,0:T(8,128)}, bf16[1024,2048]{1,0:T(8,128)(2,1)}, bf16[1024,2048]{1,0:T(8,128)(2,1)}) custom-call(bf16[2048,1408]{1,0:T(8,128)(2,1)} %convolution_convert_fusion.2.refs_0_, bf16[2048,1408]{1,0:T(8,128)(2,1)} %convolution_convert_fusion.1.refs_1_, ...), custom_call_target="tpu_custom_call" | custom-call | tf_op jit(solution)/shard_map/exchange_2/pallas_call | solution.py:708
  627.1 7.8 fusion.9
  635.4 8.2 fusion.8
  643.6 7.5 fusion.29
  660.1 6.4 fusion.94
  668.3 12.8 %recur_backward.1 = (bf16[1024,1024]{1,0:T(8,128)(2,1)}, f32[1024,256]{1,0:T(8,128)}) custom-call(f32[1024,256]{1,0:T(8,128)} %convolution_add_fusion.pre_ref, bf16[1024,1024]{1,0:T(8,128)(2,1)} %convolution_convert_fusion.9.q_ref.k_ref.v_ref, bf16[1024,1024]{1,0:T(8,128)(2,1)} %convolution_convert_fusion.9.q_ref.k_ref.v_ref, ...), custom_call_target="tpu_custom_call" | custom-call | flops 8000000000 | bytes 10485760 | tf_op jit(solution)/shard_map/recur_backward/pallas_call | solution.py:205
  681.2 10.7 %fusion.108 = f32[1024,2048]{1,0:T(8,128)} fusion(bf16[1024,1024]{1,0:T(8,128)(2,1)} %get-tuple-element.52, bf16[2048,1024]{1,0:T(8,128)(2,1)} %get-tuple-element.40), kind=kOutput, calls=%fused_computation.223 | convolution fusion | flops 4294967296 | bytes 14680064 | tf_op jit(solution)/shard_map/dot_general | solution.py:41
  691.9 6.7 convolution_convert_fusion.5.refs_2_
  703.6 8.6 fusion.103
  713.5 116.4 %exchange_3.1 = (f32[256,512]{1,0:T(8,128)}, f32[256,512]{1,0:T(8,128)}, f32[256,1024]{1,0:T(8,128)}, f32[256,128]{1,0:T(8,128)}, bf16[1024,2048]{1,0:T(8,128)(2,1)}) custom-call(bf16[2048,512]{1,0:T(8,128)(2,1)} %convolution_convert_fusion.7.refs_0_, bf16[2048,512]{1,0:T(8,128)(2,1)} %convolution_convert_fusion.6.refs_1_, ...), custom_call_target="tpu_custom_call" | custom-call | tf_op jit(solution)/shard_map/exchange_3/pallas_call | solution.py:708
  837.5 6.2 fusion.16
  (215 shorter events, 93.7 us)
Async XLA Ops:
  109.8 16.2 %copy-start.30 = (f32[2048]{0:T(1024)}, f32[2048]{0:T(1024)S(1)}, u32[]{:S(2)}) copy-start(f32[2048]{0:T(1024)S(1)} %get-tuple-element.115) | copy-start | bytes 24580
  112.4 13.6 %copy-start.32 = (f32[1024]{0:T(1024)}, f32[1024]{0:T(1024)S(1)}, u32[]{:S(2)}) copy-start(f32[1024]{0:T(1024)S(1)} %add_rsqrt_fusion.1) | copy-start | bytes 12292
  121.8 10.4 %copy-start.28 = (f32[1024,16]{0,1:T(8,128)}, f32[1024,16]{0,1:T(8,128)S(1)}, u32[]{:S(2)}) copy-start(f32[1024,16]{0,1:T(8,128)S(1)} %fusion.47) | copy-start | bytes 196612
  126.0 19.1 %copy-start.24 = (bf16[1024,512]{1,0:T(8,128)(2,1)}, bf16[1024,512]{1,0:T(8,128)(2,1)S(1)}, u32[]{:S(2)}) copy-start(bf16[1024,512]{1,0:T(8,128)(2,1)S(1)} %convolution_convert_fusion.10) | copy-start | bytes 3145732
  322.0 8.6 slice-start
  327.9 11.2 %slice-start.2 = ((s8[5767168]{0:T(1024)(128)(4,1)}), s8[4194304]{0:T(1024)(128)(4,1)S(1)}, s32[]{:S(2)}) async-start(s8[5767168]{0:T(1024)(128)(4,1)} %bitcast.87), calls=%async_computation.2 | async-start | bytes 8388608
  330.6 8.5 slice-start.3
  339.1 8.9 %copy-start.16 = (bf16[1024,2048]{1,0:T(8,128)(2,1)S(1)}, bf16[1024,2048]{1,0:T(8,128)(2,1)}, u32[]{:S(2)}) copy-start(bf16[1024,2048]{1,0:T(8,128)(2,1)} %param.33) | copy-start | bytes 12582916
  373.6 8.6 copy-start.39
  393.2 9.0 %copy-start.40 = (bf16[1024,1408]{1,0:T(8,128)(2,1)S(1)}, bf16[1024,1408]{1,0:T(8,128)(2,1)}, u32[]{:S(2)}) copy-start(bf16[1024,1408]{1,0:T(8,128)(2,1)} %get-tuple-element.118) | copy-start | bytes 8650756
  627.1 7.8 copy-start.3
  627.1 7.8 copy-start.8
  627.1 8.3 copy-start.11
  635.4 8.2 copy-start.15
  643.6 7.5 copy-start.9
  643.6 7.5 copy-start.25
  681.2 10.7 %copy-start.4 = (bf16[1024,2048]{1,0:T(8,128)(2,1)S(1)}, bf16[1024,2048]{1,0:T(8,128)(2,1)}, u32[]{:S(2)}) copy-start(bf16[1024,2048]{1,0:T(8,128)(2,1)} %param.17) | copy-start | bytes 12582916
  681.2 10.7 %copy-start.38 = (bf16[1024,1024]{1,0:T(8,128)(2,1)S(1)}, bf16[1024,1024]{1,0:T(8,128)(2,1)}, u32[]{:S(2)}) copy-start(bf16[1024,1024]{1,0:T(8,128)(2,1)} %get-tuple-element.52) | copy-start | bytes 6291460
  691.9 7.3 copy-start.12
  831.5 21.3 %collective-permute-start = (bf16[256,128]{1,0:T(8,128)(2,1)}, bf16[256,128]{1,0:T(8,128)(2,1)}, u32[]{:S(2)}, u32[]{:S(2)}) collective-permute-start(bf16[256,128]{1,0:T(8,128)(2,1)} %convert_element_type.235), channel_id=1, source_target_pairs={{0,1},{1,0},{2,3},{3,2},{4,5},{5,4},{6,7},{7,6},{8,9},{9,8},{10,11... | collective-permute-start | bytes 196616 | tf_op jit(solution)/shard_map/ppermute | solution.py:961
  843.7 16.8 %copy-start.27 = (f32[256,512]{1,0:T(8,128)S(1)}, f32[256,512]{1,0:T(8,128)}, u32[]{:S(2)}) copy-start(f32[256,512]{1,0:T(8,128)} %get-tuple-element.164) | copy-start | bytes 1572868
  843.7 17.6 %copy-start.22 = (f32[256,1408]{1,0:T(8,128)S(1)}, f32[256,1408]{1,0:T(8,128)}, u32[]{:S(2)}) copy-start(f32[256,1408]{1,0:T(8,128)} %get-tuple-element.171) | copy-start | bytes 4325380
  846.1 16.3 %copy-start.21 = (f32[256,1408]{1,0:T(8,128)S(1)}, f32[256,1408]{1,0:T(8,128)}, u32[]{:S(2)}) copy-start(f32[256,1408]{1,0:T(8,128)} %get-tuple-element.172) | copy-start | bytes 4325380
  853.7 4.6 collective-permute-start.1
  (23 other events, 118.7 us)

commit v2 on v1

--- a/solution.py
+++ b/solution.py
@@ -98,26 +98,12 @@
     state[...] = whole * state_now + dot(k_out, v, TN)
 
 
-def backward_body(
-    pre_ref, q_ref, k_ref, v_ref, d_ref, score_ref, state_ref, span_ref,
-    dqkv_ref, dpre_ref, carry,
-):
-    @pl.when(pl.program_id(0) == 0)
-    def _():
-        carry[...] = jnp.zeros_like(carry)
-
+def backward_math(pre, q, k, v, d_mixed, scores, state_half, span_ref, carry):
     levels = level_count()
-    pre = pre_ref[...]
     decay = log_decay(pre)
     sums = dot(span_ref[...], split_two(decay), NN)
-    q = q_ref[...]
-    k = k_ref[...]
-    v = v_ref[...]
-    d_mixed = d_ref[...]
     q32 = q.astype(f32)
     k32 = k.astype(f32)
-    scores = score_ref[...]
-    state_half = state_ref[0]
     carry_now = carry[...]
     carry_half = carry_now.astype(half)
     rows, cols, _ = level_parts(0)
@@ -152,18 +138,28 @@
     pieces.append((k_out * back_k).astype(half))
     dq = dq + head_grow * back_q
     dk = dk + tail_grow * back_k
-    wide = q.shape[1]
-    dqkv_ref[:, :wide] = dq.astype(half)
-    dqkv_ref[:, wide : 2 * wide] = dk.astype(half)
-    dqkv_ref[:, 2 * wide :] = (
-        dot(scores, d_mixed, TN) + dot(k_out_half, carry_half, NN)
-    ).astype(half)
+    dv = dot(scores, d_mixed, TN) + dot(k_out_half, carry_half, NN)
+    d_qkv = jnp.concatenate([dq.astype(half), dk.astype(half), dv.astype(half)], axis=1)
     whole = jnp.exp(jnp.transpose(head_sum[CHUNK - 8 :, :]))[:, 7:8]
     end_col = whole * jnp.sum(state_half.astype(f32) * carry_now, axis=1, keepdims=True)
     end_row = jnp.transpose(jnp.broadcast_to(end_col, (end_col.shape[0], 128)))[0:1, :]
     d_decay = dot(span_ref[:, :CHUNK], jnp.concatenate(pieces, axis=0), TN) + end_row
-    dpre_ref[...] = d_decay * (jax.nn.sigmoid(-pre) * (1.0 / 16.0))
     carry[...] = whole * carry_now + dot(q_in.astype(half), d_mixed, TN)
+    return d_qkv, d_decay * (jax.nn.sigmoid(-pre) * (1.0 / 16.0))
+
+
+def backward_body(
+    pre_ref, q_ref, k_ref, v_ref, d_ref, score_ref, state_ref, span_ref,
+    dqkv_ref, dpre_ref, carry,
+):
+    @pl.when(pl.program_id(0) == 0)
+    def _():
+        carry[...] = jnp.zeros_like(carry)
+
+    dqkv_ref[...], dpre_ref[...] = backward_math(
+        pre_ref[...], q_ref[...], k_ref[...], v_ref[...], d_ref[...], score_ref[...],
+        state_ref[0], span_ref, carry,
+    )
 
 
 def recur_forward(pre, qkv, span, dk, dv):
@@ -627,11 +623,15 @@
             links.copy(index, self.first.at[j], dst, links.partner()).start()
             self.store(j).start()
 
-    def finish(self):
+    def landed(self):
         links = self.links
         for j in range(PIECES):
             links.arrived(self.base + 2 * PIECES + j, self.at(self.out, 1 - links.core, j))
             self.store(j).wait()
+
+    def finish(self):
+        links = self.links
+        for j in range(PIECES):
             for stage in range(3):
                 links.sent(self.base + stage * PIECES + j, self.mine.at[j])
 
@@ -700,6 +700,8 @@
             item.close(False)
         for item in gather:
             item.rest_step(3)
+        for item in total:
+            item.landed()
         for item in gather + scatter + total:
             item.finish()
 
@@ -721,6 +723,209 @@
         name=f"exchange_{number}",
     )(*shards, *totals, *parts)
     return outs[:gathers], outs[gathers : gathers + scatters], outs[gathers + scatters :]
+
+
+class Stream:
+    def __init__(self, sems, base, arrays, buffers, index):
+        self.sems, self.base, self.arrays, self.buffers, self.index = (
+            sems, base, arrays, buffers, index,
+        )
+
+    def copies(self, i, inward):
+        slot = i % 2
+        for n, (array, buffer) in enumerate(zip(self.arrays, self.buffers)):
+            rows = buffer.shape[1]
+            first = pl.multiple_of(self.index(i) * rows, rows)
+            far, near = array.at[pl.ds(first, rows), :], buffer.at[slot]
+            sem = self.sems.at[self.base + 2 * n + slot]
+            src, dst = (far, near) if inward else (near, far)
+            yield pltpu.make_async_copy(src, dst, sem)
+
+    def start(self, i, inward):
+        for copy in self.copies(i, inward):
+            copy.start()
+
+    def wait(self, i, inward):
+        for copy in self.copies(i, inward):
+            copy.wait()
+
+
+def row_sum(values):
+    return jnp.sum(values, axis=0, keepdims=True)
+
+
+def attention_back(tile, weights, gains, sums, carry):
+    (cot, middle, d_out, tokens, qkv, mixed, outgate, pre, scores, state) = tile
+    (w_out, w_qkv, w_gate, w_small, w_decay, span) = weights
+    gain_ffn, gain_head = gains
+    sum_ffn, sum_head, sum_bias, sum_attn = sums
+    unit, scale = rms_parts(middle[...].astype(f32))
+    cot = cot[...].astype(f32)
+    sum_ffn[...] += row_sum(cot * unit)
+    weighted = cot * gain_ffn[...]
+    inner = jnp.mean(weighted * unit, axis=-1, keepdims=True)
+    d_attn = (d_out[...].astype(f32) + scale * (weighted - unit * inner)).astype(half)
+    d_gated = dot(d_attn, w_out[...], NN)
+    rows = mixed[...].astype(f32)
+    gate = outgate[...].astype(f32)
+    head_scale = lax.rsqrt(jnp.mean(rows * rows, axis=-1, keepdims=True) + head_eps)
+    head_unit = rows * head_scale
+    sig = jax.nn.sigmoid(gate)
+    d_outgate = (
+        d_gated * head_unit * gain_head[...] * sig * (1.0 + gate * (1.0 - sig))
+    ).astype(half)
+    d_normed_head = d_gated * gate * sig
+    sum_head[...] += row_sum(d_normed_head * head_unit)
+    weighted = d_normed_head * gain_head[...]
+    inner = jnp.mean(weighted * head_unit, axis=-1, keepdims=True)
+    d_mixed = (head_scale * (weighted - head_unit * inner)).astype(half)
+    dk = w_decay.shape[1]
+    d_qkv, d_pre = backward_math(
+        pre[...], qkv[:, :dk], qkv[:, dk : 2 * dk], qkv[:, 2 * dk :], d_mixed,
+        scores[...], state[...], span, carry,
+    )
+    sum_bias[...] += row_sum(d_pre)
+    d_pre = d_pre.astype(half)
+    d_rank = dot(d_pre, w_decay[...], NT).astype(half)
+    d_normed = (
+        dot(d_qkv, w_qkv[...], NT) + dot(d_outgate, w_gate[...], NT) + dot(d_rank, w_small[...], NT)
+    )
+    unit, _ = rms_parts(tokens[...].astype(f32))
+    sum_attn[...] += row_sum(d_normed * unit)
+    return d_attn, d_outgate, d_qkv, d_pre, d_rank, d_normed.astype(half)
+
+
+def backward_exchange(number, totals, part, rows_in, weights, gains):
+    scatters = len(totals)
+    length, width = part.shape
+    count = length // CHUNK
+    dk = weights[4].shape[1]
+    dv = weights[0].shape[1]
+    outs_wide = (width, dv, 2 * dk + dv, dk, 128, width)
+    in_shapes = [(CHUNK, width)] + [(a.shape[0] // count, a.shape[1]) for a in rows_in]
+    in_types = [half] + [a.dtype for a in rows_in]
+    streams = len(in_shapes)
+    sum_wide = (width, dv, dk, width)
+    scratch = []
+    for total in totals:
+        scratch += Scatter.scratch(total.shape[0] // (2 * LINE), total.shape[1])
+    scratch += Total.scratch(length, width)
+    scratch += [pltpu.VMEM((2,) + s, t) for s, t in zip(in_shapes, in_types)]
+    scratch += [pltpu.VMEM((2, CHUNK, w), half) for w in outs_wide]
+    scratch += [pltpu.VMEM(w.shape, half) for w in weights]
+    scratch += [pltpu.VMEM((dk, dv), f32)]
+    remote = Scatter.SEMS * scatters + Total.SEMS
+    near = 12 * scatters + 2 * PIECES
+    extra = 2 * streams + 2 * len(outs_wide) + len(weights)
+    scratch += [
+        pltpu.SemaphoreType.DMA((remote,)),
+        pltpu.SemaphoreType.DMA((remote,)),
+        pltpu.SemaphoreType.DMA((near,)),
+        pltpu.SemaphoreType.DMA((extra,)),
+    ]
+
+    def kernel(*refs):
+        refs = list(refs)
+
+        def pop(count):
+            taken, refs[:count] = refs[:count], []
+            return taken
+
+        total_refs, (part_ref,), row_refs = pop(scatters), pop(1), pop(streams - 1)
+        weight_refs, gain_refs = pop(len(weights)), pop(2)
+        own_refs, (sum_ref,), out_refs, gain_sums = pop(scatters), pop(1), pop(6), pop(4)
+        buffers = [pop(6) for _ in range(scatters)]
+        sum_buffers = pop(3)
+        in_buffers, out_buffers, near_weights = pop(streams), pop(6), pop(len(weights))
+        (carry,) = pop(1)
+        sems = refs.pop()
+        links = Links(*refs)
+        scatter = [Scatter(links, *a) for a in zip(total_refs, own_refs, buffers)]
+        total = Total(links, part_ref, sum_ref, sum_buffers)
+        inputs = Stream(sems, 0, [sum_ref] + row_refs, in_buffers, lambda i: count - 1 - i)
+        outputs = Stream(sems, 2 * streams, out_refs, out_buffers, lambda i: count - 1 - i)
+        loads = [
+            pltpu.make_async_copy(far, close, sems.at[2 * streams + 12 + n])
+            for n, (far, close) in enumerate(zip(weight_refs, near_weights))
+        ]
+        links.greet()
+        for item in scatter:
+            item.start()
+        total.start()
+        for load in loads:
+            load.start()
+        total.middle()
+        for k in range(LINE - 1):
+            for item in scatter:
+                item.step(k, True)
+        for item in scatter:
+            item.close(True)
+        for k in range(2):
+            for item in scatter:
+                item.step(k, False)
+        total.spread()
+        total.landed()
+        for load in loads:
+            load.wait()
+        for ref in (*gain_sums, carry):
+            ref[...] = jnp.zeros_like(ref)
+        inputs.start(0, True)
+
+        def body(i, state):
+            @pl.when(i + 1 < count)
+            def _():
+                inputs.start(i + 1, True)
+
+            inputs.wait(i, True)
+            slot = i % 2
+            results = attention_back(
+                [b.at[slot] for b in in_buffers], near_weights, gain_refs, gain_sums, carry
+            )
+
+            @pl.when(i >= 2)
+            def _():
+                outputs.wait(i - 2, False)
+
+            for buffer, value in zip(out_buffers, results):
+                buffer[slot] = value
+            outputs.start(i, False)
+
+            @pl.when(i == 2)
+            def _():
+                for item in scatter:
+                    item.step(2, False)
+
+            @pl.when(i == 5)
+            def _():
+                for item in scatter:
+                    item.close(False)
+
+            return state
+
+        lax.fori_loop(0, count, body, 0)
+        outputs.wait(count - 2, False)
+        outputs.wait(count - 1, False)
+        for item in scatter:
+            item.finish()
+        total.finish()
+
+    whole = pl.BlockSpec(memory_space=pl.ANY)
+    near_spec = pl.BlockSpec(memory_space=pltpu.VMEM)
+    outs = pl.pallas_call(
+        kernel,
+        in_specs=[whole] * (scatters + 1 + len(rows_in) + len(weights)) + [near_spec] * 2,
+        out_specs=[near_spec] * scatters + [whole] * 7 + [near_spec] * 4,
+        out_shape=[jax.ShapeDtypeStruct((t.shape[0] // (2 * LINE), t.shape[1]), f32) for t in totals]
+        + [jax.ShapeDtypeStruct(part.shape, half)]
+        + [jax.ShapeDtypeStruct((length, w), half) for w in outs_wide]
+        + [jax.ShapeDtypeStruct((1, w), f32) for w in sum_wide],
+        scratch_shapes=scratch,
+        compiler_params=pltpu.CompilerParams(
+            collective_id=number, has_side_effects=True, vmem_limit_bytes=62 * 2**20
+        ),
+        name=f"backward_exchange_{number}",
+    )(*totals, part, *rows_in, *weights, *gains)
+    return outs[:scatters], outs[scatters + 1 : scatters + 7], outs[scatters + 7 :]
 
 
 class Ring:
@@ -910,28 +1115,45 @@
     grad_gate = dot(normed_ffn, d_gate, TN).astype(half)
     grad_up = dot(normed_ffn, d_up, TN).astype(half)
     ffn = dot(hidden, down_full, NT).astype(half)
-    (down_own, gate_own, up_own), (d_normed_ffn, ffn) = deliver(
-        2, (grad_down, grad_gate, grad_up), (d_normed_ffn, ffn)
-    )
-    output = (mask * (middle + ffn.astype(f32))).astype(half)
-    d_back, grad_gain_ffn = rms_back(unit_ffn, scale_ffn, gain_ffn, d_normed_ffn.astype(f32))
-    d_middle = d_out + d_back
-    d_attn = d_middle.astype(half)
+    if fast:
+        w_decay = jnp.pad(decay_weight, ((0, 128 - rank), (0, 0))).astype(half)
+        (down_own, gate_own), outs, sums = backward_exchange(
+            2,
+            (grad_down, grad_gate),
+            d_normed_ffn,
+            (
+                middle.astype(half), d_out_half, tokens, qkv, mixed, outgate, pre, scores,
+                states.reshape(-1, dv),
+            ),
+            (out_full, qkv_full, outgate_full, small_full, w_decay, span),
+            (gain_ffn[None, :], gain_head[None, :]),
+        )
+        d_attn, d_outgate, d_qkv, d_pre_half, d_rank, d_normed = outs
+        grad_gain_ffn, grad_head, grad_bias, grad_gain_attn = sums
+        d_middle = d_attn.astype(f32)
+        d_rank = d_rank[:, :rank]
+    else:
+        d_normed_ffn = tensor_sum(d_normed_ffn)
+        d_back, grad_gain_ffn = rms_back(unit_ffn, scale_ffn, gain_ffn, d_normed_ffn.astype(f32))
+        d_middle = d_out + d_back
+        d_attn = d_middle.astype(half)
+        d_mixed, d_outgate, grad_head = pull_gated(dot(d_attn, out_full, NN))
+        d_outgate = d_outgate.astype(half)
+        d_qkv, d_pre = recur_backward(pre, qkv, d_mixed.astype(half), scores, states, span, dk, dv)
+        d_rank = dot(d_pre.astype(half), decay_weight.astype(half), NT).astype(half)
+        d_normed = (
+            dot(d_qkv, qkv_full, NT) + dot(d_outgate, outgate_full, NT) + dot(d_rank, rank_full, NT)
+        )
+        grad_gain_attn = jnp.sum(d_normed * unit, axis=0)
+        d_normed = d_normed.astype(half)
+        d_pre_half = d_pre.astype(half)
+        grad_bias = jnp.sum(d_pre, axis=0)
     grad_out = dot(d_attn, gated, TN).astype(half)
-    d_mixed, d_outgate, grad_head = pull_gated(dot(d_attn, out_full, NN))
-    d_outgate = d_outgate.astype(half)
     grad_outgate = dot(normed, d_outgate, TN).astype(half)
-    d_qkv, d_pre = recur_backward(pre, qkv, d_mixed.astype(half), scores, states, span, dk, dv)
-    d_rank = dot(d_pre.astype(half), decay_weight.astype(half), NT).astype(half)
-    d_normed = (
-        dot(d_qkv, qkv_full, NT) + dot(d_outgate, outgate_full, NT) + dot(d_rank, rank_full, NT)
-    )
-    grad_gain_attn = jnp.sum(d_normed * unit, axis=0)
-    d_normed = d_normed.astype(half)
     grad_qkv = dot(normed, d_qkv, TN).astype(half)
     grad_rank = dot(normed, d_rank, TN)
     grad_decay = jnp.transpose(
-        dot(rank_rows.astype(half), d_pre.astype(half), TN).reshape(rank, size, bits), (1, 0, 2)
+        dot(rank_rows.astype(half), d_pre_half, TN).reshape(rank, size, bits), (1, 0, 2)
     ).reshape(size, decay_cols, width)
 
     def spread(values):
@@ -944,7 +1166,7 @@
             grad_gain_attn.reshape(size, width, 1),
             grad_gain_ffn.reshape(size, width, 1),
             spread(grad_head),
-            spread(jnp.sum(d_pre, axis=0)),
+            spread(grad_bias),
             jnp.transpose(grad_decay, (0, 2, 1)),
         ],
         axis=2,
@@ -952,9 +1174,19 @@
     grad_small = jnp.pad(grad_small, ((0, 0), (0, 0), (0, 128 - grad_small.shape[2])))
     grad_small = grad_small.reshape(size * width, 128).astype(half)
 
-    (out_own, outgate_own, qkv_own, small_own), (d_normed,) = deliver(
-        3, (grad_out, grad_outgate, grad_qkv, grad_small), (d_normed,)
-    )
+    if fast:
+        waiting = (grad_up, grad_out, grad_outgate, grad_qkv, grad_small)
+        (up_own, out_own, outgate_own, qkv_own, small_own), (d_normed, ffn) = deliver(
+            3, waiting, (d_normed, ffn)
+        )
+    else:
+        waiting = (
+            grad_down, grad_gate, grad_up, grad_out, grad_outgate, grad_qkv, grad_small,
+        )
+        (down_own, gate_own, up_own, out_own, outgate_own, qkv_own, small_own), (
+            d_normed, ffn,
+        ) = deliver(3, waiting, (d_normed, ffn))
+    output = (mask * (middle + ffn.astype(f32))).astype(half)
     d_back, _ = rms_back(unit, scale, gain_attn, d_normed.astype(f32))
     grad_tokens = (d_middle + d_back).astype(half)
     heads_own = small_own.astype(half)

time: 873 us -> 848 us (0.971)
  matrix products: 166 us -> 135 us
  Pallas kernels: 608 us -> 621 us
    pallas_call x1, Pallas kernels: 12.8 us -> 129 us  [backward_exchange(): pl.pallas_call(kernel, in_specs=[whole] * (scatters + 1 + len(rows_in) +...]
    pallas_call x4 -> x3, Pallas kernels: 586 us -> 481 us  [exchange(): pl.pallas_call(kernel, in_specs=[near_spec] * gathers + [whole] * (scatte...]
    dot_general x23 -> x18, matrix products: 164 us -> 134 us  [dot(): lax.dot_general(left, right, (dims, ((), ())), preferred_element_type=f32)]
  transfers between devices with their start and end apart: 2 -> 2, of which waited for: 1 -> 1; matrix products, arithmetic and copies ran while one was open for 2% -> 3% of each run, Pallas kernels for 0% -> 0%
where the time goes in v2:
time: 848 us; the launch traced here: 840 us
  Pallas kernels  621 us (73%)
  matrix products  135 us (16%)
  other arithmetic  49.3 us (6%)
  local copies, waits for them, and re-layouts  26.9 us (3%)
    pallas_call x3, Pallas kernels, exchange(): pl.pallas_call(kernel, in_specs=[near_spec] * gathers + [whole] * (scatte...  481 us
    dot_general x18, matrix products, dot(): lax.dot_general(left, right, (dims, ((), ())), preferred_element_type=f32)  134 us
    pallas_call x1, Pallas kernels, backward_exchange(): pl.pallas_call(kernel, in_specs=[whole] * (scatters + 1 + len(rows_in) +...  129 us
  transfers between devices with their start and end apart: 2, of which 1 were waited for; matrix products, arithmetic and copies ran while one was open for 3% of the time, Pallas kernels for 0%

profile of v2, /device:TPU:0, one launch (start us, length us, event | category | flops | bytes accessed | tf_op | source)
XLA Modules:
  0.0 839.8 jit_solution(4195335264502657899)
XLA Ops:
  13.4 93.4 %exchange_0.1 = (bf16[2048,1024]{1,0:T(8,128)(2,1)}, bf16[2048,128]{1,0:T(8,128)(2,1)}, bf16[2048,512]{1,0:T(8,128)(2,1)}, bf16[2048,512]{1,0:T(8,128)(2,1)}) custom-call(bf16[256,1024]{1,0:T(8,128)(2,1)} %pad_maximum_fusion.refs_0_, bf16[256,128]{1,0:T(8,128)(2,1)} %pad.37.refs_1_, bf16[256,512]{1,0:T(8,128)(2,1)} %convert_element_type.166.refs_2_, ...), custom_call_target="tpu_custom_call" | custom-call | tf_op jit(solution)/shard_map/exchange_0/pallas_call | solution.py:710
  124.8 3.6 fusion.22
  131.8 6.5 convolution_convert_fusion.9.q_ref.k_ref.v_ref.refs_6_
  139.9 9.8 %recur_forward.1 = (bf16[1024,512]{1,0:T(8,128)(2,1)}, bf16[1024,128]{1,0:T(8,128)(2,1)}, bf16[8,256,512]{2,1,0:T(8,128)(2,1)}) custom-call(f32[1024,256]{1,0:T(8,128)} %convolution_add_fusion.pre_ref.refs_9_, bf16[1024,1024]{1,0:T(8,128)(2,1)} %convolution_convert_fusion.9.q_ref.k_ref.v_ref.refs_6_, ...), custom_call_target="tpu_custom_call" | custom-call | flops 6000000000 | bytes 8388608 | tf_op jit(solution)/shard_map/recur_forward/pallas_call | solution.py:172
  151.2 6.3 convolution_convert_fusion.4.refs_3_
  157.6 170.2 %exchange_1.1 = (bf16[2048,1408]{1,0:T(8,128)(2,1)}, bf16[2048,1408]{1,0:T(8,128)(2,1)}, bf16[2048,1408]{1,0:T(8,128)(2,1)}, bf16[1024,2048]{1,0:T(8,128)(2,1)}) custom-call(bf16[256,1408]{1,0:T(8,128)(2,1)} %convert_element_type.162.refs_0_, bf16[256,1408]{1,0:T(8,128)(2,1)} %convert_element_type.163.refs_1_, bf16[256,1408]{1,0:T(8,128)(2,1)} %bitcast.72, ...), custom_call_target="tpu_custom_call" | custom-call | tf_op jit(solution)/shard_map/exchange_1/pallas_call | solution.py:710
  327.8 5.0 multiply_reduce_fusion
  334.4 8.4 %fusion.74 = f32[1024,1408]{1,0:T(8,128)} fusion(bf16[1024,2048]{1,0:T(8,128)(2,1)S(1)} %multiply_convert_fusion.1.refs_4_, bf16[2048,1408]{1,0:T(8,128)(2,1)S(1)} %bitcast.94), kind=kOutput, calls=%fused_computation.185 | convolution fusion | flops 5905580032 | bytes 15728640 | tf_op jit(solution)/shard_map/dot_general | solution.py:41
  342.9 4.5 fusion.10
  347.4 8.4 %fusion.75 = f32[1024,1408]{1,0:T(8,128)} fusion(bf16[1024,2048]{1,0:T(8,128)(2,1)S(1)} %get-tuple-element.132, bf16[2048,1408]{1,0:T(8,128)(2,1)S(1)} %bitcast.92), kind=kOutput, calls=%fused_computation.186 | convolution fusion | flops 5905580032 | bytes 15728640 | tf_op jit(solution)/shard_map/dot_general | solution.py:41
  355.8 13.8 %fusion.13 = (bf16[1024,1408]{1,0:T(8,128)(2,1)}, bf16[1024,1408]{1,0:T(8,128)(2,1)}, bf16[1024,1408]{1,0:T(8,128)(2,1)}) fusion(f32[1024,1408]{1,0:T(8,128)} %fusion.74, f32[1024,1408]{1,0:T(8,128)} %fusion.75, bf16[1024,2048]{1,0:T(8,128)(2,1)S(1)} %get-tuple-element.132, bf16[2048,1408]{1,0:T(8,128)(2,1)S(1)} %bitcast.96), kind=kOutput, calls=%fused_computation.26 | convolution fusion | flops 5928648704 | bytes 30146560 | tf_op jit(solution)/shard_map/dot_general | solution.py:41
  369.6 10.4 %fusion.76 = f32[1024,2048]{1,0:T(8,128)} fusion(bf16[1024,1408]{1,0:T(8,128)(2,1)} %get-tuple-element.128, bf16[2048,1408]{1,0:T(8,128)(2,1)S(1)} %bitcast.96), kind=kOutput, calls=%fused_computation.187 | convolution fusion | flops 5905580032 | bytes 17039360 | tf_op jit(solution)/shard_map/dot_general | solution.py:41
  380.1 8.8 %convolution_convert_fusion.refs_1_ = bf16[2048,1408]{1,0:T(8,128)(2,1)} fusion(bf16[1024,2048]{1,0:T(8,128)(2,1)S(1)} %get-tuple-element.132, bf16[1024,1408]{1,0:T(8,128)(2,1)S(1)} %copy-done.38), kind=kOutput, calls=%fused_computation.20 | convolution fusion | flops 5908463616 | bytes 12845056 | tf_op jit(solution)/shard_map/dot_general | solution.py:41
  388.9 8.3 convolution_convert_fusion.3.refs_6_
  397.2 8.7 %convolution_convert_fusion.1.refs_0_ = bf16[2048,1408]{1,0:T(8,128)(2,1)} fusion(bf16[1024,2048]{1,0:T(8,128)(2,1)S(1)} %multiply_convert_fusion.1.refs_4_, bf16[1024,1408]{1,0:T(8,128)(2,1)S(1)} %copy-done.40), kind=kOutput, calls=%fused_computation.21 | convolution fusion | flops 5908463616 | bytes 12845056 | tf_op jit(solution)/shard_map/dot_general | solution.py:41
  407.0 11.4 %convolution_convert_fusion.2.refs_0_ = bf16[2048,1408]{1,0:T(8,128)(2,1)} fusion(bf16[1024,2048]{1,0:T(8,128)(2,1)} %copy-done.11, bf16[1024,1408]{1,0:T(8,128)(2,1)} %get-tuple-element.130), kind=kOutput, calls=%fused_computation.22 | convolution fusion | flops 5908463616 | bytes 12845056 | tf_op jit(solution)/shard_map/dot_general | solution.py:41
  418.4 12.3 %add_convert_fusion.refs_2_ = bf16[1024,2048]{1,0:T(8,128)(2,1)} fusion(f32[1024,2048]{1,0:T(8,128)} %fusion.76, bf16[1024,1408]{1,0:T(8,128)(2,1)S(1)} %copy-done.39, bf16[2048,1408]{1,0:T(8,128)(2,1)} %get-tuple-element.54), kind=kOutput, calls=%fused_computation.16 | convolution fusion | flops 5909774336 | bytes 21233664 | tf_op jit(solution)/shard_map/dot_general | solution.py:41
  430.6 129.3 %backward_exchange_2.1 = (f32[256,1408]{1,0:T(8,128)}, f32[256,1408]{1,0:T(8,128)}, bf16[1024,2048]{1,0:T(8,128)(2,1)}, bf16[1024,2048]{1,0:T(8,128)(2,1)}, bf16...) custom-call(bf16[2048,1408]{1,0:T(8,128)(2,1)} %convolution_convert_, ...), custom_call_target="tpu_custom_call" | custom-call | tf_op jit(solution)/shard_map/backward_exchange_2/pallas_call | solution.py:914
  560.0 6.6 convolution_convert_fusion.7.refs_1_
  572.2 6.3 convolution_convert_fusion.6.refs_2_
  578.5 6.9 convolution_convert_fusion.5.refs_3_
  585.4 217.9 %exchange_3.1 = (f32[256,1408]{1,0:T(8,128)}, f32[256,512]{1,0:T(8,128)}, f32[256,512]{1,0:T(8,128)}, f32[256,1024]{1,0:T(8,128)}, f32[256,128]{1,0:T(8,128)}, /...) custom-call(bf16[2048,1408]{1,0:T(8,128)(2,1)} %convolution_convert_fusion.2.refs_0_, ...), custom_call_target="tpu_custom_call" | custom-call | tf_op jit(solution)/shard_map/exchange_3/pallas_call | solution.py:710
  806.7 4.6 fusion.4
  812.8 9.5 %fusion.8 = (bf16[1024,2048]{1,0:T(8,128)(2,1)}, bf16[1024,2048]{1,0:T(8,128)(2,1)}) fusion(bf16[1024,2048]{1,0:T(8,128)(2,1)S(1)} %copy-done.3, bf16[1024,2048]{1,0:T(8,128)(2,1)} %get-tuple-element.68, bf16[1024,2048]{1,0:T(8,128)(2,1)} %get-tuple-element.57, f32[1024]{0:T(1024)S(1)} %broadcast_multiply_fusion, f32[2048]{0:T(1024)S(1)} %copy-done.26, ...), kind=kLoop, calls=%fused_computation.12 | loop fusion | flops 33554432 | bytes 29380608 | tf_op jit(solution)/shard_map/convert_element_type | solution.py:1191
  (216 shorter events, 66.6 us)
Async XLA Ops:
  109.2 22.6 %copy-start.25 = (f32[2048]{0:T(1024)}, f32[2048]{0:T(1024)S(1)}, u32[]{:S(2)}) copy-start(f32[2048]{0:T(1024)S(1)} %get-tuple-element.125) | copy-start | bytes 24580
  109.2 233.6 %copy-start.24 = (f32[2048]{0:T(1024)}, f32[2048]{0:T(1024)S(1)}, u32[]{:S(2)}) copy-start(f32[2048]{0:T(1024)S(1)} %get-tuple-element.124) | copy-start | bytes 24580
  111.3 221.5 %copy-start.27 = (f32[1024]{0:T(1024)}, f32[1024]{0:T(1024)S(1)}, u32[]{:S(2)}) copy-start(f32[1024]{0:T(1024)S(1)} %fusion.63) | copy-start | bytes 12292
  114.4 17.4 %copy-start.29 = (f32[1024]{0:T(1024)}, f32[1024]{0:T(1024)S(1)}, u32[]{:S(2)}) copy-start(f32[1024]{0:T(1024)S(1)} %add_rsqrt_fusion.2) | copy-start | bytes 12292
  128.4 9.9 %copy-start.22 = (f32[1024,16]{0,1:T(8,128)}, f32[1024,16]{0,1:T(8,128)S(1)}, u32[]{:S(2)}) copy-start(f32[1024,16]{0,1:T(8,128)S(1)} %fusion.22) | copy-start | bytes 196612
  139.9 11.4 %copy-start.13 = (bf16[2048,512]{1,0:T(8,128)(2,1)S(1)}, bf16[2048,512]{1,0:T(8,128)(2,1)}, u32[]{:S(2)}) copy-start(bf16[2048,512]{1,0:T(8,128)(2,1)} %get-tuple-element.50.refs_12_) | copy-start | bytes 6291460
  332.8 14.6 %slice-start = ((s8[5767168]{0:T(1024)(128)(4,1)}), s8[1572864]{0:T(1024)(128)(4,1)S(1)}, s32[]{:S(2)}) async-start(s8[5767168]{0:T(1024)(128)(4,1)} %bitcast.91), calls=%async_computation | async-start | bytes 3145728
  333.6 63.6 %copy-start.6 = (bf16[1024,2048]{1,0:T(8,128)(2,1)}, bf16[1024,2048]{1,0:T(8,128)(2,1)S(1)}, u32[]{:S(2)}) copy-start(bf16[1024,2048]{1,0:T(8,128)(2,1)S(1)} %multiply_convert_fusion.1.refs_4_) | copy-start | bytes 12582916
  334.4 8.4 %copy-start.4 = (bf16[1024,2048]{1,0:T(8,128)(2,1)S(1)}, bf16[1024,2048]{1,0:T(8,128)(2,1)}, u32[]{:S(2)}) copy-start(bf16[1024,2048]{1,0:T(8,128)(2,1)} %get-tuple-element.51) | copy-start | bytes 12582916
  334.4 13.0 %slice-start.1 = ((s8[5767168]{0:T(1024)(128)(4,1)}), s8[4194304]{0:T(1024)(128)(4,1)S(1)}, s32[]{:S(2)}) async-start(s8[5767168]{0:T(1024)(128)(4,1)} %bitcast.91), calls=%async_computation.1 | async-start | bytes 8388608
  342.8 13.0 %slice-start.4 = ((s8[5767168]{0:T(1024)(128)(4,1)}), s8[4194304]{0:T(1024)(128)(4,1)S(1)}, s32[]{:S(2)}) async-start(s8[5767168]{0:T(1024)(128)(4,1)} %bitcast.95), calls=%async_computation.4 | async-start | bytes 8388608
  347.4 32.7 %copy-start.11 = (bf16[1024,2048]{1,0:T(8,128)(2,1)}, bf16[1024,2048]{1,0:T(8,128)(2,1)S(1)}, u32[]{:S(2)}) copy-start(bf16[1024,2048]{1,0:T(8,128)(2,1)S(1)} %get-tuple-element.132) | copy-start | bytes 12582916
  347.4 8.4 %slice-start.5 = ((s8[5767168]{0:T(1024)(128)(4,1)}), s8[1572864]{0:T(1024)(128)(4,1)S(1)}, s32[]{:S(2)}) async-start(s8[5767168]{0:T(1024)(128)(4,1)} %bitcast.95), calls=%async_computation.5 | async-start | bytes 3145728
  369.6 10.4 %copy-start.38 = (bf16[1024,1408]{1,0:T(8,128)(2,1)S(1)}, bf16[1024,1408]{1,0:T(8,128)(2,1)}, u32[]{:S(2)}) copy-start(bf16[1024,1408]{1,0:T(8,128)(2,1)} %get-tuple-element.128) | copy-start | bytes 8650756
  380.1 8.8 %copy-start.40 = (bf16[1024,1408]{1,0:T(8,128)(2,1)S(1)}, bf16[1024,1408]{1,0:T(8,128)(2,1)}, u32[]{:S(2)}) copy-start(bf16[1024,1408]{1,0:T(8,128)(2,1)} %get-tuple-element.129) | copy-start | bytes 8650756
  407.0 11.4 %copy-start.39 = (bf16[1024,1408]{1,0:T(8,128)(2,1)S(1)}, bf16[1024,1408]{1,0:T(8,128)(2,1)}, u32[]{:S(2)}) copy-start(bf16[1024,1408]{1,0:T(8,128)(2,1)} %get-tuple-element.130) | copy-start | bytes 8650756
  430.6 129.3 %copy-start.9 = (bf16[1024,512]{1,0:T(8,128)(2,1)S(1)}, bf16[1024,512]{1,0:T(8,128)(2,1)}, u32[]{:S(2)}) copy-start(bf16[1024,512]{1,0:T(8,128)(2,1)} %get-tuple-element.48.refs_7_) | copy-start | bytes 3145732
  804.9 24.3 %collective-permute-start = (bf16[256,128]{1,0:T(8,128)(2,1)}, bf16[256,128]{1,0:T(8,128)(2,1)}, u32[]{:S(2)}, u32[]{:S(2)}) collective-permute-start(bf16[256,128]{1,0:T(8,128)(2,1)} %convert_element_type.200), channel_id=1, source_target_pairs={{0,1},{1,0},{2,3},{3,2},{4,5},{5,4},{6,7},{7,6},{8,9},{9,8},{10,11... | collective-permute-start | bytes 196616 | tf_op jit(solution)/shard_map/ppermute | solution.py:1193
  812.8 9.5 %copy-start.18 = (f32[256,128]{1,0:T(8,128)S(1)}, f32[256,128]{1,0:T(8,128)}, u32[]{:S(2)}) copy-start(f32[256,128]{1,0:T(8,128)} %get-tuple-element.69) | copy-start | bytes 393220
  812.8 11.1 %copy-start.16 = (f32[256,1408]{1,0:T(8,128)S(1)}, f32[256,1408]{1,0:T(8,128)}, u32[]{:S(2)}) copy-start(f32[256,1408]{1,0:T(8,128)} %get-tuple-element.75) | copy-start | bytes 4325380
  822.3 14.4 %copy-start.21 = (f32[256,512]{1,0:T(8,128)S(1)}, f32[256,512]{1,0:T(8,128)}, u32[]{:S(2)}) copy-start(f32[256,512]{1,0:T(8,128)} %get-tuple-element.173) | copy-start | bytes 1572868
  822.3 15.2 %copy-start.15 = (f32[256,1408]{1,0:T(8,128)S(1)}, f32[256,1408]{1,0:T(8,128)}, u32[]{:S(2)}) copy-start(f32[256,1408]{1,0:T(8,128)} %get-tuple-element.180) | copy-start | bytes 4325380
  825.4 13.1 %copy-start.17 = (f32[256,1408]{1,0:T(8,128)S(1)}, f32[256,1408]{1,0:T(8,128)}, u32[]{:S(2)}) copy-start(f32[256,1408]{1,0:T(8,128)} %get-tuple-element.181) | copy-start | bytes 4325380
  830.1 4.3 collective-permute-start.1
  (25 other events, 156.0 us)

commit v3 on v2

--- a/solution.py
+++ b/solution.py
@@ -462,13 +462,14 @@
         return pltpu.make_async_copy(src, dst, links.local.at[self.loads + 3 * k + part])
 
     def start(self):
-        links = self.links
         for k in range(LINE):
             for part in range(3):
                 self.load(k, part).start()
-        for k in range(LINE):
-            src = self.block(self.order[k], 1 - links.x, False)
-            links.copy(self.base + k, src, self.beside.at[k], links.beside()).start()
+
+    def aside(self, k):
+        links = self.links
+        src = self.block(self.order[k], 1 - links.x, False)
+        links.copy(self.base + k, src, self.beside.at[k], links.beside()).start()
 
     def step(self, k, rest):
         links = self.links
@@ -669,6 +670,9 @@
         links.greet()
         for item in gather + scatter + total:
             item.start()
+        for k in range(LINE):
+            for item in scatter:
+                item.aside(k)
         for item in total:
             item.middle()
         for k in range(LINE - 1):
@@ -852,6 +856,9 @@
         for item in scatter:
             item.start()
         total.start()
+        for k in range(LINE):
+            for item in scatter:
+                item.aside(k)
         for load in loads:
             load.start()
         total.middle()

time: 848 us -> 799 us (0.942)
  Pallas kernels: 621 us -> 573 us
    pallas_call x3, Pallas kernels: 481 us -> 442 us  [exchange(): pl.pallas_call(kernel, in_specs=[near_spec] * gathers + [whole] * (scatte...]
where the time goes in v3:
time: 799 us; the launch traced here: 791 us
  Pallas kernels  573 us (72%)
  matrix products  135 us (17%)
  other arithmetic  49.3 us (6%)
  local copies, waits for them, and re-layouts  26.9 us (3%)
    pallas_call x3, Pallas kernels, exchange(): pl.pallas_call(kernel, in_specs=[near_spec] * gathers + [whole] * (scatte...  442 us
    dot_general x18, matrix products, dot(): lax.dot_general(left, right, (dims, ((), ())), preferred_element_type=f32)  134 us
    pallas_call x1, Pallas kernels, backward_exchange(): pl.pallas_call(kernel, in_specs=[whole] * (scatters + 1 + len(rows_in) +...  121 us
  transfers between devices with their start and end apart: 2, of which 1 were waited for; matrix products, arithmetic and copies ran while one was open for 3% of the time, Pallas kernels for 0%

profile of v3, /device:TPU:0, one launch (start us, length us, event | category | flops | bytes accessed | tf_op | source)
XLA Modules:
  0.0 791.2 jit_solution(4674434310991702195)
XLA Ops:
  13.4 93.4 %exchange_0.1 = (bf16[2048,1024]{1,0:T(8,128)(2,1)}, bf16[2048,128]{1,0:T(8,128)(2,1)}, bf16[2048,512]{1,0:T(8,128)(2,1)}, bf16[2048,512]{1,0:T(8,128)(2,1)}) custom-call(bf16[256,1024]{1,0:T(8,128)(2,1)} %pad_maximum_fusion.refs_0_, bf16[256,128]{1,0:T(8,128)(2,1)} %pad.37.refs_1_, bf16[256,512]{1,0:T(8,128)(2,1)} %convert_element_type.166.refs_2_, ...), custom_call_target="tpu_custom_call" | custom-call | tf_op jit(solution)/shard_map/exchange_0/pallas_call | solution.py:714
  124.8 3.6 fusion.22
  131.8 6.5 convolution_convert_fusion.9.q_ref.k_ref.v_ref.refs_6_
  139.9 9.8 %recur_forward.1 = (bf16[1024,512]{1,0:T(8,128)(2,1)}, bf16[1024,128]{1,0:T(8,128)(2,1)}, bf16[8,256,512]{2,1,0:T(8,128)(2,1)}) custom-call(f32[1024,256]{1,0:T(8,128)} %convolution_add_fusion.pre_ref.refs_9_, bf16[1024,1024]{1,0:T(8,128)(2,1)} %convolution_convert_fusion.9.q_ref.k_ref.v_ref.refs_6_, ...), custom_call_target="tpu_custom_call" | custom-call | flops 6000000000 | bytes 8388608 | tf_op jit(solution)/shard_map/recur_forward/pallas_call | solution.py:172
  151.2 6.3 convolution_convert_fusion.4.refs_3_
  157.6 170.2 %exchange_1.1 = (bf16[2048,1408]{1,0:T(8,128)(2,1)}, bf16[2048,1408]{1,0:T(8,128)(2,1)}, bf16[2048,1408]{1,0:T(8,128)(2,1)}, bf16[1024,2048]{1,0:T(8,128)(2,1)}) custom-call(bf16[256,1408]{1,0:T(8,128)(2,1)} %convert_element_type.162.refs_0_, bf16[256,1408]{1,0:T(8,128)(2,1)} %convert_element_type.163.refs_1_, bf16[256,1408]{1,0:T(8,128)(2,1)} %bitcast.72, ...), custom_call_target="tpu_custom_call" | custom-call | tf_op jit(solution)/shard_map/exchange_1/pallas_call | solution.py:714
  327.8 5.0 multiply_reduce_fusion
  334.4 8.4 %fusion.74 = f32[1024,1408]{1,0:T(8,128)} fusion(bf16[1024,2048]{1,0:T(8,128)(2,1)S(1)} %multiply_convert_fusion.1.refs_4_, bf16[2048,1408]{1,0:T(8,128)(2,1)S(1)} %bitcast.94), kind=kOutput, calls=%fused_computation.185 | convolution fusion | flops 5905580032 | bytes 15728640 | tf_op jit(solution)/shard_map/dot_general | solution.py:41
  342.9 4.5 fusion.10
  347.4 8.4 %fusion.75 = f32[1024,1408]{1,0:T(8,128)} fusion(bf16[1024,2048]{1,0:T(8,128)(2,1)S(1)} %get-tuple-element.132, bf16[2048,1408]{1,0:T(8,128)(2,1)S(1)} %bitcast.92), kind=kOutput, calls=%fused_computation.186 | convolution fusion | flops 5905580032 | bytes 15728640 | tf_op jit(solution)/shard_map/dot_general | solution.py:41
  355.8 13.8 %fusion.13 = (bf16[1024,1408]{1,0:T(8,128)(2,1)}, bf16[1024,1408]{1,0:T(8,128)(2,1)}, bf16[1024,1408]{1,0:T(8,128)(2,1)}) fusion(f32[1024,1408]{1,0:T(8,128)} %fusion.74, f32[1024,1408]{1,0:T(8,128)} %fusion.75, bf16[1024,2048]{1,0:T(8,128)(2,1)S(1)} %get-tuple-element.132, bf16[2048,1408]{1,0:T(8,128)(2,1)S(1)} %bitcast.96), kind=kOutput, calls=%fused_computation.26 | convolution fusion | flops 5928648704 | bytes 30146560 | tf_op jit(solution)/shard_map/dot_general | solution.py:41
  369.6 10.4 %fusion.76 = f32[1024,2048]{1,0:T(8,128)} fusion(bf16[1024,1408]{1,0:T(8,128)(2,1)} %get-tuple-element.128, bf16[2048,1408]{1,0:T(8,128)(2,1)S(1)} %bitcast.96), kind=kOutput, calls=%fused_computation.187 | convolution fusion | flops 5905580032 | bytes 17039360 | tf_op jit(solution)/shard_map/dot_general | solution.py:41
  380.1 8.8 %convolution_convert_fusion.refs_1_ = bf16[2048,1408]{1,0:T(8,128)(2,1)} fusion(bf16[1024,2048]{1,0:T(8,128)(2,1)S(1)} %get-tuple-element.132, bf16[1024,1408]{1,0:T(8,128)(2,1)S(1)} %copy-done.38), kind=kOutput, calls=%fused_computation.20 | convolution fusion | flops 5908463616 | bytes 12845056 | tf_op jit(solution)/shard_map/dot_general | solution.py:41
  388.9 8.3 %convolution_convert_fusion.3.refs_6_ = bf16[1024,2048]{1,0:T(8,128)(2,1)} fusion(bf16[1024,1408]{1,0:T(8,128)(2,1)S(1)} %copy-done.40, bf16[2048,1408]{1,0:T(8,128)(2,1)S(1)} %bitcast.94), kind=kOutput, calls=%fused_computation.31 | convolution fusion | flops 5907677184 | bytes 12845056 | tf_op jit(solution)/shard_map/dot_general | solution.py:41
  397.2 8.7 %convolution_convert_fusion.1.refs_0_ = bf16[2048,1408]{1,0:T(8,128)(2,1)} fusion(bf16[1024,2048]{1,0:T(8,128)(2,1)S(1)} %multiply_convert_fusion.1.refs_4_, bf16[1024,1408]{1,0:T(8,128)(2,1)S(1)} %copy-done.40), kind=kOutput, calls=%fused_computation.21 | convolution fusion | flops 5908463616 | bytes 12845056 | tf_op jit(solution)/shard_map/dot_general | solution.py:41
  407.0 11.4 %convolution_convert_fusion.2.refs_0_ = bf16[2048,1408]{1,0:T(8,128)(2,1)} fusion(bf16[1024,2048]{1,0:T(8,128)(2,1)} %copy-done.11, bf16[1024,1408]{1,0:T(8,128)(2,1)} %get-tuple-element.130), kind=kOutput, calls=%fused_computation.22 | convolution fusion | flops 5908463616 | bytes 12845056 | tf_op jit(solution)/shard_map/dot_general | solution.py:41
  418.4 12.3 %add_convert_fusion.refs_2_ = bf16[1024,2048]{1,0:T(8,128)(2,1)} fusion(f32[1024,2048]{1,0:T(8,128)} %fusion.76, bf16[1024,1408]{1,0:T(8,128)(2,1)S(1)} %copy-done.39, bf16[2048,1408]{1,0:T(8,128)(2,1)} %get-tuple-element.54), kind=kOutput, calls=%fused_computation.16 | convolution fusion | flops 5909774336 | bytes 21233664 | tf_op jit(solution)/shard_map/dot_general | solution.py:41
  430.6 121.2 %backward_exchange_2.1 = (f32[256,1408]{1,0:T(8,128)}, f32[256,1408]{1,0:T(8,128)}, bf16[1024,2048]{1,0:T(8,128)(2,1)}, bf16[1024,2048]{1,0:T(8,128)(2,1)}, bf16...) custom-call(bf16[2048,1408]{1,0:T(8,128)(2,1)} %convolution_convert_, ...), custom_call_target="tpu_custom_call" | custom-call | tf_op jit(solution)/shard_map/backward_exchange_2/pallas_call | solution.py:921
  552.0 6.6 convolution_convert_fusion.7.refs_1_
  564.1 6.3 convolution_convert_fusion.6.refs_2_
  570.4 6.9 convolution_convert_fusion.5.refs_3_
  577.3 178.8 %exchange_3.1 = (f32[256,1408]{1,0:T(8,128)}, f32[256,512]{1,0:T(8,128)}, f32[256,512]{1,0:T(8,128)}, f32[256,1024]{1,0:T(8,128)}, f32[256,128]{1,0:T(8,128)}, /...) custom-call(bf16[2048,1408]{1,0:T(8,128)(2,1)} %convolution_convert_fusion.2.refs_0_, ...), custom_call_target="tpu_custom_call" | custom-call | tf_op jit(solution)/shard_map/exchange_3/pallas_call | solution.py:714
  757.9 4.6 fusion.4
  764.0 9.5 %fusion.8 = (bf16[1024,2048]{1,0:T(8,128)(2,1)}, bf16[1024,2048]{1,0:T(8,128)(2,1)}) fusion(bf16[1024,2048]{1,0:T(8,128)(2,1)S(1)} %copy-done.3, bf16[1024,2048]{1,0:T(8,128)(2,1)} %get-tuple-element.68, bf16[1024,2048]{1,0:T(8,128)(2,1)} %get-tuple-element.57, f32[1024]{0:T(1024)S(1)} %broadcast_multiply_fusion, f32[2048]{0:T(1024)S(1)} %copy-done.26, ...), kind=kLoop, calls=%fused_computation.12 | loop fusion | flops 33554432 | bytes 29380608 | tf_op jit(solution)/shard_map/convert_element_type | solution.py:1198
  (216 shorter events, 65.1 us)
Async XLA Ops:
  109.2 22.6 %copy-start.25 = (f32[2048]{0:T(1024)}, f32[2048]{0:T(1024)S(1)}, u32[]{:S(2)}) copy-start(f32[2048]{0:T(1024)S(1)} %get-tuple-element.125) | copy-start | bytes 24580
  109.2 233.6 %copy-start.24 = (f32[2048]{0:T(1024)}, f32[2048]{0:T(1024)S(1)}, u32[]{:S(2)}) copy-start(f32[2048]{0:T(1024)S(1)} %get-tuple-element.124) | copy-start | bytes 24580
  111.3 221.5 %copy-start.27 = (f32[1024]{0:T(1024)}, f32[1024]{0:T(1024)S(1)}, u32[]{:S(2)}) copy-start(f32[1024]{0:T(1024)S(1)} %fusion.63) | copy-start | bytes 12292
  114.4 17.4 %copy-start.29 = (f32[1024]{0:T(1024)}, f32[1024]{0:T(1024)S(1)}, u32[]{:S(2)}) copy-start(f32[1024]{0:T(1024)S(1)} %add_rsqrt_fusion.2) | copy-start | bytes 12292
  128.4 9.9 %copy-start.22 = (f32[1024,16]{0,1:T(8,128)}, f32[1024,16]{0,1:T(8,128)S(1)}, u32[]{:S(2)}) copy-start(f32[1024,16]{0,1:T(8,128)S(1)} %fusion.22) | copy-start | bytes 196612
  139.9 11.4 %copy-start.13 = (bf16[2048,512]{1,0:T(8,128)(2,1)S(1)}, bf16[2048,512]{1,0:T(8,128)(2,1)}, u32[]{:S(2)}) copy-start(bf16[2048,512]{1,0:T(8,128)(2,1)} %get-tuple-element.50.refs_12_) | copy-start | bytes 6291460
  332.8 14.6 %slice-start = ((s8[5767168]{0:T(1024)(128)(4,1)}), s8[1572864]{0:T(1024)(128)(4,1)S(1)}, s32[]{:S(2)}) async-start(s8[5767168]{0:T(1024)(128)(4,1)} %bitcast.91), calls=%async_computation | async-start | bytes 3145728
  333.6 63.6 %copy-start.6 = (bf16[1024,2048]{1,0:T(8,128)(2,1)}, bf16[1024,2048]{1,0:T(8,128)(2,1)S(1)}, u32[]{:S(2)}) copy-start(bf16[1024,2048]{1,0:T(8,128)(2,1)S(1)} %multiply_convert_fusion.1.refs_4_) | copy-start | bytes 12582916
  334.4 8.4 %copy-start.4 = (bf16[1024,2048]{1,0:T(8,128)(2,1)S(1)}, bf16[1024,2048]{1,0:T(8,128)(2,1)}, u32[]{:S(2)}) copy-start(bf16[1024,2048]{1,0:T(8,128)(2,1)} %get-tuple-element.51) | copy-start | bytes 12582916
  334.4 13.0 %slice-start.1 = ((s8[5767168]{0:T(1024)(128)(4,1)}), s8[4194304]{0:T(1024)(128)(4,1)S(1)}, s32[]{:S(2)}) async-start(s8[5767168]{0:T(1024)(128)(4,1)} %bitcast.91), calls=%async_computation.1 | async-start | bytes 8388608
  342.8 13.0 %slice-start.4 = ((s8[5767168]{0:T(1024)(128)(4,1)}), s8[4194304]{0:T(1024)(128)(4,1)S(1)}, s32[]{:S(2)}) async-start(s8[5767168]{0:T(1024)(128)(4,1)} %bitcast.95), calls=%async_computation.4 | async-start | bytes 8388608
  347.4 32.7 %copy-start.11 = (bf16[1024,2048]{1,0:T(8,128)(2,1)}, bf16[1024,2048]{1,0:T(8,128)(2,1)S(1)}, u32[]{:S(2)}) copy-start(bf16[1024,2048]{1,0:T(8,128)(2,1)S(1)} %get-tuple-element.132) | copy-start | bytes 12582916
  347.4 8.4 %slice-start.5 = ((s8[5767168]{0:T(1024)(128)(4,1)}), s8[1572864]{0:T(1024)(128)(4,1)S(1)}, s32[]{:S(2)}) async-start(s8[5767168]{0:T(1024)(128)(4,1)} %bitcast.95), calls=%async_computation.5 | async-start | bytes 3145728
  369.6 10.4 %copy-start.38 = (bf16[1024,1408]{1,0:T(8,128)(2,1)S(1)}, bf16[1024,1408]{1,0:T(8,128)(2,1)}, u32[]{:S(2)}) copy-start(bf16[1024,1408]{1,0:T(8,128)(2,1)} %get-tuple-element.128) | copy-start | bytes 8650756
  380.1 8.8 %copy-start.40 = (bf16[1024,1408]{1,0:T(8,128)(2,1)S(1)}, bf16[1024,1408]{1,0:T(8,128)(2,1)}, u32[]{:S(2)}) copy-start(bf16[1024,1408]{1,0:T(8,128)(2,1)} %get-tuple-element.129) | copy-start | bytes 8650756
  407.0 11.4 %copy-start.39 = (bf16[1024,1408]{1,0:T(8,128)(2,1)S(1)}, bf16[1024,1408]{1,0:T(8,128)(2,1)}, u32[]{:S(2)}) copy-start(bf16[1024,1408]{1,0:T(8,128)(2,1)} %get-tuple-element.130) | copy-start | bytes 8650756
  430.6 121.2 %copy-start.9 = (bf16[1024,512]{1,0:T(8,128)(2,1)S(1)}, bf16[1024,512]{1,0:T(8,128)(2,1)}, u32[]{:S(2)}) copy-start(bf16[1024,512]{1,0:T(8,128)(2,1)} %get-tuple-element.48.refs_7_) | copy-start | bytes 3145732
  757.8 22.7 %collective-permute-start = (bf16[256,128]{1,0:T(8,128)(2,1)}, bf16[256,128]{1,0:T(8,128)(2,1)}, u32[]{:S(2)}, u32[]{:S(2)}) collective-permute-start(bf16[256,128]{1,0:T(8,128)(2,1)} %convert_element_type.200), channel_id=1, source_target_pairs={{0,1},{1,0},{2,3},{3,2},{4,5},{5,4},{6,7},{7,6},{8,9},{9,8},{10,11... | collective-permute-start | bytes 196616 | tf_op jit(solution)/shard_map/ppermute | solution.py:1200
  764.0 9.5 %copy-start.18 = (f32[256,128]{1,0:T(8,128)S(1)}, f32[256,128]{1,0:T(8,128)}, u32[]{:S(2)}) copy-start(f32[256,128]{1,0:T(8,128)} %get-tuple-element.69) | copy-start | bytes 393220
  764.0 11.1 %copy-start.16 = (f32[256,1408]{1,0:T(8,128)S(1)}, f32[256,1408]{1,0:T(8,128)}, u32[]{:S(2)}) copy-start(f32[256,1408]{1,0:T(8,128)} %get-tuple-element.75) | copy-start | bytes 4325380
  773.5 14.5 %copy-start.21 = (f32[256,512]{1,0:T(8,128)S(1)}, f32[256,512]{1,0:T(8,128)}, u32[]{:S(2)}) copy-start(f32[256,512]{1,0:T(8,128)} %get-tuple-element.173) | copy-start | bytes 1572868
  773.5 15.3 %copy-start.15 = (f32[256,1408]{1,0:T(8,128)S(1)}, f32[256,1408]{1,0:T(8,128)}, u32[]{:S(2)}) copy-start(f32[256,1408]{1,0:T(8,128)} %get-tuple-element.180) | copy-start | bytes 4325380
  776.7 13.3 %copy-start.17 = (f32[256,1408]{1,0:T(8,128)S(1)}, f32[256,1408]{1,0:T(8,128)}, u32[]{:S(2)}) copy-start(f32[256,1408]{1,0:T(8,128)} %get-tuple-element.181) | copy-start | bytes 4325380
  781.3 4.5 collective-permute-start.1
  (25 other events, 154.4 us)

commit v4 on v3

--- a/solution.py
+++ b/solution.py
@@ -222,6 +222,7 @@
 MESH = pl.DeviceIdType.MESH
 BULK = 13
 PIECES = 4
+VMEM_LIMIT = 63 * 2**20
 
 
 class Links:
@@ -413,6 +414,15 @@
 
 
 ORDER = ((3, 3, 0, 0), (2, 0, 3, 1), (1, 2, 1, 2), (0, 1, 2, 3))
+
+
+def turn(order, k):
+    return (
+        (1 - k) * (2 - k) * (3 - k) // 6 * order[0]
+        + k * (2 - k) * (3 - k) // 2 * order[1]
+        + k * (k - 1) * (3 - k) // 2 * order[2]
+        + k * (k - 1) * (k - 2) // 6 * order[3]
+    )
 
 
 class Scatter:
@@ -451,9 +461,14 @@
         first = (z * 2 + x) * self.rows + (self.bulk if rest else 0)
         return self.total.at[pl.ds(first, self.rest if rest else self.bulk), :]
 
+    def turn(self, k):
+        if isinstance(k, int):
+            return self.order[k]
+        return turn(self.order, k)
+
     def load(self, k, part):
         links = self.links
-        d = self.order[k]
+        d = self.turn(k)
         if part == 2:
             src, dst = self.block(d, links.x, False), self.kept.at[k]
         else:
@@ -463,12 +478,15 @@
 
     def start(self):
         for k in range(LINE):
-            for part in range(3):
-                self.load(k, part).start()
+            self.fetch(k)
+
+    def fetch(self, k):
+        for part in range(3):
+            self.load(k, part).start()
 
     def aside(self, k):
         links = self.links
-        src = self.block(self.order[k], 1 - links.x, False)
+        src = self.block(self.turn(k), 1 - links.x, False)
         links.copy(self.base + k, src, self.beside.at[k], links.beside()).start()
 
     def step(self, k, rest):
@@ -754,6 +772,88 @@
             copy.wait()
 
 
+class Maker:
+    STEPS = 2 * LINE
+
+    def __init__(self, links, sems, base, lefts, left_buffers, pairs):
+        self.links, self.sems, self.base = links, sems, base
+        self.lefts, self.left_buffers, self.pairs = lefts, left_buffers, pairs
+        self.rows = left_buffers[0].shape[2]
+
+    @staticmethod
+    def sem_count(lefts, pairs):
+        return 2 * (lefts + pairs)
+
+    def place(self, j):
+        order = self.pairs[0][4].order
+        x = self.links.x
+        column = 1 - x + (j % 2) * (2 * x - 1)
+        return (turn(order, j // 2) * 2 + column) * self.rows
+
+    def moves(self, j):
+        first = pl.multiple_of(self.place(j), self.rows)
+        slot = j % 2
+        for n, (left, buffer) in enumerate(zip(self.lefts, self.left_buffers)):
+            yield pltpu.make_async_copy(
+                left.at[:, pl.ds(first, self.rows)], buffer.at[slot],
+                self.sems.at[self.base + 2 * n + slot],
+            )
+
+    def stores(self, j):
+        first = pl.multiple_of(self.place(j), self.rows)
+        slot = j % 2
+        base = self.base + 2 * len(self.lefts)
+        for n, (_, _, buffer, total, _) in enumerate(self.pairs):
+            yield pltpu.make_async_copy(
+                buffer.at[slot], total.at[pl.ds(first, self.rows), :],
+                self.sems.at[base + 2 * n + slot],
+            )
+
+    def start(self):
+        for move in self.moves(0):
+            move.start()
+
+    def run(self, between):
+        def body(j, state):
+            @pl.when(j + 1 < self.STEPS)
+            def _():
+                for move in self.moves(j + 1):
+                    move.start()
+
+            for move in self.moves(j):
+                move.wait()
+            slot = j % 2
+            for which, b, buffer, _, _ in self.pairs:
+                left = self.left_buffers[which][slot]
+                buffer[slot] = dot(left, b[...], TN).astype(half)
+            for store in self.stores(j):
+                store.start()
+
+            @pl.when(j >= 1)
+            def _():
+                for store in self.stores(j - 1):
+                    store.wait()
+
+            @pl.when(j % 2 == 1)
+            def _():
+                for pair in self.pairs:
+                    pair[4].aside(j // 2)
+
+            @pl.when((j % 2 == 0) & (j >= 2))
+            def _():
+                for pair in self.pairs:
+                    pair[4].fetch(j // 2 - 1)
+
+            between(j)
+            return state
+
+        lax.fori_loop(0, self.STEPS, body, 0)
+        for store in self.stores(self.STEPS - 1):
+            store.wait()
+        for pair in self.pairs:
+            pair[4].fetch(LINE - 1)
+
+
 def row_sum(values):
     return jnp.sum(values, axis=0, keepdims=True)
 
@@ -799,8 +899,8 @@
     return d_attn, d_outgate, d_qkv, d_pre, d_rank, d_normed.astype(half)
 
 
-def backward_exchange(number, totals, part, rows_in, weights, gains):
-    scatters = len(totals)
+def backward_exchange(number, totals, part, rows_in, weights, gains, left, right):
+    scatters = len(totals) + 1
     length, width = part.shape
     count = length // CHUNK
     dk = weights[4].shape[1]
@@ -810,17 +910,21 @@
     in_types = [half] + [a.dtype for a in rows_in]
     streams = len(in_shapes)
     sum_wide = (width, dv, dk, width)
+    made = jax.ShapeDtypeStruct((left.shape[1], right.shape[1]), half)
+    rows = made.shape[0] // (2 * LINE)
     scratch = []
-    for total in totals:
+    for total in (*totals, made):
         scratch += Scatter.scratch(total.shape[0] // (2 * LINE), total.shape[1])
     scratch += Total.scratch(length, width)
     scratch += [pltpu.VMEM((2,) + s, t) for s, t in zip(in_shapes, in_types)]
     scratch += [pltpu.VMEM((2, CHUNK, w), half) for w in outs_wide]
-    scratch += [pltpu.VMEM(w.shape, half) for w in weights]
+    scratch += [pltpu.VMEM(w.shape, half) for w in (*weights, right)]
+    scratch += [pltpu.VMEM((2, length, rows), half), pltpu.VMEM((2, rows, made.shape[1]), half)]
     scratch += [pltpu.VMEM((dk, dv), f32)]
     remote = Scatter.SEMS * scatters + Total.SEMS
     near = 12 * scatters + 2 * PIECES
-    extra = 2 * streams + 2 * len(outs_wide) + len(weights)
+    maker_base = 2 * streams + 2 * len(outs_wide) + len(weights) + 1
+    extra = maker_base + Maker.sem_count(1, 1)
     scratch += [
         pltpu.SemaphoreType.DMA((remote,)),
         pltpu.SemaphoreType.DMA((remote,)),
@@ -835,44 +939,80 @@
             taken, refs[:count] = refs[:count], []
             return taken
 
-        total_refs, (part_ref,), row_refs = pop(scatters), pop(1), pop(streams - 1)
-        weight_refs, gain_refs = pop(len(weights)), pop(2)
-        own_refs, (sum_ref,), out_refs, gain_sums = pop(scatters), pop(1), pop(6), pop(4)
+        total_refs, (part_ref,), row_refs = pop(scatters - 1), pop(1), pop(streams - 1)
+        weight_refs, (left_ref, right_ref), gain_refs = pop(len(weights)), pop(2), pop(2)
+        own_refs, (sum_ref, made_ref), out_refs, gain_sums = pop(scatters), pop(2), pop(6), pop(4)
         buffers = [pop(6) for _ in range(scatters)]
         sum_buffers = pop(3)
-        in_buffers, out_buffers, near_weights = pop(streams), pop(6), pop(len(weights))
-        (carry,) = pop(1)
+        in_buffers, out_buffers, near_weights = pop(streams), pop(6), pop(len(weights) + 1)
+        (left_buffer, made_buffer, carry) = pop(3)
         sems = refs.pop()
         links = Links(*refs)
-        scatter = [Scatter(links, *a) for a in zip(total_refs, own_refs, buffers)]
+        scatter = [
+            Scatter(links, *a) for a in zip((*total_refs, made_ref), own_refs, buffers)
+        ]
+        ready, late = scatter[:-1], scatter[-1:]
         total = Total(links, part_ref, sum_ref, sum_buffers)
         inputs = Stream(sems, 0, [sum_ref] + row_refs, in_buffers, lambda i: count - 1 - i)
         outputs = Stream(sems, 2 * streams, out_refs, out_buffers, lambda i: count - 1 - i)
+        right_near = near_weights.pop()
         loads = [
             pltpu.make_async_copy(far, close, sems.at[2 * streams + 12 + n])
-            for n, (far, close) in enumerate(zip(weight_refs, near_weights))
+            for n, (far, close) in enumerate(
+                zip((right_ref, *weight_refs), (right_near, *near_weights))
+            )
         ]
+        maker = Maker(
+            links, sems, maker_base, [left_ref], [left_buffer],
+            [(0, right_near, made_buffer, made_ref, late[0])],
+        )
         links.greet()
-        for item in scatter:
-            item.start()
+        maker.start()
         total.start()
         for k in range(LINE):
-            for item in scatter:
+            for item in ready:
                 item.aside(k)
         for load in loads:
             load.start()
-        total.middle()
+        for item in ready:
+            item.start()
+        loads[0].wait()
+
+        def between(j):
+            @pl.when(j == 1)
+            def _():
+                total.middle()
+
+            @pl.when(j == 3)
+            def _():
+                for item in ready:
+                    item.step(0, True)
+
+            @pl.when(j == 5)
+            def _():
+                for item in ready:
+                    item.step(1, True)
+                    item.step(0, False)
+
+            @pl.when(j == 7)
+            def _():
+                for item in ready:
+                    item.step(2, True)
+
+        maker.run(between)
+        for item in ready:
+            item.close(True)
+            item.step(1, False)
         for k in range(LINE - 1):
-            for item in scatter:
+            for item in late:
                 item.step(k, True)
-        for item in scatter:
+        for item in ready:
+            item.step(2, False)
+        for item in late:
             item.close(True)
-        for k in range(2):
-            for item in scatter:
-                item.step(k, False)
         total.spread()
         total.landed()
-        for load in loads:
+        for load in loads[1:]:
             load.wait()
         for ref in (*gain_sums, carry):
             ref[...] = jnp.zeros_like(ref)
@@ -897,14 +1037,26 @@
                 buffer[slot] = value
             outputs.start(i, False)
 
+            @pl.when(i == 0)
+            def _():
+                for item in ready:
+                    item.close(False)
+                for item in late:
+                    item.step(0, False)
+
             @pl.when(i == 2)
             def _():
-                for item in scatter:
+                for item in late:
+                    item.step(1, False)
+
+            @pl.when(i == 4)
+            def _():
+                for item in late:
                     item.step(2, False)
 
-            @pl.when(i == 5)
-            def _():
-                for item in scatter:
+            @pl.when(i == 6)
+            def _():
+                for item in late:
                     item.close(False)
 
             return state
@@ -920,19 +1072,170 @@
     near_spec = pl.BlockSpec(memory_space=pltpu.VMEM)
     outs = pl.pallas_call(
         kernel,
-        in_specs=[whole] * (scatters + 1 + len(rows_in) + len(weights)) + [near_spec] * 2,
-        out_specs=[near_spec] * scatters + [whole] * 7 + [near_spec] * 4,
-        out_shape=[jax.ShapeDtypeStruct((t.shape[0] // (2 * LINE), t.shape[1]), f32) for t in totals]
-        + [jax.ShapeDtypeStruct(part.shape, half)]
+        in_specs=[whole] * (scatters + len(rows_in) + len(weights) + 2) + [near_spec] * 2,
+        out_specs=[near_spec] * scatters + [whole] * 8 + [near_spec] * 4,
+        out_shape=[
+            jax.ShapeDtypeStruct((t.shape[0] // (2 * LINE), t.shape[1]), f32)
+            for t in (*totals, made)
+        ]
+        + [jax.ShapeDtypeStruct(part.shape, half), made]
         + [jax.ShapeDtypeStruct((length, w), half) for w in outs_wide]
         + [jax.ShapeDtypeStruct((1, w), f32) for w in sum_wide],
         scratch_shapes=scratch,
         compiler_params=pltpu.CompilerParams(
-            collective_id=number, has_side_effects=True, vmem_limit_bytes=62 * 2**20
+            collective_id=number, has_side_effects=True, vmem_limit_bytes=VMEM_LIMIT
         ),
         name=f"backward_exchange_{number}",
-    )(*totals, part, *rows_in, *weights, *gains)
-    return outs[:scatters], outs[scatters + 1 : scatters + 7], outs[scatters + 7 :]
+    )(*totals, part, *rows_in, *weights, left, right, *gains)
+    return outs[:scatters], outs[scatters + 2 : scatters + 8], outs[scatters + 8 :]
+
+
+def last_exchange(number, total, parts, left_up, right_up, left_norm, right_norms, left_out, right_out):
+    ups = jax.ShapeDtypeStruct((left_up.shape[1], right_up.shape[1]), half)
+    rest = [jax.ShapeDtypeStruct((left_out.shape[1], right_out.shape[1]), half)]
+    rest += [jax.ShapeDtypeStruct((left_norm.shape[1], r.shape[1]), half) for r in right_norms]
+    made = [ups, *rest]
+    rights = [right_up, right_out, *right_norms]
+    lefts = [left_up, left_out, left_norm]
+    length = left_up.shape[0]
+    rows = ups.shape[0] // (2 * LINE)
+    scatters, sums = len(made) + 1, len(parts)
+    scratch = []
+    for item in (*made, total):
+        scratch += Scatter.scratch(item.shape[0] // (2 * LINE), item.shape[1])
+    for part in parts:
+        scratch += Total.scratch(part.shape[0], part.shape[1])
+    scratch += [pltpu.VMEM(r.shape, half) for r in rights]
+    scratch += [pltpu.VMEM((2, length, rows), half)] * 2
+    scratch += [pltpu.VMEM((2, rows, m.shape[1]), half) for m in made]
+    remote = Scatter.SEMS * scatters + Total.SEMS * sums
+    near = 12 * scatters + 2 * PIECES * sums
+    first_count, second_count = Maker.sem_count(1, 1), Maker.sem_count(2, len(rest))
+    scratch += [
+        pltpu.SemaphoreType.DMA((remote,)),
+        pltpu.SemaphoreType.DMA((remote,)),
+        pltpu.SemaphoreType.DMA((near,)),
+        pltpu.SemaphoreType.DMA((first_count + second_count + len(rights),)),
+    ]
+
+    def kernel(*refs):
+        refs = list(refs)
+
+        def pop(count):
+            taken, refs[:count] = refs[:count], []
+            return taken
+
+        (total_ref,), part_refs = pop(1), pop(sums)
+        left_refs, right_refs = pop(3), pop(len(rights))
+        own_refs, made_refs, sum_refs = pop(scatters), pop(len(made)), pop(sums)
+        buffers = [pop(6) for _ in range(scatters)]
+        sum_buffers = [pop(3) for _ in range(sums)]
+        near_rights, left_buffers, made_buffers = pop(len(rights)), pop(2), pop(len(made))
+        sems = refs.pop()
+        links = Links(*refs)
+        scatter = [Scatter(links, *a) for a in zip((*made_refs, total_ref), own_refs, buffers)]
+        up, late, small = scatter[0], scatter[1:], scatter[-1]
+        totals = [Total(links, *a) for a in zip(part_refs, sum_refs, sum_buffers)]
+        loads = [
+            pltpu.make_async_copy(far, close, sems.at[first_count + second_count + n])
+            for n, (far, close) in enumerate(zip(right_refs, near_rights))
+        ]
+        first = Maker(
+            links, sems, 0, left_refs[:1], left_buffers[:1],
+            [(0, near_rights[0], made_buffers[0], made_refs[0], up)],
+        )
+        second = Maker(
+            links, sems, first_count, left_refs[1:], left_buffers,
+            [
+                (min(n, 1), near_rights[n + 1], made_buffers[n + 1], made_refs[n + 1], scatter[n + 1])
+                for n in range(len(rest))
+            ],
+        )
+        links.greet()
+        loads[0].start()
+        first.start()
+        for item in totals:
+            item.start()
+        for load in loads[1:]:
+            load.start()
+        small.start()
+        loads[0].wait()
+
+        def between_first(j):
+            @pl.when(j == 5)
+            def _():
+                for item in totals:
+                    item.middle()
+
+        first.run(between_first)
+        second.start()
+        for k in range(LINE):
+            small.aside(k)
+        up.step(0, True)
+        for load in loads[1:]:
+            load.wait()
+
+        def between_second(j):
+            @pl.when(j == 1)
+            def _():
+                up.step(1, True)
+                up.step(0, False)
+
+            @pl.when(j == 3)
+            def _():
+                up.step(2, True)
+
+            @pl.when(j == 5)
+            def _():
+                up.close(True)
+                up.step(1, False)
+
+        second.run(between_second)
+        for item in late:
+            item.step(0, True)
+        up.step(2, False)
+        for item in late:
+            item.step(1, True)
+        up.close(False)
+        for item in late:
+            item.step(2, True)
+        for item in late:
+            item.step(0, False)
+        for item in late:
+            item.close(True)
+        for item in late:
+            item.step(1, False)
+        totals[0].spread()
+        for item in late:
+            item.step(2, False)
+        for item in totals[1:]:
+            item.spread()
+        for item in late:
+            item.close(False)
+        for item in totals:
+            item.landed()
+        for item in scatter + totals:
+            item.finish()
+
+    whole = pl.BlockSpec(memory_space=pl.ANY)
+    near_spec = pl.BlockSpec(memory_space=pltpu.VMEM)
+    outs = pl.pallas_call(
+        kernel,
+        in_specs=[whole] * (1 + sums + 3 + len(rights)),
+        out_specs=[near_spec] * scatters + [whole] * (len(made) + sums),
+        out_shape=[
+            jax.ShapeDtypeStruct((t.shape[0] // (2 * LINE), t.shape[1]), f32)
+            for t in (*made, total)
+        ]
+        + made
+        + [jax.ShapeDtypeStruct(p.shape, half) for p in parts],
+        scratch_shapes=scratch,
+        compiler_params=pltpu.CompilerParams(
+            collective_id=number, has_side_effects=True, vmem_limit_bytes=VMEM_LIMIT
+        ),
+        name=f"last_exchange_{number}",
+    )(total, *parts, *lefts, *rights)
+    return outs[:scatters], outs[scatters + len(made) :]
 
 
 class Ring:
@@ -1119,14 +1422,12 @@
     d_gate = d_gate.astype(half)
     d_up = d_up.astype(half)
     d_normed_ffn = (dot(d_gate, gate_full, NT) + dot(d_up, up_full, NT)).astype(half)
-    grad_gate = dot(normed_ffn, d_gate, TN).astype(half)
-    grad_up = dot(normed_ffn, d_up, TN).astype(half)
     ffn = dot(hidden, down_full, NT).astype(half)
     if fast:
         w_decay = jnp.pad(decay_weight, ((0, 128 - rank), (0, 0))).astype(half)
         (down_own, gate_own), outs, sums = backward_exchange(
             2,
-            (grad_down, grad_gate),
+            (grad_down,),
             d_normed_ffn,
             (
                 middle.astype(half), d_out_half, tokens, qkv, mixed, outgate, pre, scores,
@@ -1134,6 +1435,8 @@
             ),
             (out_full, qkv_full, outgate_full, small_full, w_decay, span),
             (gain_ffn[None, :], gain_head[None, :]),
+            normed_ffn,
+            d_gate,
         )
         d_attn, d_outgate, d_qkv, d_pre_half, d_rank, d_normed = outs
         grad_gain_ffn, grad_head, grad_bias, grad_gain_attn = sums
@@ -1155,9 +1458,6 @@
         d_normed = d_normed.astype(half)
         d_pre_half = d_pre.astype(half)
         grad_bias = jnp.sum(d_pre, axis=0)
-    grad_out = dot(d_attn, gated, TN).astype(half)
-    grad_outgate = dot(normed, d_outgate, TN).astype(half)
-    grad_qkv = dot(normed, d_qkv, TN).astype(half)
     grad_rank = dot(normed, d_rank, TN)
     grad_decay = jnp.transpose(
         dot(rank_rows.astype(half), d_pre_half, TN).reshape(rank, size, bits), (1, 0, 2)
@@ -1182,13 +1482,18 @@
     grad_small = grad_small.reshape(size * width, 128).astype(half)
 
     if fast:
-        waiting = (grad_up, grad_out, grad_outgate, grad_qkv, grad_small)
-        (up_own, out_own, outgate_own, qkv_own, small_own), (d_normed, ffn) = deliver(
-            3, waiting, (d_normed, ffn)
+        (up_own, out_own, outgate_own, qkv_own, small_own), (d_normed, ffn) = last_exchange(
+            3, grad_small, (d_normed, ffn), normed_ffn, d_up, normed, (d_outgate, d_qkv), d_attn, gated
         )
     else:
         waiting = (
-            grad_down, grad_gate, grad_up, grad_out, grad_outgate, grad_qkv, grad_small,
+            grad_down,
+            dot(normed_ffn, d_gate, TN).astype(half),
+            dot(normed_ffn, d_up, TN).astype(half),
+            dot(d_attn, gated, TN).astype(half),
+            dot(normed, d_outgate, TN).astype(half),
+            dot(normed, d_qkv, TN).astype(half),
+            grad_small,
         )
         (down_own, gate_own, up_own, out_own, outgate_own, qkv_own, small_own), (
             d_normed, ffn,

time: 799 us -> 768 us (0.961)
  matrix products: 135 us -> 93.2 us
    pallas_call x1 -> x2, Pallas kernels: 121 us -> 301 us  [the longest x1 169 us: last_exchange(): pl.pallas_call(kernel, in_specs=[whole] * (1 + sums + 3 + len(rights)), o...]
    pallas_call x3 -> x2, Pallas kernels: 442 us -> 264 us  [exchange(): pl.pallas_call(kernel, in_specs=[near_spec] * gathers + [whole] * (scatte...]
    dot_general x18 -> x13, matrix products: 134 us -> 91.6 us  [dot(): lax.dot_general(left, right, (dims, ((), ())), preferred_element_type=f32)]
    unnamed x112 -> x96, local copies, waits for them, and re-layouts: 15.4 us -> 20.1 us
where the time goes in v4:
time: 768 us; the launch traced here: 759 us
  Pallas kernels  574 us (75%)
  matrix products  93.2 us (12%)
  other arithmetic  52.3 us (7%)
  local copies, waits for them, and re-layouts  31.6 us (4%)
    pallas_call x2, Pallas kernels, exchange(): pl.pallas_call(kernel, in_specs=[near_spec] * gathers + [whole] * (scatte...  264 us
    pallas_call x1, Pallas kernels, last_exchange(): pl.pallas_call(kernel, in_specs=[whole] * (1 + sums + 3 + len(rights)), o...  169 us
    pallas_call x1, Pallas kernels, backward_exchange(): pl.pallas_call(kernel, in_specs=[whole] * (scatters + len(rows_in) + len(...  133 us
    dot_general x13, matrix products, dot(): lax.dot_general(left, right, (dims, ((), ())), preferred_element_type=f32)  91.6 us
    unnamed x96, local copies, waits for them, and re-layouts  20.1 us
  transfers between devices with their start and end apart: 2, of which 1 were waited for; matrix products, arithmetic and copies ran while one was open for 3% of the time, Pallas kernels for 0%

profile of v4, /device:TPU:0, one launch (start us, length us, event | category | flops | bytes accessed | tf_op | source)
XLA Modules:
  0.0 759.1 jit_solution(5941826419723979405)
XLA Ops:
  13.4 93.4 %exchange_0.1 = (bf16[2048,1024]{1,0:T(8,128)(2,1)}, bf16[2048,128]{1,0:T(8,128)(2,1)}, bf16[2048,512]{1,0:T(8,128)(2,1)}, bf16[2048,512]{1,0:T(8,128)(2,1)}) custom-call(bf16[256,1024]{1,0:T(8,128)(2,1)} %pad_maximum_fusion.refs_0_, bf16[256,128]{1,0:T(8,128)(2,1)} %pad.37.refs_1_, bf16[256,512]{1,0:T(8,128)(2,1)} %convert_element_type.151.refs_2_, ...), custom_call_target="tpu_custom_call" | custom-call | tf_op jit(solution)/shard_map/exchange_0/pallas_call | solution.py:732
  112.1 3.1 fusion.9
  123.6 3.2 fusion.3.refs_5_
  128.0 2.5 copy-done.8
  130.5 5.9 convolution_convert_fusion.4.q_ref.k_ref.v_ref.refs_5_
  138.0 9.8 %recur_forward.1 = (bf16[1024,512]{1,0:T(8,128)(2,1)}, bf16[1024,128]{1,0:T(8,128)(2,1)}, bf16[8,256,512]{2,1,0:T(8,128)(2,1)}) custom-call(f32[1024,256]{1,0:T(8,128)} %convolution_add_fusion.pre_ref.refs_8_, bf16[1024,1024]{1,0:T(8,128)(2,1)} %convolution_convert_fusion.4.q_ref.k_ref.v_ref.refs_5_, ...), custom_call_target="tpu_custom_call" | custom-call | flops 6000000000 | bytes 8388608 | tf_op jit(solution)/shard_map/recur_forward/pallas_call | solution.py:172
  149.3 6.3 fusion.18
  155.7 4.4 convolution_convert_fusion.2.refs_3_
  160.1 170.2 %exchange_1.1 = (bf16[2048,1408]{1,0:T(8,128)(2,1)}, bf16[2048,1408]{1,0:T(8,128)(2,1)}, bf16[2048,1408]{1,0:T(8,128)(2,1)}, bf16[1024,2048]{1,0:T(8,128)(2,1)}) custom-call(bf16[256,1408]{1,0:T(8,128)(2,1)} %convert_element_type.147.refs_0_, bf16[256,1408]{1,0:T(8,128)(2,1)} %convert_element_type.148.refs_1_, bf16[256,1408]{1,0:T(8,128)(2,1)} %bitcast.70, ...), custom_call_target="tpu_custom_call" | custom-call | tf_op jit(solution)/shard_map/exchange_1/pallas_call | solution.py:732
  330.3 5.0 multiply_reduce_fusion
  336.2 4.3 fusion.10
  340.5 8.9 %fusion.67 = f32[1024,1408]{1,0:T(8,128)} fusion(bf16[1024,2048]{1,0:T(8,128)(2,1)S(1)} %get-tuple-element.132.refs_17_.refs_3_, bf16[2048,1408]{1,0:T(8,128)(2,1)S(1)} %bitcast.90), kind=kOutput, calls=%fused_computation.181 | convolution fusion | flops 5905580032 | bytes 15728640 | tf_op jit(solution)/shard_map/dot_general | solution.py:41
  349.4 8.5 %fusion.66 = f32[1024,1408]{1,0:T(8,128)} fusion(bf16[1024,2048]{1,0:T(8,128)(2,1)S(1)} %get-tuple-element.132.refs_17_.refs_3_, bf16[2048,1408]{1,0:T(8,128)(2,1)S(1)} %bitcast.92), kind=kOutput, calls=%fused_computation.180 | convolution fusion | flops 5905580032 | bytes 15728640 | tf_op jit(solution)/shard_map/dot_general | solution.py:41
  358.7 3.4 copy-done.31
  362.0 11.8 %multiply_convert_fusion.3 = (bf16[1024,1408]{1,0:T(8,128)(2,1)S(1)}, bf16[1024,1408]{1,0:T(8,128)(2,1)}, bf16[1024,1408]{1,0:T(8,128)(2,1)}) fusion(f32[1024,1408]{1,0:T(8,128)} %fusion.66, f32[1024,1408]{1,0:T(8,128)S(1)} %copy-done.31, bf16[1024,2048]{1,0:T(8,128)(2,1)S(1)} %multiply_convert_fusion.2.refs_3_, bf16[2048,1408]{1,0:T(8,128)(2,1)S(1)} %bitcast.94), kind=kOutput, calls=%fused_computation.25 | convolution fusion | flops 5928648704 | bytes 30146560 | tf_op jit(solution)/shard_map/dot_general | solution.py:41
  373.9 11.2 %convolution_convert_fusion.1.refs_2_ = bf16[1024,2048]{1,0:T(8,128)(2,1)} fusion(bf16[1024,1408]{1,0:T(8,128)(2,1)} %get-tuple-element.130, bf16[2048,1408]{1,0:T(8,128)(2,1)S(1)} %bitcast.94), kind=kOutput, calls=%fused_computation.29 | convolution fusion | flops 5907677184 | bytes 12845056 | tf_op jit(solution)/shard_map/dot_general | solution.py:41
  385.1 8.8 %convolution_convert_fusion.refs_0_ = bf16[2048,1408]{1,0:T(8,128)(2,1)} fusion(bf16[1024,2048]{1,0:T(8,128)(2,1)S(1)} %multiply_convert_fusion.2.refs_3_, bf16[1024,1408]{1,0:T(8,128)(2,1)S(1)} %copy-done.32), kind=kOutput, calls=%fused_computation.20 | convolution fusion | flops 5908463616 | bytes 12845056 | tf_op jit(solution)/shard_map/dot_general | solution.py:41
  394.9 9.6 %fusion.68 = f32[1024,2048]{1,0:T(8,128)S(1)} fusion(bf16[1024,1408]{1,0:T(8,128)(2,1)} %get-tuple-element.129.refs_18_, bf16[2048,1408]{1,0:T(8,128)(2,1)} %get-tuple-element.52), kind=kOutput, calls=%fused_computation.182 | convolution fusion | flops 5905580032 | bytes 17039360 | tf_op jit(solution)/shard_map/dot_general | solution.py:41
  404.6 11.0 %add_convert_fusion.refs_1_ = bf16[1024,2048]{1,0:T(8,128)(2,1)} fusion(f32[1024,2048]{1,0:T(8,128)S(1)} %fusion.68, bf16[1024,1408]{1,0:T(8,128)(2,1)S(1)} %get-tuple-element.128.refs_6_, bf16[2048,1408]{1,0:T(8,128)(2,1)} %get-tuple-element.53), kind=kOutput, calls=%fused_computation.16 | convolution fusion | flops 5909774336 | bytes 21233664 | tf_op jit(solution)/shard_map/dot_general | solution.py:41
  415.6 132.5 %backward_exchange_2.1 = (f32[256,1408]{1,0:T(8,128)}, f32[256,1408]{1,0:T(8,128)}, bf16[1024,2048]{1,0:T(8,128)(2,1)}, bf16[2048,1408]{1,0:T(8,128)(2,1)}, bf16...) custom-call(bf16[2048,1408]{1,0:T(8,128)(2,1)} %convolution_convert_, ...), custom_call_target="tpu_custom_call" | custom-call | tf_op jit(solution)/shard_map/backward_exchange_2/pallas_call | solution.py:1073
  549.4 2.9 convolution_convert_fusion.3
  554.2 168.5 %last_exchange_3.1 = (f32[256,1408]{1,0:T(8,128)}, f32[256,512]{1,0:T(8,128)}, f32[256,512]{1,0:T(8,128)}, f32[256,1024]{1,0:T(8,128)}, f32[256,128]{1,0:T(8,128...) custom-call(bf16[2048,128]{1,0:T(8,128)(2,1)} %bitcast.72, ...), custom_call_target="tpu_custom_call" | custom-call | tf_op jit(solution)/shard_map/last_exchange_3/pallas_call | solution.py:1222
  726.0 4.6 fusion.4
  732.1 9.4 %fusion.8 = (bf16[1024,2048]{1,0:T(8,128)(2,1)}, bf16[1024,2048]{1,0:T(8,128)(2,1)}) fusion(bf16[1024,2048]{1,0:T(8,128)(2,1)S(1)} %copy-done.1, bf16[1024,2048]{1,0:T(8,128)(2,1)} %get-tuple-element.68, bf16[1024,2048]{1,0:T(8,128)(2,1)} %get-tuple-element.64.refs_4_, f32[1024]{0:T(1024)S(1)} %broadcast_multiply_fusion, f32[2048]{0:T(1024)S(1)} %copy-done.23, ...), kind=kLoop, calls=%fused_computation.12 | loop fusion | flops 33554432 | bytes 29380608 | tf_op jit(solution)/shard_map/convert_element_type | solution.py:1503
  (196 shorter events, 57.7 us)
Async XLA Ops:
  108.0 9.1 %copy-start.14 = (f32[256,1408]{1,0:T(8,128)S(1)}, f32[256,1408]{1,0:T(8,128)}, u32[]{:S(2)}) copy-start(f32[256,1408]{1,0:T(8,128)} %param.30) | copy-start | bytes 4325380
  109.2 14.4 %copy-start.22 = (f32[2048]{0:T(1024)}, f32[2048]{0:T(1024)S(1)}, u32[]{:S(2)}) copy-start(f32[2048]{0:T(1024)S(1)} %get-tuple-element.125) | copy-start | bytes 24580
  109.2 226.1 %copy-start.24 = (f32[2048]{0:T(1024)}, f32[2048]{0:T(1024)S(1)}, u32[]{:S(2)}) copy-start(f32[2048]{0:T(1024)S(1)} %get-tuple-element.124) | copy-start | bytes 24580
  126.8 9.6 %copy-start.2 = (bf16[1024,2048]{1,0:T(8,128)(2,1)}, bf16[1024,2048]{1,0:T(8,128)(2,1)S(1)}, u32[]{:S(2)}) copy-start(bf16[1024,2048]{1,0:T(8,128)(2,1)S(1)} %fusion.3.refs_5_) | copy-start | bytes 12582916
  138.0 11.3 %copy-start.11 = (bf16[2048,512]{1,0:T(8,128)(2,1)S(1)}, bf16[2048,512]{1,0:T(8,128)(2,1)}, u32[]{:S(2)}) copy-start(bf16[2048,512]{1,0:T(8,128)(2,1)} %get-tuple-element.49.refs_13_) | copy-start | bytes 6291460
  330.3 10.2 %slice-start = ((s8[5767168]{0:T(1024)(128)(4,1)}), s8[1572864]{0:T(1024)(128)(4,1)S(1)}, s32[]{:S(2)}) async-start(s8[5767168]{0:T(1024)(128)(4,1)} %bitcast.89), calls=%async_computation | async-start | bytes 3145728
  336.2 13.2 %slice-start.2 = ((s8[5767168]{0:T(1024)(128)(4,1)}), s8[4194304]{0:T(1024)(128)(4,1)S(1)}, s32[]{:S(2)}) async-start(s8[5767168]{0:T(1024)(128)(4,1)} %bitcast.91), calls=%async_computation.2 | async-start | bytes 8388608
  340.5 8.9 %copy-start.3 = (bf16[1024,2048]{1,0:T(8,128)(2,1)}, bf16[1024,2048]{1,0:T(8,128)(2,1)S(1)}, u32[]{:S(2)}) copy-start(bf16[1024,2048]{1,0:T(8,128)(2,1)S(1)} %get-tuple-element.132.refs_17_.refs_3_) | copy-start | bytes 12582916
  340.5 8.9 %slice-start.3 = ((s8[5767168]{0:T(1024)(128)(4,1)}), s8[1572864]{0:T(1024)(128)(4,1)S(1)}, s32[]{:S(2)}) async-start(s8[5767168]{0:T(1024)(128)(4,1)} %bitcast.91), calls=%async_computation.3 | async-start | bytes 3145728
  340.5 18.1 %slice-start.4 = ((s8[5767168]{0:T(1024)(128)(4,1)}), s8[4194304]{0:T(1024)(128)(4,1)S(1)}, s32[]{:S(2)}) async-start(s8[5767168]{0:T(1024)(128)(4,1)} %bitcast.93), calls=%async_computation.4 | async-start | bytes 8388608
  349.4 9.3 %slice-start.5 = ((s8[5767168]{0:T(1024)(128)(4,1)}), s8[1572864]{0:T(1024)(128)(4,1)S(1)}, s32[]{:S(2)}) async-start(s8[5767168]{0:T(1024)(128)(4,1)} %bitcast.93), calls=%async_computation.5 | async-start | bytes 3145728
  358.6 26.4 %copy-start.6 = (bf16[1024,2048]{1,0:T(8,128)(2,1)}, bf16[1024,2048]{1,0:T(8,128)(2,1)S(1)}, u32[]{:S(2)}) copy-start(bf16[1024,2048]{1,0:T(8,128)(2,1)S(1)} %multiply_convert_fusion.2.refs_3_) | copy-start | bytes 12582916
  373.9 30.7 %copy-start.10 = (bf16[1024,1408]{1,0:T(8,128)(2,1)}, bf16[1024,1408]{1,0:T(8,128)(2,1)S(1)}, u32[]{:S(2)}) copy-start(bf16[1024,1408]{1,0:T(8,128)(2,1)S(1)} %get-tuple-element.128.refs_6_) | copy-start | bytes 8650756
  373.9 11.2 %copy-start.32 = (bf16[1024,1408]{1,0:T(8,128)(2,1)S(1)}, bf16[1024,1408]{1,0:T(8,128)(2,1)}, u32[]{:S(2)}) copy-start(bf16[1024,1408]{1,0:T(8,128)(2,1)} %get-tuple-element.130) | copy-start | bytes 8650756
  385.1 8.8 %copy-start.13 = (bf16[8,256,2]{2,1,0:T(8,128)(2,1)S(1)}, bf16[8,256,2]{2,1,0:T(8,128)(2,1)}, u32[]{:S(2)}) copy-start(bf16[8,256,2]{2,1,0:T(8,128)(2,1)} %slice.94) | copy-start | bytes 24580
  554.2 171.8 %copy-start.23 = (f32[2048]{0:T(1024)S(1)}, f32[2048]{0:T(1024)}, u32[]{:S(2)}) copy-start(f32[2048]{0:T(1024)} %copy-done.22) | copy-start | bytes 24580
  554.2 171.8 %copy-start.26 = (f32[1024]{0:T(1024)S(1)}, f32[1024]{0:T(1024)}, u32[]{:S(2)}) copy-start(f32[1024]{0:T(1024)} %copy-done.25) | copy-start | bytes 12292
  724.3 24.2 %collective-permute-start = (bf16[256,128]{1,0:T(8,128)(2,1)}, bf16[256,128]{1,0:T(8,128)(2,1)}, u32[]{:S(2)}, u32[]{:S(2)}) collective-permute-start(bf16[256,128]{1,0:T(8,128)(2,1)} %convert_element_type.180), channel_id=1, source_target_pairs={{0,1},{1,0},{2,3},{3,2},{4,5},{5,4},{6,7},{7,6},{8,9},{9,8},{10,11... | collective-permute-start | bytes 196616 | tf_op jit(solution)/shard_map/ppermute | solution.py:1505
  732.1 9.4 %copy-start.18 = (f32[256,128]{1,0:T(8,128)S(1)}, f32[256,128]{1,0:T(8,128)}, u32[]{:S(2)}) copy-start(f32[256,128]{1,0:T(8,128)} %get-tuple-element.69) | copy-start | bytes 393220
  732.1 11.0 %copy-start.16 = (f32[256,1408]{1,0:T(8,128)S(1)}, f32[256,1408]{1,0:T(8,128)}, u32[]{:S(2)}) copy-start(f32[256,1408]{1,0:T(8,128)} %get-tuple-element.75) | copy-start | bytes 4325380
  741.5 14.4 %copy-start.21 = (f32[256,512]{1,0:T(8,128)S(1)}, f32[256,512]{1,0:T(8,128)}, u32[]{:S(2)}) copy-start(f32[256,512]{1,0:T(8,128)} %get-tuple-element.175) | copy-start | bytes 1572868
  741.5 15.2 %copy-start.15 = (f32[256,1408]{1,0:T(8,128)S(1)}, f32[256,1408]{1,0:T(8,128)}, u32[]{:S(2)}) copy-start(f32[256,1408]{1,0:T(8,128)} %get-tuple-element.182) | copy-start | bytes 4325380
  744.7 13.1 %copy-start.17 = (f32[256,1408]{1,0:T(8,128)S(1)}, f32[256,1408]{1,0:T(8,128)}, u32[]{:S(2)}) copy-start(f32[256,1408]{1,0:T(8,128)} %get-tuple-element.183) | copy-start | bytes 4325380
  749.3 4.3 collective-permute-start.1
  (17 other events, 95.4 us)

commit v5 on v4

--- a/solution.py
+++ b/solution.py
@@ -62,16 +62,9 @@
     return rows, cols, (lax.shift_right_logical(rows ^ cols, level) == 1)
 
 
-def forward_body(pre_ref, q_ref, k_ref, v_ref, span_ref, mixed_ref, score_ref, state_ref, state):
-    @pl.when(pl.program_id(0) == 0)
-    def _():
-        state[...] = jnp.zeros_like(state)
-
-    decay = log_decay(pre_ref[...])
+def forward_math(pre, q, k, v, span_ref, state):
+    decay = log_decay(pre)
     sums = dot(span_ref[...], split_two(decay), NN)
-    q = q_ref[...]
-    k = k_ref[...]
-    v = v_ref[...]
     q32 = q.astype(f32)
     k32 = k.astype(f32)
     rows, cols, _ = level_parts(0)
@@ -91,11 +84,20 @@
     score_half = scores.astype(half)
     state_now = state[...]
     state_half = state_now.astype(half)
-    mixed_ref[...] = (dot(score_half, v, NN) + dot(q_in, state_half, NN)).astype(mixed_ref.dtype)
-    score_ref[...] = score_half
-    state_ref[0] = state_half
+    mixed = dot(score_half, v, NN) + dot(q_in, state_half, NN)
     whole = jnp.exp(jnp.transpose(head_sum[CHUNK - 8 :, :]))[:, 7:8]
     state[...] = whole * state_now + dot(k_out, v, TN)
+    return mixed.astype(half), score_half, state_half
+
+
+def forward_body(pre_ref, q_ref, k_ref, v_ref, span_ref, mixed_ref, score_ref, state_ref, state):
+    @pl.when(pl.program_id(0) == 0)
+    def _():
+        state[...] = jnp.zeros_like(state)
+
+    mixed_ref[...], score_ref[...], state_ref[0] = forward_math(
+        pre_ref[...], q_ref[...], k_ref[...], v_ref[...], span_ref, state
+    )
 
 
 def backward_math(pre, q, k, v, d_mixed, scores, state_half, span_ref, carry):
@@ -305,7 +307,7 @@
             return self.shard.at[pl.ds(self.bulk, self.rows - self.bulk), :]
         return self.shard.at[pl.ds(0, self.bulk), :]
 
-    def go(self, index, src, dst, target, when=None):
+    def go(self, index, rest, src, dst, target, when=None):
         links = self.links
 
         def start():
@@ -314,38 +316,48 @@
         if when is None:
             start()
         else:
-            pl.when(when)(start)
-        self.pending.append((index, src, when))
+            pl.when(when())(start)
+        self.pending.append((index, rest, when))
+
+    def keep(self):
+        links = self.links
+        own = self.full.at[pl.ds((links.z * 2 + links.x) * self.rows, self.rows), :]
+        return pltpu.make_async_copy(self.shard, own, links.local.at[self.own_sem])
+
+    def there(self, side):
+        place = self.links.z + side
+        return place >= 0 if side < 0 else place <= LINE - 1
+
+    def onward(self, side):
+        z = self.links.z
+        more = z < LINE - 1 if side <= 0 else z > 0
+        return self.there(side) & more
 
     def start(self):
         links = self.links
         z, x = links.z, links.x
-        keep = self.full.at[pl.ds((z * 2 + x) * self.rows, self.rows), :]
-        self.keep = pltpu.make_async_copy(self.shard, keep, links.local.at[self.own_sem])
-        self.keep.start()
-        self.go(0, self.mine(False), self.at(z, x, False), links.up(), z < 3)
-        self.go(3, self.mine(False), self.at(z, x, False), links.down(), z > 0)
-        self.go(13, self.mine(True), self.at(z, x, True), links.beside())
-        self.go(6, self.mine(False), self.at(z, x, False), links.beside())
+        self.keep().start()
+        own, rest = self.mine(False), self.mine(True)
+        self.go(0, False, own, self.at(z, x, False), links.up(), lambda: z < LINE - 1)
+        self.go(3, False, own, self.at(z, x, False), links.down(), lambda: z > 0)
+        self.go(13, True, rest, self.at(z, x, True), links.beside())
+        self.go(6, False, own, self.at(z, x, False), links.beside())
 
     def bulk_step(self, k):
         links = self.links
         z, x = links.z, links.x
-        for side, base, cross, target, more in (
-            (-k, 0, 7, links.up(), z < 3),
-            (k, 3, 10, links.down(), z > 0),
-        ):
-            there = z + side
-            valid = there >= 0 if side < 0 else there <= 3
-            piece = self.at(there, x, False)
-
-            @pl.when(valid)
+        for side, base, cross, target in ((-k, 0, 7, links.up()), (k, 3, 10, links.down())):
+            piece = self.at(z + side, x, False)
+
+            @pl.when(self.there(side))
             def _():
                 links.arrived(self.base + base + k - 1, piece)
 
             if k < 3:
-                self.go(base + k, piece, piece, target, valid & more)
-            self.go(cross + k - 1, piece, piece, links.beside(), valid)
+                self.go(base + k, False, piece, piece, target, lambda side=side: self.onward(side))
+            self.go(
+                cross + k - 1, False, piece, piece, links.beside(), lambda side=side: self.there(side)
+            )
 
     def rest_start(self):
         links = self.links
@@ -354,29 +366,31 @@
         links.arrived(self.base + 13, other)
         mine = self.mine(True)
         for index, src, dst in ((14, mine, self.at(z, x, True)), (15, other, other)):
-            self.go(index, src, dst, links.up(), z < 3)
-            self.go(index + 6, src, dst, links.down(), z > 0)
+            self.go(index, True, src, dst, links.up(), lambda: z < LINE - 1)
+            self.go(index + 6, True, src, dst, links.down(), lambda: z > 0)
 
     def rest_step(self, k):
         links = self.links
         z, x = links.z, links.x
-        for side, base, target, more in (
-            (-k, 14, links.up(), z < 3),
-            (k, 20, links.down(), z > 0),
-        ):
-            there = z + side
-            valid = there >= 0 if side < 0 else there <= 3
+        for side, base, target in ((-k, 14, links.up()), (k, 20, links.down())):
             for which in range(2):
-                piece = self.at(there, x if which == 0 else 1 - x, True)
-
-                @pl.when(valid)
+                piece = self.at(z + side, x if which == 0 else 1 - x, True)
+
+                @pl.when(self.there(side))
                 def _():
                     links.arrived(self.base + base + 2 * (k - 1) + which, piece)
 
                 if k < 3:
-                    self.go(base + 2 * k + which, piece, piece, target, valid & more)
+                    self.go(
+                        base + 2 * k + which, True, piece, piece, target,
+                        lambda side=side: self.onward(side),
+                    )
 
     def finish(self):
+        self.landed()
+        self.drain()
+
+    def landed(self):
         links = self.links
         z, x = links.z, links.x
         links.arrived(self.base + 6, self.at(z, 1 - x, False))
@@ -389,16 +403,19 @@
                 def _():
                     links.arrived(self.base + cross + k - 1, self.at(there, 1 - x, False))
 
-        for index, src, when in self.pending:
+        self.keep().wait()
+
+    def drain(self):
+        links = self.links
+        for index, rest, when in self.pending:
 
             def done():
-                links.sent(self.base + index, src)
+                links.sent(self.base + index, self.mine(rest))
 
             if when is None:
                 done()
             else:
-                pl.when(when)(done)
-        self.keep.wait()
+                pl.when(when())(done)
 
 
 def add_rows(out, outs_at, terms, rows):
@@ -1238,6 +1255,272 @@
     return outs[:scatters], outs[scatters + len(made) :]
 
 
+def tile_loop(count, inputs, outputs, compute, between):
+    inputs.start(0, True)
+
+    def body(i, state):
+        @pl.when(i + 1 < count)
+        def _():
+            inputs.start(i + 1, True)
+
+        inputs.wait(i, True)
+        slot = i % 2
+        results = compute([b.at[slot] for b in inputs.buffers])
+
+        @pl.when(i >= 2)
+        def _():
+            outputs.wait(i - 2, False)
+
+        for buffer, value in zip(outputs.buffers, results):
+            buffer[slot] = value
+        outputs.start(i, False)
+        between(i)
+        return state
+
+    lax.fori_loop(0, count, body, 0)
+    outputs.wait(count - 2, False)
+    outputs.wait(count - 1, False)
+
+
+def front_exchange(number, tokens, nears, rows_near, shards, flips):
+    length, width = tokens.shape
+    count = length // CHUNK
+    w_qkv, w_small, w_decay, span = nears
+    dk = w_decay.shape[1]
+    dv = w_qkv.shape[1] - 2 * dk
+    shapes = [s.shape[::-1] if flip else s.shape for s, flip in zip(shards, flips)]
+    ff = shapes[2][1]
+    number_of = len(shards)
+    first_out = [
+        ((CHUNK, width), half), ((CHUNK, 2 * dk + dv), half), ((CHUNK, 128), f32),
+        ((CHUNK, dk), f32), ((CHUNK, dv), half), ((CHUNK, CHUNK), half), ((dk, dv), half),
+    ]
+    second_in = [((CHUNK, width), half), ((CHUNK, dv), half)]
+    second_out = [((CHUNK, dv), half), ((CHUNK, dv), half), ((CHUNK, width), half)]
+    third_in = [((CHUNK, width), half), ((CHUNK, width), half)]
+    third_out = [((CHUNK, width), half), ((CHUNK, width), half), ((CHUNK, ff), half), ((CHUNK, ff), half)]
+    first_in = [((CHUNK, width), half)]
+    groups = [first_in, first_out, second_in, second_out, third_in, third_out]
+    fulls = [jax.ShapeDtypeStruct((s[0] * 2 * LINE, s[1]), half) for s in shapes]
+    scratch = [pltpu.VMEM(s.shape, f32) for s in shards]
+    scratch += [pltpu.VMEM(s, half) for s in shapes]
+    scratch += Total.scratch(length, width)
+    for group in groups:
+        scratch += [pltpu.VMEM((2,) + s, t) for s, t in group]
+    scratch += [pltpu.VMEM(w.shape, w.dtype) for w in nears]
+    scratch += [pltpu.VMEM(f.shape, half) for f in fulls[:4]]
+    scratch += [pltpu.VMEM((dk, dv), f32)]
+    remote = Gather.SEMS * number_of + Total.SEMS
+    near = number_of + 2 * PIECES
+    bases = [2 * sum(len(g) for g in groups[:n]) for n in range(len(groups) + 1)]
+    extra = bases[-1] + number_of + len(nears) + 4
+    scratch += [
+        pltpu.SemaphoreType.DMA((remote,)),
+        pltpu.SemaphoreType.DMA((remote,)),
+        pltpu.SemaphoreType.DMA((near,)),
+        pltpu.SemaphoreType.DMA((extra,)),
+    ]
+    outs_first = [((length // CHUNK) * s[0], s[1], t) for s, t in first_out]
+    outs_second = [(length, s[1], t) for s, t in second_out]
+    outs_third = [(length, s[1], t) for s, t in third_out]
+
+    def kernel(*refs):
+        refs = list(refs)
+
+        def pop(count):
+            taken, refs[:count] = refs[:count], []
+            return taken
+
+        (tokens_ref,), near_refs, shard_refs = pop(1), pop(len(nears)), pop(number_of)
+        gain_attn, bias, gain_head, gain_ffn = pop(4)
+        full_refs, (sum_ref,) = pop(number_of), pop(1)
+        first_refs, second_refs, third_refs = pop(7), pop(3), pop(4)
+        staged, cast = pop(number_of), pop(number_of)
+        sum_buffers = pop(3)
+        buffers = [pop(len(g)) for g in groups]
+        close, full_near, (state,) = pop(len(nears)), pop(4), pop(1)
+        sems = refs.pop()
+        links = Links(*refs)
+        gathers = [Gather(links, c, f) for c, f in zip(cast, full_refs)]
+        early, (gate, up, down) = gathers[:2], gathers[2:]
+        total = Total(links, second_refs[2], sum_ref, sum_buffers)
+        sources = [
+            [tokens_ref], first_refs, [first_refs[0], first_refs[4]], second_refs,
+            [sum_ref, tokens_ref], third_refs,
+        ]
+        streams = [
+            Stream(sems, b, arrays, near_by, lambda i: i)
+            for b, arrays, near_by in zip(bases, sources, buffers)
+        ]
+        at = bases[-1]
+        arrive = [
+            pltpu.make_async_copy(far, by, sems.at[at + n])
+            for n, (far, by) in enumerate(zip(shard_refs, staged))
+        ]
+        at += number_of
+        loads = [
+            pltpu.make_async_copy(far, by, sems.at[at + n])
+            for n, (far, by) in enumerate(zip(near_refs, close))
+        ]
+        at += len(nears)
+        weights = [
+            pltpu.make_async_copy(far, by, sems.at[at + n])
+            for n, (far, by) in enumerate(zip(full_refs, full_near))
+        ]
+
+        def prepare(n):
+            arrive[n].wait()
+            values = staged[n][...]
+            cast[n][...] = (jnp.transpose(values) if flips[n] else values).astype(half)
+
+        for copy in arrive:
+            copy.start()
+        for copy in loads:
+            copy.start()
+        links.greet()
+        for n in range(3):
+            prepare(n)
+        for item in gathers[:3]:
+            item.start()
+        for n in range(3, number_of):
+            prepare(n)
+        for copy in loads:
+            copy.wait()
+        state[...] = jnp.zeros_like(state)
+
+        def first(tile):
+            unit, _ = rms_parts(tile[0][...].astype(f32))
+            normed = (unit * gain_attn[...]).astype(half)
+            qkv = dot(normed, close[0][...], NN).astype(half)
+            rank = dot(normed, close[1][...], NN)
+            pre = bias[...] + lax.dot_general(
+                rank, close[2][...], (NN, ((), ())),
+                precision=highest_precision, preferred_element_type=f32,
+            )
+            results = forward_math(
+                pre, qkv[:, :dk], qkv[:, dk : 2 * dk], qkv[:, 2 * dk :], close[3], state
+            )
+            return normed, qkv, rank, pre, *results
+
+        def first_between(i):
+            @pl.when(i == 1)
+            def _():
+                for item in early:
+                    item.bulk_step(1)
+                for item in early:
+                    item.rest_start()
+                up.start()
+
+            @pl.when(i == 4)
+            def _():
+                for item in early:
+                    item.bulk_step(2)
+                for item in early:
+                    item.rest_step(1)
+
+            @pl.when(i == 6)
+            def _():
+                gate.bulk_step(1)
+                gate.rest_start()
+
+        tile_loop(count, streams[0], streams[1], first, first_between)
+        up.bulk_step(1)
+        up.rest_start()
+        for item in early:
+            item.bulk_step(3)
+        for k in (2, 3):
+            for item in early:
+                item.rest_step(k)
+        for item in early:
+            item.landed()
+        for copy in weights[:2]:
+            copy.start()
+        for copy in weights[:2]:
+            copy.wait()
+
+        def second(tile):
+            normed, mixed = tile
+            outgate = dot(normed[...], full_near[0][...], NN).astype(half)
+            gated = gated_rows(mixed[...].astype(f32), outgate.astype(f32), gain_head[...]).astype(half)
+            return outgate, gated, dot(gated, full_near[1][...], NT).astype(half)
+
+        def second_between(i):
+            @pl.when(i == 3)
+            def _():
+                gate.bulk_step(2)
+                gate.rest_step(1)
+
+            @pl.when(i == 6)
+            def _():
+                up.bulk_step(2)
+                up.rest_step(1)
+                down.start()
+
+        tile_loop(count, streams[2], streams[3], second, second_between)
+        total.start()
+        total.middle()
+        gate.bulk_step(3)
+        gate.rest_step(2)
+        up.bulk_step(3)
+        up.rest_step(2)
+        down.bulk_step(1)
+        down.rest_start()
+        gate.rest_step(3)
+        up.rest_step(3)
+        total.spread()
+        gate.landed()
+        weights[2].start()
+        up.landed()
+        weights[3].start()
+        total.landed()
+        for copy in weights[2:]:
+            copy.wait()
+
+        def third(tile):
+            middle = tile[1][...].astype(f32) + tile[0][...].astype(f32)
+            unit, _ = rms_parts(middle)
+            normed = (unit * gain_ffn[...]).astype(half)
+            gate_rows = dot(normed, full_near[2][...], NN).astype(half)
+            return middle.astype(half), normed, gate_rows, dot(normed, full_near[3][...], NN).astype(half)
+
+        def third_between(i):
+            @pl.when(i == 0)
+            def _():
+                down.bulk_step(2)
+                down.rest_step(1)
+
+            @pl.when(i == 3)
+            def _():
+                down.bulk_step(3)
+                down.rest_step(2)
+
+        tile_loop(count, streams[4], streams[5], third, third_between)
+        down.rest_step(3)
+        down.landed()
+        for item in gathers:
+            item.drain()
+        total.finish()
+
+    whole = pl.BlockSpec(memory_space=pl.ANY)
+    near_spec = pl.BlockSpec(memory_space=pltpu.VMEM)
+    outs = pl.pallas_call(
+        kernel,
+        in_specs=[whole] * (1 + len(nears) + number_of) + [near_spec] * 4,
+        out_specs=[whole] * (number_of + 1 + 14),
+        out_shape=fulls
+        + [jax.ShapeDtypeStruct(tokens.shape, half)]
+        + [
+            jax.ShapeDtypeStruct((r, c), t) for r, c, t in (*outs_first, *outs_second, *outs_third)
+        ],
+        scratch_shapes=scratch,
+        compiler_params=pltpu.CompilerParams(
+            collective_id=number, has_side_effects=True, vmem_limit_bytes=VMEM_LIMIT
+        ),
+        name=f"front_exchange_{number}",
+    )(tokens, *nears, *shards, *rows_near)
+    return outs[2:number_of], outs[number_of + 1 :], outs[:2]
+
+
 class Ring:
     def __init__(self, size):
         self.size = size
@@ -1358,8 +1641,6 @@
     )
     small = jnp.pad(small, ((0, 0), (0, 128 - small.shape[1]))).astype(half)
     qkv = jnp.concatenate([query_proj * 0.0625, key_proj, value_proj], axis=1).astype(half)
-    first = (qkv, small, outgate_proj.astype(half), out_proj.T.astype(half))
-    second = (gate_proj.astype(half), up_proj.astype(half), down_proj.T.astype(half))
     fast = size == 2 * LINE
 
     def collect(number, shards, parts):
@@ -1374,7 +1655,11 @@
             return owns, sums
         return [scatter(ring, t) for t in totals], [tensor_sum(p) for p in parts]
 
-    (qkv_full, small_full, outgate_full, out_full), _ = collect(0, first, ())
+    if fast:
+        (qkv_full, small_full), _ = collect(0, (qkv, small), ())
+    else:
+        late = (outgate_proj.astype(half), out_proj.T.astype(half))
+        (qkv_full, small_full, outgate_full, out_full), _ = collect(0, (qkv, small, *late), ())
     rank_full = small_full[:, :rank]
     small32 = small_full.astype(f32)
     gain_attn = small32[:, rank]
@@ -1393,26 +1678,48 @@
     mask = (positions[None, :] < lengths[:, None]).astype(f32).reshape(rows_total, 1)
     tokens32 = tokens.astype(f32)
     unit, scale = rms_parts(tokens32)
-    normed = (unit * gain_attn).astype(half)
-    qkv = dot(normed, qkv_full, NN).astype(half)
-    rank_rows = dot(normed, rank_full, NN)
-    pre = (
-        jnp.dot(rank_rows, decay_weight, precision=highest_precision, preferred_element_type=f32)
-        + bias
-    )
     span = span_matrix()
-    mixed, scores, states = recur_forward(pre, qkv, span, dk, dv)
-    outgate = dot(normed, outgate_full, NN).astype(half)
-    gated, pull_gated = jax.vjp(gated_rows, mixed.astype(f32), outgate.astype(f32), gain_head)
-    gated = gated.astype(half)
-    (gate_full, up_full, down_full), (attn,) = collect(
-        1, second, (dot(gated, out_full, NT).astype(half),)
-    )
-    middle = tokens32 + attn.astype(f32)
-    unit_ffn, scale_ffn = rms_parts(middle)
-    normed_ffn = (unit_ffn * gain_ffn).astype(half)
-    gate_rows = dot(normed_ffn, gate_full, NN)
-    up_rows = dot(normed_ffn, up_full, NN)
+    if fast:
+        w_decay = jnp.pad(decay_weight, ((0, 128 - rank), (0, 0)))
+        (gate_full, up_full, down_full), outs, (outgate_full, out_full) = front_exchange(
+            1,
+            tokens,
+            (qkv_full, small_full, w_decay, span),
+            (gain_attn[None, :], bias[None, :], gain_head[None, :], gain_ffn[None, :]),
+            (outgate_proj, out_proj, gate_proj, up_proj, down_proj),
+            (False, True, False, False, True),
+        )
+        (
+            normed, qkv, rank_rows, pre, mixed, scores, states, outgate, gated, _,
+            middle_half, normed_ffn, gate_rows, up_rows,
+        ) = outs
+        rank_rows = rank_rows[:, :rank]
+        middle = middle_half.astype(f32)
+        gate_rows = gate_rows.astype(f32)
+        up_rows = up_rows.astype(f32)
+    else:
+        normed = (unit * gain_attn).astype(half)
+        qkv = dot(normed, qkv_full, NN).astype(half)
+        rank_rows = dot(normed, rank_full, NN)
+        pre = (
+            jnp.dot(
+                rank_rows, decay_weight, precision=highest_precision, preferred_element_type=f32
+            )
+            + bias
+        )
+        mixed, scores, states = recur_forward(pre, qkv, span, dk, dv)
+        outgate = dot(normed, outgate_full, NN).astype(half)
+        gated, pull_gated = jax.vjp(gated_rows, mixed.astype(f32), outgate.astype(f32), gain_head)
+        gated = gated.astype(half)
+        second = (gate_proj.astype(half), up_proj.astype(half), down_proj.T.astype(half))
+        (gate_full, up_full, down_full), (attn,) = collect(
+            1, second, (dot(gated, out_full, NT).astype(half),)
+        )
+        middle = tokens32 + attn.astype(f32)
+        unit_ffn, scale_ffn = rms_parts(middle)
+        normed_ffn = (unit_ffn * gain_ffn).astype(half)
+        gate_rows = dot(normed_ffn, gate_full, NN)
+        up_rows = dot(normed_ffn, up_full, NN)
     hidden, pull_glu = jax.vjp(lambda g, u: jax.nn.silu(g) * u, gate_rows, up_rows)
     hidden = hidden.astype(half)
     d_out = cotangent.astype(f32) * mask
@@ -1424,16 +1731,14 @@
     d_normed_ffn = (dot(d_gate, gate_full, NT) + dot(d_up, up_full, NT)).astype(half)
     ffn = dot(hidden, down_full, NT).astype(half)
     if fast:
-        w_decay = jnp.pad(decay_weight, ((0, 128 - rank), (0, 0))).astype(half)
         (down_own, gate_own), outs, sums = backward_exchange(
             2,
             (grad_down,),
             d_normed_ffn,
             (
-                middle.astype(half), d_out_half, tokens, qkv, mixed, outgate, pre, scores,
-                states.reshape(-1, dv),
+                middle_half, d_out_half, tokens, qkv, mixed, outgate, pre, scores, states,
             ),
-            (out_full, qkv_full, outgate_full, small_full, w_decay, span),
+            (out_full, qkv_full, outgate_full, small_full, w_decay.astype(half), span),
             (gain_ffn[None, :], gain_head[None, :]),
             normed_ffn,
             d_gate,

time: 768 us -> 700 us (0.911)
  matrix products: 93.2 us -> 56.4 us
  other arithmetic: 52.3 us -> 35.5 us
  local copies, waits for them, and re-layouts: 31.6 us -> 20.9 us
    pallas_call x2 -> x1, Pallas kernels: 264 us -> 53.8 us  [exchange(): pl.pallas_call(kernel, in_specs=[near_spec] * gathers + [whole] * (scatte...]
    pallas_call x1, Pallas kernels: 9.83 us -> 219 us  [front_exchange(): pl.pallas_call(kernel, in_specs=[whole] * (1 + len(nears) + number_of) +...]
    dot_general x13 -> x7, matrix products: 91.6 us -> 56.4 us  [dot(): lax.dot_general(left, right, (dims, ((), ())), preferred_element_type=f32)]
    unnamed x96 -> x66, local copies, waits for them, and re-layouts: 20.1 us -> 8.64 us
    convert_element_type x5 -> x1, other arithmetic: 12.5 us -> 3.25 us  [local(): output = (mask * (middle + ffn.astype(f32))).astype(half)]
where the time goes in v5:
time: 700 us; the launch traced here: 695 us
  Pallas kernels  575 us (82%)
  matrix products  56.4 us (8%)
  other arithmetic  35.5 us (5%)
  local copies, waits for them, and re-layouts  20.9 us (3%)
    pallas_call x1, Pallas kernels, front_exchange(): pl.pallas_call(kernel, in_specs=[whole] * (1 + len(nears) + number_of) +...  219 us
    pallas_call x1, Pallas kernels, last_exchange(): pl.pallas_call(kernel, in_specs=[whole] * (1 + sums + 3 + len(rights)), o...  172 us
    pallas_call x1, Pallas kernels, backward_exchange(): pl.pallas_call(kernel, in_specs=[whole] * (scatters + len(rows_in) + len(...  130 us
    dot_general x7, matrix products, dot(): lax.dot_general(left, right, (dims, ((), ())), preferred_element_type=f32)  56.4 us
    pallas_call x1, Pallas kernels, exchange(): pl.pallas_call(kernel, in_specs=[near_spec] * gathers + [whole] * (scatte...  53.8 us
  transfers between devices with their start and end apart: 2, of which 1 were waited for; matrix products, arithmetic and copies ran while one was open for 3% of the time, Pallas kernels for 0%

profile of v5, /device:TPU:0, one launch (start us, length us, event | category | flops | bytes accessed | tf_op | source)
XLA Modules:
  0.0 694.7 jit_solution(16887165823807208277)
XLA Ops:
  9.8 53.8 %exchange_0.1 = (bf16[2048,1024]{1,0:T(8,128)(2,1)}, bf16[2048,128]{1,0:T(8,128)(2,1)}) custom-call(bf16[256,1024]{1,0:T(8,128)(2,1)} %pad_maximum_fusion.refs_0_, bf16[256,128]{1,0:T(8,128)(2,1)} %pad.36.refs_1_), custom_call_target="tpu_custom_call" | custom-call | tf_op jit(solution)/shard_map/exchange_0/pallas_call | solution.py:749
  63.6 1.1 convert_element_type.106
  64.7 1.8 slice_reduce_fusion
  72.3 4.9 multiply_convert_fusion.1.refs_3_
  77.3 218.5 %front_exchange_1.1 = (bf16[2048,512]{1,0:T(8,128)(2,1)}, bf16[2048,512]{1,0:T(8,128)(2,1)}, bf16[2048,1408]{1,0:T(8,128)(2,1)}, bf16[2048,1408]{1,0:T(8,128)(2,...) custom-call(bf16[1024,2048]{1,0:T(8,128)(2,1)} %refs_4_.1, ...), custom_call_target="tpu_custom_call" | custom-call | tf_op jit(solution)/shard_map/front_exchange_1/pallas_call | solution.py:1506
  295.9 12.5 %convolution_convert_fusion.1.refs_2_ = bf16[1024,2048]{1,0:T(8,128)(2,1)} fusion(bf16[2048,1408]{1,0:T(8,128)(2,1)} %get-tuple-element.61, bf16[1024,1408]{1,0:T(8,128)(2,1)} %get-tuple-element.60, bf16[1024,1408]{1,0:T(8,128)(2,1)} %get-tuple-element.59), kind=kOutput, calls=%fused_computation.29 | convolution fusion | flops 5919211520 | bytes 15728640 | tf_op jit(solution)/shard_map/dot_general | solution.py:41
  308.4 11.3 %multiply_convert_fusion.2 = (bf16[1024,1408]{1,0:T(8,128)(2,1)S(1)}, bf16[1024,1408]{1,0:T(8,128)(2,1)S(1)}) fusion(bf16[1024,1408]{1,0:T(8,128)(2,1)S(1)} %copy-done.19, bf16[1024,1408]{1,0:T(8,128)(2,1)S(1)} %copy-done.20, bf16[1024,2048]{1,0:T(8,128)(2,1)S(1)} %copy-done.4, bf16[2048,1408]{1,0:T(8,128)(2,1)} %get-tuple-element.61), kind=kOutput, calls=%fused_computation.28 | convolution fusion | flops 5928648704 | bytes 21495808 | tf_op jit(solution)/shard_map/dot_general | solution.py:41
  319.7 9.0 %convolution_convert_fusion.refs_0_ = bf16[2048,1408]{1,0:T(8,128)(2,1)} fusion(bf16[1024,2048]{1,0:T(8,128)(2,1)S(1)} %copy-done.4, bf16[1024,1408]{1,0:T(8,128)(2,1)S(1)} %copy-done.20, bf16[1024,1408]{1,0:T(8,128)(2,1)S(1)} %copy-done.19), kind=kOutput, calls=%fused_computation.18 | convolution fusion | flops 5919997952 | bytes 15728640 | tf_op jit(solution)/shard_map/dot_general | solution.py:41
  329.4 9.0 %fusion.58 = f32[1024,2048]{1,0:T(8,128)} fusion(bf16[1024,1408]{1,0:T(8,128)(2,1)S(1)} %get-tuple-element.147.refs_18_, bf16[2048,1408]{1,0:T(8,128)(2,1)S(1)} %bitcast.60), kind=kOutput, calls=%fused_computation.160 | convolution fusion | flops 5905580032 | bytes 17039360 | tf_op jit(solution)/shard_map/dot_general | solution.py:41
  338.4 10.5 %add_convert_fusion.refs_1_ = bf16[1024,2048]{1,0:T(8,128)(2,1)} fusion(f32[1024,2048]{1,0:T(8,128)} %fusion.58, bf16[1024,1408]{1,0:T(8,128)(2,1)S(1)} %get-tuple-element.146.refs_6_, bf16[2048,1408]{1,0:T(8,128)(2,1)S(1)} %bitcast.58), kind=kOutput, calls=%fused_computation.16 | convolution fusion | flops 5909774336 | bytes 21233664 | tf_op jit(solution)/shard_map/dot_general | solution.py:41
  348.9 130.1 %backward_exchange_2.1 = (f32[256,1408]{1,0:T(8,128)}, f32[256,1408]{1,0:T(8,128)}, bf16[1024,2048]{1,0:T(8,128)(2,1)}, bf16[2048,1408]{1,0:T(8,128)(2,1)}, bf16...) custom-call(bf16[2048,1408]{1,0:T(8,128)(2,1)} %convolution_convert_, ...), custom_call_target="tpu_custom_call" | custom-call | tf_op jit(solution)/shard_map/backward_exchange_2/pallas_call | solution.py:1090
  479.0 1.3 convolution_convert_fusion.3
  480.5 2.9 convolution_convert_fusion.2
  485.0 172.2 %last_exchange_3.1 = (f32[256,1408]{1,0:T(8,128)}, f32[256,512]{1,0:T(8,128)}, f32[256,512]{1,0:T(8,128)}, f32[256,1024]{1,0:T(8,128)}, f32[256,128]{1,0:T(8,128...) custom-call(bf16[2048,128]{1,0:T(8,128)(2,1)} %bitcast.42, ...), custom_call_target="tpu_custom_call" | custom-call | tf_op jit(solution)/shard_map/last_exchange_3/pallas_call | solution.py:1239
  657.2 1.7 convert_element_type.126
  658.9 1.7 collective-permute-start
  660.6 3.7 fusion.7
  664.4 3.7 fusion.2
  668.1 4.2 fusion.6
  673.0 3.2 multiply_convert_fusion
  678.7 2.0 copy.79
  682.4 1.5 copy.80
  684.9 1.6 collective-permute-start.1
  687.2 2.1 collective-permute-done.1
  (145 shorter events, 28.3 us)
Async XLA Ops:
  295.8 12.5 %copy-start.4 = (bf16[1024,2048]{1,0:T(8,128)(2,1)S(1)}, bf16[1024,2048]{1,0:T(8,128)(2,1)}, u32[]{:S(2)}) copy-start(bf16[1024,2048]{1,0:T(8,128)(2,1)} %multiply_convert_fusion.1.refs_3_) | copy-start | bytes 12582916
  295.8 12.5 %copy-start.19 = (bf16[1024,1408]{1,0:T(8,128)(2,1)S(1)}, bf16[1024,1408]{1,0:T(8,128)(2,1)}, u32[]{:S(2)}) copy-start(bf16[1024,1408]{1,0:T(8,128)(2,1)} %get-tuple-element.59) | copy-start | bytes 8650756
  295.8 12.5 %copy-start.20 = (bf16[1024,1408]{1,0:T(8,128)(2,1)S(1)}, bf16[1024,1408]{1,0:T(8,128)(2,1)}, u32[]{:S(2)}) copy-start(bf16[1024,1408]{1,0:T(8,128)(2,1)} %get-tuple-element.60) | copy-start | bytes 8650756
  295.9 33.5 %slice-start.2 = ((s8[5767168]{0:T(1024)(128)(4,1)}), s8[4194304]{0:T(1024)(128)(4,1)S(1)}, s32[]{:S(2)}) async-start(s8[5767168]{0:T(1024)(128)(4,1)} %bitcast.59), calls=%async_computation.2 | async-start | bytes 8388608
  308.4 21.0 %slice-start.3 = ((s8[5767168]{0:T(1024)(128)(4,1)}), s8[1572864]{0:T(1024)(128)(4,1)S(1)}, s32[]{:S(2)}) async-start(s8[5767168]{0:T(1024)(128)(4,1)} %bitcast.59), calls=%async_computation.3 | async-start | bytes 3145728
  308.4 30.0 %slice-start = ((s8[5767168]{0:T(1024)(128)(4,1)}), s8[4194304]{0:T(1024)(128)(4,1)S(1)}, s32[]{:S(2)}) async-start(s8[5767168]{0:T(1024)(128)(4,1)} %bitcast.57), calls=%async_computation | async-start | bytes 8388608
  319.7 9.6 %copy-start.7 = (bf16[1024,1408]{1,0:T(8,128)(2,1)}, bf16[1024,1408]{1,0:T(8,128)(2,1)S(1)}, u32[]{:S(2)}) copy-start(bf16[1024,1408]{1,0:T(8,128)(2,1)S(1)} %get-tuple-element.147.refs_18_) | copy-start | bytes 8650756
  319.7 18.7 %copy-start.6 = (bf16[1024,1408]{1,0:T(8,128)(2,1)}, bf16[1024,1408]{1,0:T(8,128)(2,1)S(1)}, u32[]{:S(2)}) copy-start(bf16[1024,1408]{1,0:T(8,128)(2,1)S(1)} %get-tuple-element.146.refs_6_) | copy-start | bytes 8650756
  319.7 18.7 %slice-start.1 = ((s8[5767168]{0:T(1024)(128)(4,1)}), s8[1572864]{0:T(1024)(128)(4,1)S(1)}, s32[]{:S(2)}) async-start(s8[5767168]{0:T(1024)(128)(4,1)} %bitcast.57), calls=%async_computation.1 | async-start | bytes 3145728
  348.9 130.1 %copy-start.14 = (f32[1024,128]{1,0:T(8,128)S(1)}, f32[1024,128]{1,0:T(8,128)}, u32[]{:S(2)}) copy-start(f32[1024,128]{1,0:T(8,128)} %get-tuple-element.78) | copy-start | bytes 1572868
  478.9 4.5 copy-start.16
  479.0 4.6 copy-start.18
  479.0 4.7 copy-start.21
  485.0 179.3 %copy-start.15 = (f32[2048]{0:T(1024)S(1)}, f32[2048]{0:T(1024)}, u32[]{:S(2)}) copy-start(f32[2048]{0:T(1024)} %get-tuple-element.143) | copy-start | bytes 24580
  657.2 7.1 %copy-start = (bf16[1024,2048]{1,0:T(8,128)(2,1)S(1)}, bf16[1024,2048]{1,0:T(8,128)(2,1)}, u32[]{:S(2)}) copy-start(bf16[1024,2048]{1,0:T(8,128)(2,1)} %refs_4_.1) | copy-start | bytes 12582916
  658.9 9.2 %copy-start.1 = (bf16[1024,2048]{1,0:T(8,128)(2,1)S(1)}, bf16[1024,2048]{1,0:T(8,128)(2,1)}, u32[]{:S(2)}) copy-start(bf16[1024,2048]{1,0:T(8,128)(2,1)} %get-tuple-element.81.refs_4_) | copy-start | bytes 12582916
  658.9 9.2 %copy-start.3 = (bf16[1024,2048]{1,0:T(8,128)(2,1)S(1)}, bf16[1024,2048]{1,0:T(8,128)(2,1)}, u32[]{:S(2)}) copy-start(bf16[1024,2048]{1,0:T(8,128)(2,1)} %get-tuple-element.86) | copy-start | bytes 12582916
  658.9 25.0 %collective-permute-start = (bf16[256,128]{1,0:T(8,128)(2,1)}, bf16[256,128]{1,0:T(8,128)(2,1)}, u32[]{:S(2)}, u32[]{:S(2)}) collective-permute-start(bf16[256,128]{1,0:T(8,128)(2,1)} %convert_element_type.126), channel_id=1, source_target_pairs={{0,1},{1,0},{2,3},{3,2},{4,5},{5,4},{6,7},{7,6},{8,9},{9,8},{10,11... | collective-permute-start | bytes 196616 | tf_op jit(solution)/shard_map/ppermute | solution.py:1810
  668.1 4.9 copy-start.5
  673.0 9.4 %copy-start.9 = (f32[256,1408]{1,0:T(8,128)S(1)}, f32[256,1408]{1,0:T(8,128)}, u32[]{:S(2)}) copy-start(f32[256,1408]{1,0:T(8,128)} %get-tuple-element.93) | copy-start | bytes 4325380
  676.3 15.2 %copy-start.13 = (f32[256,512]{1,0:T(8,128)S(1)}, f32[256,512]{1,0:T(8,128)}, u32[]{:S(2)}) copy-start(f32[256,512]{1,0:T(8,128)} %get-tuple-element.186) | copy-start | bytes 1572868
  676.3 16.0 %copy-start.8 = (f32[256,1408]{1,0:T(8,128)S(1)}, f32[256,1408]{1,0:T(8,128)}, u32[]{:S(2)}) copy-start(f32[256,1408]{1,0:T(8,128)} %get-tuple-element.193) | copy-start | bytes 4325380
  683.9 9.4 %copy-start.10 = (f32[256,1408]{1,0:T(8,128)S(1)}, f32[256,1408]{1,0:T(8,128)}, u32[]{:S(2)}) copy-start(f32[256,1408]{1,0:T(8,128)} %get-tuple-element.194) | copy-start | bytes 4325380
  684.9 4.3 collective-permute-start.1
  (4 other events, 16.1 us)

commit v6 on v5

--- a/solution.py
+++ b/solution.py
@@ -224,7 +224,7 @@
 MESH = pl.DeviceIdType.MESH
 BULK = 13
 PIECES = 4
-VMEM_LIMIT = 63 * 2**20
+VMEM_LIMIT = 67043328
 
 
 class Links:
@@ -608,21 +608,21 @@
 
 
 class Total:
-    SEMS = 3 * PIECES
-
-    def __init__(self, links, part, out, buffers):
-        self.links, self.part, self.out = links, part, out
+    def __init__(self, links, part, out, buffers, reverse=False):
+        self.links, self.part, self.out, self.reverse = links, part, out, reverse
         self.mine, self.first, self.second = buffers
-        self.rows = part.shape[0] // 2 // PIECES
-        self.base = links.take(self.SEMS)
-        self.loads = links.take_local(2 * PIECES)
+        self.pieces, self.rows = self.mine.shape[0], self.mine.shape[1]
+        self.base = links.take(3 * self.pieces)
+        self.loads = links.take_local(2 * self.pieces)
 
     @staticmethod
-    def scratch(rows, n):
-        return [pltpu.VMEM((PIECES, rows // 2 // PIECES, n), half) for _ in range(3)]
+    def scratch(rows, n, pieces=PIECES):
+        return [pltpu.VMEM((pieces, rows // 2 // pieces, n), half) for _ in range(3)]
 
     def at(self, ref, core, j):
-        return ref.at[pl.ds((core * PIECES + j) * self.rows, self.rows), :]
+        place = self.pieces - 1 - j if self.reverse else j
+        first = (place * 2 + core) * self.rows
+        return ref.at[pl.ds(pl.multiple_of(first, self.rows), self.rows), :]
 
     def load(self, j):
         src = self.at(self.part, self.links.core, j)
@@ -630,46 +630,59 @@
 
     def store(self, j):
         dst = self.at(self.out, self.links.core, j)
-        sem = self.links.local.at[self.loads + PIECES + j]
+        sem = self.links.local.at[self.loads + self.pieces + j]
         return pltpu.make_async_copy(self.first.at[j], dst, sem)
 
     def start(self):
         links = self.links
-        for j in range(PIECES):
+        for j in range(self.pieces):
             self.load(j).start()
             src = self.at(self.part, 1 - links.core, j)
             links.copy(self.base + j, src, self.first.at[j], links.partner()).start()
 
     def middle(self):
         links = self.links
-        for j in range(PIECES):
+
+        def body(j, state):
             self.load(j).wait()
             links.arrived(self.base + j, self.first.at[j])
             add_rows(self.mine.at[j], 0, [self.mine.at[j], self.first.at[j]], self.rows)
-            index = self.base + PIECES + j
+            index = self.base + self.pieces + j
             links.copy(index, self.mine.at[j], self.second.at[j], links.across()).start()
+            return state
+
+        lax.fori_loop(0, self.pieces, body, 0)
+
+    def spread_piece(self, j):
+        links = self.links
+        links.arrived(self.base + self.pieces + j, self.second.at[j])
+        add_rows(self.first.at[j], 0, [self.mine.at[j], self.second.at[j]], self.rows)
+        index = self.base + 2 * self.pieces + j
+        dst = self.at(self.out, links.core, j)
+        links.copy(index, self.first.at[j], dst, links.partner()).start()
+        self.store(j).start()
+
+    def landed_piece(self, j):
+        links = self.links
+        links.arrived(self.base + 2 * self.pieces + j, self.at(self.out, 1 - links.core, j))
+        self.store(j).wait()
 
     def spread(self):
-        links = self.links
-        for j in range(PIECES):
-            links.arrived(self.base + PIECES + j, self.second.at[j])
-            add_rows(self.first.at[j], 0, [self.mine.at[j], self.second.at[j]], self.rows)
-            index = self.base + 2 * PIECES + j
-            dst = self.at(self.out, links.core, j)
-            links.copy(index, self.first.at[j], dst, links.partner()).start()
-            self.store(j).start()
+        def body(j, state):
+            self.spread_piece(j)
+            return state
+
+        lax.fori_loop(0, self.pieces, body, 0)
 
     def landed(self):
-        links = self.links
-        for j in range(PIECES):
-            links.arrived(self.base + 2 * PIECES + j, self.at(self.out, 1 - links.core, j))
-            self.store(j).wait()
+        for j in range(self.pieces):
+            self.landed_piece(j)
 
     def finish(self):
         links = self.links
-        for j in range(PIECES):
+        for j in range(self.pieces):
             for stage in range(3):
-                links.sent(self.base + stage * PIECES + j, self.mine.at[j])
+                links.sent(self.base + stage * self.pieces + j, self.mine.at[j])
 
 
 def exchange(number, shards=(), totals=(), parts=()):
@@ -679,7 +692,7 @@
         scratch += Scatter.scratch(total.shape[0] // (2 * LINE), total.shape[1])
     for part in parts:
         scratch += Total.scratch(part.shape[0], part.shape[1])
-    remote = Gather.SEMS * gathers + Scatter.SEMS * scatters + Total.SEMS * sums
+    remote = Gather.SEMS * gathers + Scatter.SEMS * scatters + 3 * PIECES * sums
     near = gathers + 12 * scatters + 2 * PIECES * sums
     scratch += [
         pltpu.SemaphoreType.DMA((remote,)),
@@ -916,8 +929,8 @@
     return d_attn, d_outgate, d_qkv, d_pre, d_rank, d_normed.astype(half)
 
 
-def backward_exchange(number, totals, part, rows_in, weights, gains, left, right):
-    scatters = len(totals) + 1
+def backward_exchange(number, part, rows_in, weights, gains, lefts, rights, w_down):
+    scatters = len(lefts)
     length, width = part.shape
     count = length // CHUNK
     dk = weights[4].shape[1]
@@ -927,21 +940,22 @@
     in_types = [half] + [a.dtype for a in rows_in]
     streams = len(in_shapes)
     sum_wide = (width, dv, dk, width)
-    made = jax.ShapeDtypeStruct((left.shape[1], right.shape[1]), half)
+    made = jax.ShapeDtypeStruct((lefts[0].shape[1], rights[0].shape[1]), half)
     rows = made.shape[0] // (2 * LINE)
     scratch = []
-    for total in (*totals, made):
-        scratch += Scatter.scratch(total.shape[0] // (2 * LINE), total.shape[1])
-    scratch += Total.scratch(length, width)
+    for _ in range(scatters):
+        scratch += Scatter.scratch(rows, made.shape[1])
+    scratch += Total.scratch(length, width, count)
     scratch += [pltpu.VMEM((2,) + s, t) for s, t in zip(in_shapes, in_types)]
     scratch += [pltpu.VMEM((2, CHUNK, w), half) for w in outs_wide]
-    scratch += [pltpu.VMEM(w.shape, half) for w in (*weights, right)]
+    scratch += [pltpu.VMEM(w.shape, half) for w in (*weights, rights[0], w_down)]
     scratch += [pltpu.VMEM((2, length, rows), half), pltpu.VMEM((2, rows, made.shape[1]), half)]
     scratch += [pltpu.VMEM((dk, dv), f32)]
-    remote = Scatter.SEMS * scatters + Total.SEMS
-    near = 12 * scatters + 2 * PIECES
-    maker_base = 2 * streams + 2 * len(outs_wide) + len(weights) + 1
-    extra = maker_base + Maker.sem_count(1, 1)
+    remote = Scatter.SEMS * scatters + 3 * count
+    near = 12 * scatters + 2 * count
+    ffn_base = 2 * streams + 2 * len(outs_wide) + len(weights) + 3
+    maker_base = ffn_base + 2
+    extra = maker_base + scatters * Maker.sem_count(1, 1)
     scratch += [
         pltpu.SemaphoreType.DMA((remote,)),
         pltpu.SemaphoreType.DMA((remote,)),
@@ -956,80 +970,100 @@
             taken, refs[:count] = refs[:count], []
             return taken
 
-        total_refs, (part_ref,), row_refs = pop(scatters - 1), pop(1), pop(streams - 1)
-        weight_refs, (left_ref, right_ref), gain_refs = pop(len(weights)), pop(2), pop(2)
-        own_refs, (sum_ref, made_ref), out_refs, gain_sums = pop(scatters), pop(2), pop(6), pop(4)
+        (part_ref,), row_refs = pop(1), pop(streams - 1)
+        weight_refs, left_refs, right_refs = pop(len(weights)), pop(scatters), pop(scatters)
+        (down_ref,), gain_refs = pop(1), pop(2)
+        own_refs, (sum_ref, ffn_ref), made_refs = pop(scatters), pop(2), pop(scatters)
+        out_refs, gain_sums = pop(6), pop(4)
         buffers = [pop(6) for _ in range(scatters)]
         sum_buffers = pop(3)
-        in_buffers, out_buffers, near_weights = pop(streams), pop(6), pop(len(weights) + 1)
-        (left_buffer, made_buffer, carry) = pop(3)
+        in_buffers, out_buffers, near_weights = pop(streams), pop(6), pop(len(weights))
+        right_near, down_near, left_buffer, made_buffer, carry = pop(5)
         sems = refs.pop()
         links = Links(*refs)
-        scatter = [
-            Scatter(links, *a) for a in zip((*total_refs, made_ref), own_refs, buffers)
-        ]
-        ready, late = scatter[:-1], scatter[-1:]
-        total = Total(links, part_ref, sum_ref, sum_buffers)
+        scatter = [Scatter(links, *a) for a in zip(made_refs, own_refs, buffers)]
+        down, gate = scatter
+        total = Total(links, part_ref, sum_ref, sum_buffers, True)
         inputs = Stream(sems, 0, [sum_ref] + row_refs, in_buffers, lambda i: count - 1 - i)
         outputs = Stream(sems, 2 * streams, out_refs, out_buffers, lambda i: count - 1 - i)
-        right_near = near_weights.pop()
+        ffn_out = Stream(sems, ffn_base, [ffn_ref], out_buffers[:1], lambda i: i)
+        near_base = 2 * streams + 12
         loads = [
-            pltpu.make_async_copy(far, close, sems.at[2 * streams + 12 + n])
+            pltpu.make_async_copy(far, close, sems.at[near_base + n])
             for n, (far, close) in enumerate(
-                zip((right_ref, *weight_refs), (right_near, *near_weights))
+                zip(
+                    (right_refs[0], right_refs[1], down_ref, *weight_refs),
+                    (right_near, right_near, down_near, *near_weights),
+                )
             )
         ]
-        maker = Maker(
-            links, sems, maker_base, [left_ref], [left_buffer],
-            [(0, right_near, made_buffer, made_ref, late[0])],
-        )
+        makers = [
+            Maker(
+                links, sems, maker_base + n * Maker.sem_count(1, 1), [left_refs[n]], [left_buffer],
+                [(0, right_near, made_buffer, made_refs[n], scatter[n])],
+            )
+            for n in range(scatters)
+        ]
+        loads[0].start()
+        makers[0].start()
+        for load in loads[2:]:
+            load.start()
         links.greet()
-        maker.start()
         total.start()
-        for k in range(LINE):
-            for item in ready:
-                item.aside(k)
-        for load in loads:
-            load.start()
-        for item in ready:
-            item.start()
         loads[0].wait()
 
-        def between(j):
-            @pl.when(j == 1)
+        def between_first(j):
+            @pl.when(j == 2)
             def _():
                 total.middle()
 
-            @pl.when(j == 3)
-            def _():
-                for item in ready:
-                    item.step(0, True)
-
-            @pl.when(j == 5)
-            def _():
-                for item in ready:
-                    item.step(1, True)
-                    item.step(0, False)
+        makers[0].run(between_first)
+        makers[1].start()
+        down.step(0, True)
+        loads[2].wait()
+
+        def ffn_body(i, state):
+            tile = right_near[pl.ds(pl.multiple_of(2 * i * CHUNK, 2 * CHUNK), 2 * CHUNK), :]
+            value = dot(tile, down_near[...], NT).astype(half)
+
+            @pl.when(i >= 1)
+            def _():
+                ffn_out.wait(2 * i - 2, False)
+                ffn_out.wait(2 * i - 1, False)
+
+            for part in range(2):
+                out_buffers[0][part] = value[part * CHUNK : (part + 1) * CHUNK]
+                ffn_out.start(2 * i + part, False)
+
+            @pl.when(i == 1)
+            def _():
+                down.step(1, True)
+                down.step(0, False)
+
+            return state
+
+        lax.fori_loop(0, count // 2, ffn_body, 0)
+        loads[1].start()
+        down.step(2, True)
+        ffn_out.wait(count - 2, False)
+        ffn_out.wait(count - 1, False)
+        loads[1].wait()
+
+        def between_second(j):
+            @pl.when(j == 2)
+            def _():
+                down.close(True)
+                down.step(1, False)
 
             @pl.when(j == 7)
             def _():
-                for item in ready:
-                    item.step(2, True)
-
-        maker.run(between)
-        for item in ready:
-            item.close(True)
-            item.step(1, False)
-        for k in range(LINE - 1):
-            for item in late:
-                item.step(k, True)
-        for item in ready:
-            item.step(2, False)
-        for item in late:
-            item.close(True)
-        total.spread()
-        total.landed()
-        for load in loads[1:]:
+                down.step(2, False)
+
+        makers[1].run(between_second)
+        for j in range(3):
+            total.spread_piece(j)
+        total.landed_piece(0)
+        for load in loads[3:]:
             load.wait()
         for ref in (*gain_sums, carry):
             ref[...] = jnp.zeros_like(ref)
@@ -1038,7 +1072,12 @@
         def body(i, state):
             @pl.when(i + 1 < count)
             def _():
+                total.landed_piece(i + 1)
                 inputs.start(i + 1, True)
+
+            @pl.when(i + 3 < count)
+            def _():
+                total.spread_piece(i + 3)
 
             inputs.wait(i, True)
             slot = i % 2
@@ -1056,31 +1095,36 @@
 
             @pl.when(i == 0)
             def _():
-                for item in ready:
-                    item.close(False)
-                for item in late:
-                    item.step(0, False)
+                gate.step(0, True)
+
+            @pl.when(i == 1)
+            def _():
+                gate.step(1, True)
+                down.close(False)
 
             @pl.when(i == 2)
             def _():
-                for item in late:
-                    item.step(1, False)
+                gate.step(2, True)
+                gate.step(0, False)
+
+            @pl.when(i == 3)
+            def _():
+                gate.close(True)
 
             @pl.when(i == 4)
             def _():
-                for item in late:
-                    item.step(2, False)
+                gate.step(1, False)
 
             @pl.when(i == 6)
             def _():
-                for item in late:
-                    item.close(False)
+                gate.step(2, False)
 
             return state
 
         lax.fori_loop(0, count, body, 0)
         outputs.wait(count - 2, False)
         outputs.wait(count - 1, False)
+        gate.close(False)
         for item in scatter:
             item.finish()
         total.finish()
@@ -1089,13 +1133,11 @@
     near_spec = pl.BlockSpec(memory_space=pltpu.VMEM)
     outs = pl.pallas_call(
         kernel,
-        in_specs=[whole] * (scatters + len(rows_in) + len(weights) + 2) + [near_spec] * 2,
-        out_specs=[near_spec] * scatters + [whole] * 8 + [near_spec] * 4,
-        out_shape=[
-            jax.ShapeDtypeStruct((t.shape[0] // (2 * LINE), t.shape[1]), f32)
-            for t in (*totals, made)
-        ]
-        + [jax.ShapeDtypeStruct(part.shape, half), made]
+        in_specs=[whole] * (2 + len(rows_in) + len(weights) + 2 * scatters) + [near_spec] * 2,
+        out_specs=[near_spec] * scatters + [whole] * (2 + scatters + 6) + [near_spec] * 4,
+        out_shape=[jax.ShapeDtypeStruct((rows, made.shape[1]), f32)] * scatters
+        + [jax.ShapeDtypeStruct(part.shape, half)] * 2
+        + [made] * scatters
         + [jax.ShapeDtypeStruct((length, w), half) for w in outs_wide]
         + [jax.ShapeDtypeStruct((1, w), f32) for w in sum_wide],
         scratch_shapes=scratch,
@@ -1103,8 +1145,9 @@
             collective_id=number, has_side_effects=True, vmem_limit_bytes=VMEM_LIMIT
         ),
         name=f"backward_exchange_{number}",
-    )(*totals, part, *rows_in, *weights, left, right, *gains)
-    return outs[:scatters], outs[scatters + 2 : scatters + 8], outs[scatters + 8 :]
+    )(part, *rows_in, *weights, *lefts, *rights, w_down, *gains)
+    rest = outs[2 * scatters + 2 :]
+    return outs[:scatters], outs[scatters + 1], rest[:6], rest[6:]
 
 
 def last_exchange(number, total, parts, left_up, right_up, left_norm, right_norms, left_out, right_out):
@@ -1125,7 +1168,7 @@
     scratch += [pltpu.VMEM(r.shape, half) for r in rights]
     scratch += [pltpu.VMEM((2, length, rows), half)] * 2
     scratch += [pltpu.VMEM((2, rows, m.shape[1]), half) for m in made]
-    remote = Scatter.SEMS * scatters + Total.SEMS * sums
+    remote = Scatter.SEMS * scatters + 3 * PIECES * sums
     near = 12 * scatters + 2 * PIECES * sums
     first_count, second_count = Maker.sem_count(1, 1), Maker.sem_count(2, len(rest))
     scratch += [
@@ -1310,7 +1353,7 @@
     scratch += [pltpu.VMEM(w.shape, w.dtype) for w in nears]
     scratch += [pltpu.VMEM(f.shape, half) for f in fulls[:4]]
     scratch += [pltpu.VMEM((dk, dv), f32)]
-    remote = Gather.SEMS * number_of + Total.SEMS
+    remote = Gather.SEMS * number_of + 3 * PIECES
     near = number_of + 2 * PIECES
     bases = [2 * sum(len(g) for g in groups[:n]) for n in range(len(groups) + 1)]
     extra = bases[-1] + number_of + len(nears) + 4
@@ -1724,24 +1767,22 @@
     hidden = hidden.astype(half)
     d_out = cotangent.astype(f32) * mask
     d_out_half = d_out.astype(half)
-    grad_down = dot(d_out_half, hidden, TN).astype(half)
     d_gate, d_up = pull_glu(dot(d_out_half, down_full, NN))
     d_gate = d_gate.astype(half)
     d_up = d_up.astype(half)
     d_normed_ffn = (dot(d_gate, gate_full, NT) + dot(d_up, up_full, NT)).astype(half)
-    ffn = dot(hidden, down_full, NT).astype(half)
     if fast:
-        (down_own, gate_own), outs, sums = backward_exchange(
+        (down_own, gate_own), ffn, outs, sums = backward_exchange(
             2,
-            (grad_down,),
             d_normed_ffn,
             (
                 middle_half, d_out_half, tokens, qkv, mixed, outgate, pre, scores, states,
             ),
             (out_full, qkv_full, outgate_full, small_full, w_decay.astype(half), span),
             (gain_ffn[None, :], gain_head[None, :]),
-            normed_ffn,
-            d_gate,
+            (d_out_half, normed_ffn),
+            (hidden, d_gate),
+            down_full,
         )
         d_attn, d_outgate, d_qkv, d_pre_half, d_rank, d_normed = outs
         grad_gain_ffn, grad_head, grad_bias, grad_gain_attn = sums
@@ -1791,8 +1832,9 @@
             3, grad_small, (d_normed, ffn), normed_ffn, d_up, normed, (d_outgate, d_qkv), d_attn, gated
         )
     else:
+        ffn = dot(hidden, down_full, NT).astype(half)
         waiting = (
-            grad_down,
+            dot(d_out_half, hidden, TN).astype(half),
             dot(normed_ffn, d_gate, TN).astype(half),
             dot(normed_ffn, d_up, TN).astype(half),
             dot(d_attn, gated, TN).astype(half),

time: 700 us -> 671 us (0.959)
  matrix products: 56.4 us -> 34.2 us
  Pallas kernels: 575 us -> 568 us
    dot_general x7 -> x5, matrix products: 56.4 us -> 34.2 us  [dot(): lax.dot_general(left, right, (dims, ((), ())), preferred_element_type=f32)]
where the time goes in v6:
time: 671 us; the launch traced here: 665 us
  Pallas kernels  568 us (85%)
  other arithmetic  34.8 us (5%)
  matrix products  34.2 us (5%)
  local copies, waits for them, and re-layouts  21.9 us (3%)
    pallas_call x1, Pallas kernels, front_exchange(): pl.pallas_call(kernel, in_specs=[whole] * (1 + len(nears) + number_of) +...  219 us
    pallas_call x1, Pallas kernels, last_exchange(): pl.pallas_call(kernel, in_specs=[whole] * (1 + sums + 3 + len(rights)), o...  167 us
    pallas_call x1, Pallas kernels, backward_exchange(): pl.pallas_call(kernel, in_specs=[whole] * (2 + len(rows_in) + len(weights...  129 us
    pallas_call x1, Pallas kernels, exchange(): pl.pallas_call(kernel, in_specs=[near_spec] * gathers + [whole] * (scatte...  53.8 us
    dot_general x5, matrix products, dot(): lax.dot_general(left, right, (dims, ((), ())), preferred_element_type=f32)  34.2 us
  transfers between devices with their start and end apart: 2, of which 1 were waited for; matrix products, arithmetic and copies ran while one was open for 3% of the time, Pallas kernels for 0%

profile of v6, /device:TPU:0, one launch (start us, length us, event | category | flops | bytes accessed | tf_op | source)
XLA Modules:
  0.0 665.2 jit_solution(15547729561278448532)
XLA Ops:
  0.8 1.1 convert.78
  9.8 53.8 %exchange_0.1 = (bf16[2048,1024]{1,0:T(8,128)(2,1)}, bf16[2048,128]{1,0:T(8,128)(2,1)}) custom-call(bf16[256,1024]{1,0:T(8,128)(2,1)} %pad_maximum_fusion.refs_0_, bf16[256,128]{1,0:T(8,128)(2,1)} %pad.36.refs_1_), custom_call_target="tpu_custom_call" | custom-call | tf_op jit(solution)/shard_map/exchange_0/pallas_call | solution.py:762
  63.6 1.1 convert_element_type.100
  64.7 1.8 slice_reduce_fusion
  73.0 4.9 multiply_convert_fusion.1.refs_2_.refs_16_
  77.9 218.5 %front_exchange_1.1 = (bf16[2048,512]{1,0:T(8,128)(2,1)}, bf16[2048,512]{1,0:T(8,128)(2,1)}, bf16[2048,1408]{1,0:T(8,128)(2,1)}, bf16[2048,1408]{1,0:T(8,128)(2,...) custom-call(bf16[1024,2048]{1,0:T(8,128)(2,1)} %refs_3_.1, ...), custom_call_target="tpu_custom_call" | custom-call | tf_op jit(solution)/shard_map/front_exchange_1/pallas_call | solution.py:1549
  296.5 14.9 %multiply_convert_fusion.2 = (bf16[1024,1408]{1,0:T(8,128)(2,1)S(1)}, bf16[1024,1408]{1,0:T(8,128)(2,1)S(1)}, bf16[1024,1408]{1,0:T(8,128)(2,1)}) fusion(bf16[1024,1408]{1,0:T(8,128)(2,1)} %get-tuple-element.62, bf16[1024,1408]{1,0:T(8,128)(2,1)} %get-tuple-element.61, bf16[1024,2048]{1,0:T(8,128)(2,1)} %multiply_convert_fusion.1.refs_2_.refs_16_, ...), kind=kOutput, calls=%fused_computation.27 | convolution fusion | flops 5931532288 | bytes 24379392 | tf_op jit(solution)/shard_map/dot_general | solution.py:41
  311.5 6.7 %fusion.56 = f32[1024,2048]{1,0:T(8,128)S(1)} fusion(bf16[1024,1408]{1,0:T(8,128)(2,1)S(1)} %get-tuple-element.149.refs_19_, bf16[2048,1408]{1,0:T(8,128)(2,1)S(1)} %copy-done.20), kind=kOutput, calls=%fused_computation.158 | convolution fusion | flops 5905580032 | bytes 17039360 | tf_op jit(solution)/shard_map/dot_general | solution.py:41
  318.2 8.2 %add_convert_fusion.refs_0_ = bf16[1024,2048]{1,0:T(8,128)(2,1)} fusion(f32[1024,2048]{1,0:T(8,128)S(1)} %fusion.56, bf16[1024,1408]{1,0:T(8,128)(2,1)S(1)} %get-tuple-element.148.refs_6_, bf16[2048,1408]{1,0:T(8,128)(2,1)S(1)} %copy-done.19), kind=kOutput, calls=%fused_computation.16 | convolution fusion | flops 5909774336 | bytes 21233664 | tf_op jit(solution)/shard_map/dot_general | solution.py:41
  326.4 128.7 %backward_exchange_2.1 = (f32[256,1408]{1,0:T(8,128)}, f32[256,1408]{1,0:T(8,128)}, bf16[1024,2048]{1,0:T(8,128)(2,1)}, bf16[1024,2048]{1,0:T(8,128)(2,1)}, bf16...) custom-call(bf16[1024,2048]{1,0:T(8,128)(2,1)} %add_convert_fusion.r, ...), custom_call_target="tpu_custom_call" | custom-call | tf_op jit(solution)/shard_map/backward_exchange_2/pallas_call | solution.py:1134
  455.1 1.4 convolution_convert_fusion.1
  456.8 2.9 convolution_convert_fusion
  461.3 167.4 %last_exchange_3.1 = (f32[256,1408]{1,0:T(8,128)}, f32[256,512]{1,0:T(8,128)}, f32[256,512]{1,0:T(8,128)}, f32[256,1024]{1,0:T(8,128)}, f32[256,128]{1,0:T(8,128...) custom-call(bf16[2048,128]{1,0:T(8,128)(2,1)} %bitcast.40, ...), custom_call_target="tpu_custom_call" | custom-call | tf_op jit(solution)/shard_map/last_exchange_3/pallas_call | solution.py:1282
  628.8 1.7 convert_element_type.118
  630.5 3.1 fusion.7
  633.6 3.9 fusion.2
  638.3 4.2 fusion.6
  643.3 3.2 multiply_convert_fusion
  649.0 2.0 copy.79
  652.7 1.5 copy.80
  655.2 1.6 collective-permute-start.1
  657.5 2.3 collective-permute-done.1
  662.8 1.1 copy.107
  663.9 1.1 copy.108
  (133 shorter events, 26.0 us)
Async XLA Ops:
  73.0 5.0 copy-start.14
  296.5 15.0 %copy-start.20 = (bf16[2048,1408]{1,0:T(8,128)(2,1)S(1)}, bf16[2048,1408]{1,0:T(8,128)(2,1)}, u32[]{:S(2)}) copy-start(bf16[2048,1408]{1,0:T(8,128)(2,1)} %get-tuple-element.63) | copy-start | bytes 17301508
  311.4 6.7 %copy-start.6 = (bf16[1024,1408]{1,0:T(8,128)(2,1)}, bf16[1024,1408]{1,0:T(8,128)(2,1)S(1)}, u32[]{:S(2)}) copy-start(bf16[1024,1408]{1,0:T(8,128)(2,1)S(1)} %get-tuple-element.149.refs_19_) | copy-start | bytes 8650756
  311.4 6.7 %copy-start.5 = (bf16[1024,1408]{1,0:T(8,128)(2,1)}, bf16[1024,1408]{1,0:T(8,128)(2,1)S(1)}, u32[]{:S(2)}) copy-start(bf16[1024,1408]{1,0:T(8,128)(2,1)S(1)} %get-tuple-element.148.refs_6_) | copy-start | bytes 8650756
  311.5 6.7 %copy-start.19 = (bf16[2048,1408]{1,0:T(8,128)(2,1)S(1)}, bf16[2048,1408]{1,0:T(8,128)(2,1)}, u32[]{:S(2)}) copy-start(bf16[2048,1408]{1,0:T(8,128)(2,1)} %get-tuple-element.64) | copy-start | bytes 17301508
  455.1 4.6 copy-start.17
  455.1 4.7 copy-start.16
  455.1 4.7 copy-start.18
  455.1 4.8 copy-start.21
  628.7 4.8 copy-start
  628.8 4.8 copy-start.13
  630.5 23.8 %collective-permute-start = (bf16[256,128]{1,0:T(8,128)(2,1)}, bf16[256,128]{1,0:T(8,128)(2,1)}, u32[]{:S(2)}, u32[]{:S(2)}) collective-permute-start(bf16[256,128]{1,0:T(8,128)(2,1)} %convert_element_type.118), channel_id=1, source_target_pairs={{0,1},{1,0},{2,3},{3,2},{4,5},{5,4},{6,7},{7,6},{8,9},{9,8},{10,11... | collective-permute-start | bytes 196616 | tf_op jit(solution)/shard_map/ppermute | solution.py:1852
  633.6 3.9 copy-start.1
  633.6 4.7 copy-start.3
  638.3 4.2 copy-start.2
  638.3 5.0 copy-start.4
  638.3 5.0 copy-start.15
  643.3 3.3 copy-start.11
  643.3 4.1 copy-start.10
  646.5 6.1 copy-start.8
  646.5 15.4 %copy-start.12 = (f32[256,512]{1,0:T(8,128)S(1)}, f32[256,512]{1,0:T(8,128)}, u32[]{:S(2)}) copy-start(f32[256,512]{1,0:T(8,128)} %get-tuple-element.189) | copy-start | bytes 1572868
  646.5 16.2 %copy-start.7 = (f32[256,1408]{1,0:T(8,128)S(1)}, f32[256,1408]{1,0:T(8,128)}, u32[]{:S(2)}) copy-start(f32[256,1408]{1,0:T(8,128)} %get-tuple-element.196) | copy-start | bytes 4325380
  654.2 9.7 %copy-start.9 = (f32[256,1408]{1,0:T(8,128)S(1)}, f32[256,1408]{1,0:T(8,128)}, u32[]{:S(2)}) copy-start(f32[256,1408]{1,0:T(8,128)} %get-tuple-element.197) | copy-start | bytes 4325380
  655.2 4.6 collective-permute-start.1

commit v7 on v6

--- a/solution.py
+++ b/solution.py
@@ -222,7 +222,7 @@
     )(pre, qkv, qkv, qkv, d_mixed, scores, states, span)
 
 MESH = pl.DeviceIdType.MESH
-BULK = 13
+BULK = 14
 PIECES = 4
 VMEM_LIMIT = 67043328
 

time: 671 us -> 667 us (level)
    pallas_call x1, Pallas kernels: 167 us -> 160 us  [last_exchange(): pl.pallas_call(kernel, in_specs=[whole] * (1 + sums + 3 + len(rights)), o...]
where the time goes in v7:
time: 667 us; the launch traced here: 660 us
  Pallas kernels  563 us (84%)
  other arithmetic  34.8 us (5%)
  matrix products  34.2 us (5%)
  local copies, waits for them, and re-layouts  21.9 us (3%)
    pallas_call x1, Pallas kernels, front_exchange(): pl.pallas_call(kernel, in_specs=[whole] * (1 + len(nears) + number_of) +...  224 us
    pallas_call x1, Pallas kernels, last_exchange(): pl.pallas_call(kernel, in_specs=[whole] * (1 + sums + 3 + len(rights)), o...  160 us
    pallas_call x1, Pallas kernels, backward_exchange(): pl.pallas_call(kernel, in_specs=[whole] * (2 + len(rows_in) + len(weights...  124 us
    pallas_call x1, Pallas kernels, exchange(): pl.pallas_call(kernel, in_specs=[near_spec] * gathers + [whole] * (scatte...  55.1 us
    dot_general x5, matrix products, dot(): lax.dot_general(left, right, (dims, ((), ())), preferred_element_type=f32)  34.2 us
  transfers between devices with their start and end apart: 2, of which 1 were waited for; matrix products, arithmetic and copies ran while one was open for 3% of the time, Pallas kernels for 0%

profile of v7, /device:TPU:0, one launch (start us, length us, event | category | flops | bytes accessed | tf_op | source)
XLA Modules:
  0.0 659.9 jit_solution(15754115610548395637)
XLA Ops:
  0.8 1.1 convert.78
  9.8 55.1 %exchange_0.1 = (bf16[2048,1024]{1,0:T(8,128)(2,1)}, bf16[2048,128]{1,0:T(8,128)(2,1)}) custom-call(bf16[256,1024]{1,0:T(8,128)(2,1)} %pad_maximum_fusion.refs_0_, bf16[256,128]{1,0:T(8,128)(2,1)} %pad.36.refs_1_), custom_call_target="tpu_custom_call" | custom-call | tf_op jit(solution)/shard_map/exchange_0/pallas_call | solution.py:762
  64.9 1.1 convert_element_type.100
  66.0 1.8 slice_reduce_fusion
  74.3 4.9 multiply_convert_fusion.1.refs_2_.refs_16_
  79.3 224.3 %front_exchange_1.1 = (bf16[2048,512]{1,0:T(8,128)(2,1)}, bf16[2048,512]{1,0:T(8,128)(2,1)}, bf16[2048,1408]{1,0:T(8,128)(2,1)}, bf16[2048,1408]{1,0:T(8,128)(2,...) custom-call(bf16[1024,2048]{1,0:T(8,128)(2,1)} %refs_3_.1, ...), custom_call_target="tpu_custom_call" | custom-call | tf_op jit(solution)/shard_map/front_exchange_1/pallas_call | solution.py:1549
  303.6 14.9 %multiply_convert_fusion.2 = (bf16[1024,1408]{1,0:T(8,128)(2,1)S(1)}, bf16[1024,1408]{1,0:T(8,128)(2,1)S(1)}, bf16[1024,1408]{1,0:T(8,128)(2,1)}) fusion(bf16[1024,1408]{1,0:T(8,128)(2,1)} %get-tuple-element.62, bf16[1024,1408]{1,0:T(8,128)(2,1)} %get-tuple-element.61, bf16[1024,2048]{1,0:T(8,128)(2,1)} %multiply_convert_fusion.1.refs_2_.refs_16_, ...), kind=kOutput, calls=%fused_computation.27 | convolution fusion | flops 5931532288 | bytes 24379392 | tf_op jit(solution)/shard_map/dot_general | solution.py:41
  318.6 6.7 %fusion.56 = f32[1024,2048]{1,0:T(8,128)S(1)} fusion(bf16[1024,1408]{1,0:T(8,128)(2,1)S(1)} %get-tuple-element.149.refs_19_, bf16[2048,1408]{1,0:T(8,128)(2,1)S(1)} %copy-done.20), kind=kOutput, calls=%fused_computation.158 | convolution fusion | flops 5905580032 | bytes 17039360 | tf_op jit(solution)/shard_map/dot_general | solution.py:41
  325.3 8.2 %add_convert_fusion.refs_0_ = bf16[1024,2048]{1,0:T(8,128)(2,1)} fusion(f32[1024,2048]{1,0:T(8,128)S(1)} %fusion.56, bf16[1024,1408]{1,0:T(8,128)(2,1)S(1)} %get-tuple-element.148.refs_6_, bf16[2048,1408]{1,0:T(8,128)(2,1)S(1)} %copy-done.19), kind=kOutput, calls=%fused_computation.16 | convolution fusion | flops 5909774336 | bytes 21233664 | tf_op jit(solution)/shard_map/dot_general | solution.py:41
  333.6 123.8 %backward_exchange_2.1 = (f32[256,1408]{1,0:T(8,128)}, f32[256,1408]{1,0:T(8,128)}, bf16[1024,2048]{1,0:T(8,128)(2,1)}, bf16[1024,2048]{1,0:T(8,128)(2,1)}, bf16...) custom-call(bf16[1024,2048]{1,0:T(8,128)(2,1)} %add_convert_fusion.r, ...), custom_call_target="tpu_custom_call" | custom-call | tf_op jit(solution)/shard_map/backward_exchange_2/pallas_call | solution.py:1134
  457.4 1.4 convolution_convert_fusion.1
  459.1 2.9 convolution_convert_fusion
  463.6 159.9 %last_exchange_3.1 = (f32[256,1408]{1,0:T(8,128)}, f32[256,512]{1,0:T(8,128)}, f32[256,512]{1,0:T(8,128)}, f32[256,1024]{1,0:T(8,128)}, f32[256,128]{1,0:T(8,128...) custom-call(bf16[2048,128]{1,0:T(8,128)(2,1)} %bitcast.40, ...), custom_call_target="tpu_custom_call" | custom-call | tf_op jit(solution)/shard_map/last_exchange_3/pallas_call | solution.py:1282
  623.6 1.7 convert_element_type.118
  625.2 3.1 fusion.7
  628.4 3.9 fusion.2
  633.1 4.2 fusion.6
  638.1 3.2 multiply_convert_fusion
  643.8 2.0 copy.79
  647.5 1.5 copy.80
  650.0 1.6 collective-permute-start.1
  652.3 2.3 collective-permute-done.1
  657.5 1.1 copy.107
  658.7 1.1 copy.108
  (133 shorter events, 26.0 us)
Async XLA Ops:
  74.3 5.0 copy-start.14
  303.6 15.0 %copy-start.20 = (bf16[2048,1408]{1,0:T(8,128)(2,1)S(1)}, bf16[2048,1408]{1,0:T(8,128)(2,1)}, u32[]{:S(2)}) copy-start(bf16[2048,1408]{1,0:T(8,128)(2,1)} %get-tuple-element.63) | copy-start | bytes 17301508
  318.5 6.7 %copy-start.6 = (bf16[1024,1408]{1,0:T(8,128)(2,1)}, bf16[1024,1408]{1,0:T(8,128)(2,1)S(1)}, u32[]{:S(2)}) copy-start(bf16[1024,1408]{1,0:T(8,128)(2,1)S(1)} %get-tuple-element.149.refs_19_) | copy-start | bytes 8650756
  318.6 6.7 %copy-start.5 = (bf16[1024,1408]{1,0:T(8,128)(2,1)}, bf16[1024,1408]{1,0:T(8,128)(2,1)S(1)}, u32[]{:S(2)}) copy-start(bf16[1024,1408]{1,0:T(8,128)(2,1)S(1)} %get-tuple-element.148.refs_6_) | copy-start | bytes 8650756
  318.6 6.7 %copy-start.19 = (bf16[2048,1408]{1,0:T(8,128)(2,1)S(1)}, bf16[2048,1408]{1,0:T(8,128)(2,1)}, u32[]{:S(2)}) copy-start(bf16[2048,1408]{1,0:T(8,128)(2,1)} %get-tuple-element.64) | copy-start | bytes 17301508
  457.4 4.6 copy-start.17
  457.4 4.7 copy-start.16
  457.4 4.7 copy-start.18
  457.4 4.8 copy-start.21
  623.5 4.8 copy-start
  623.5 4.8 copy-start.13
  625.2 23.8 %collective-permute-start = (bf16[256,128]{1,0:T(8,128)(2,1)}, bf16[256,128]{1,0:T(8,128)(2,1)}, u32[]{:S(2)}, u32[]{:S(2)}) collective-permute-start(bf16[256,128]{1,0:T(8,128)(2,1)} %convert_element_type.118), channel_id=1, source_target_pairs={{0,1},{1,0},{2,3},{3,2},{4,5},{5,4},{6,7},{7,6},{8,9},{9,8},{10,11... | collective-permute-start | bytes 196616 | tf_op jit(solution)/shard_map/ppermute | solution.py:1852
  628.4 3.9 copy-start.1
  628.4 4.7 copy-start.3
  633.1 4.2 copy-start.2
  633.1 5.0 copy-start.4
  633.1 5.0 copy-start.15
  638.1 3.3 copy-start.11
  638.1 4.1 copy-start.10
  641.3 6.1 copy-start.8
  641.3 15.4 %copy-start.12 = (f32[256,512]{1,0:T(8,128)S(1)}, f32[256,512]{1,0:T(8,128)}, u32[]{:S(2)}) copy-start(f32[256,512]{1,0:T(8,128)} %get-tuple-element.189) | copy-start | bytes 1572868
  641.3 16.2 %copy-start.7 = (f32[256,1408]{1,0:T(8,128)S(1)}, f32[256,1408]{1,0:T(8,128)}, u32[]{:S(2)}) copy-start(f32[256,1408]{1,0:T(8,128)} %get-tuple-element.196) | copy-start | bytes 4325380
  649.0 9.7 %copy-start.9 = (f32[256,1408]{1,0:T(8,128)S(1)}, f32[256,1408]{1,0:T(8,128)}, u32[]{:S(2)}) copy-start(f32[256,1408]{1,0:T(8,128)} %get-tuple-element.197) | copy-start | bytes 4325380
  650.0 4.6 collective-permute-start.1
